TPU v7x, 32 devices: a whole 2x2x4 slice. The times are simulated.
32 devices in a mesh: dp: 8 (over y, x, core), seq: 4 (over z).
Axes of the slice: x: 2, y: 2, z: 4, core: 2. Of those that a mesh axis runs over, the one named last changes fastest.
Arguments:
- inputs: bfloat16 [8, 1024, 1088], P('dp', 'seq'), may hold values from -6 to 6
- lengths: int32 [8], P('dp'), may hold values from 1 to 1024, 5734 in all
- cotangent: bfloat16 [8, 1024, 1088], P('dp', 'seq'), may hold values from -6 to 6
- norm1_gain: bfloat16 [1088], P('dp'), may hold values from 0.5 to 1.5
- norm1_bias: bfloat16 [1088], P('dp'), may hold values from -3 to 3
- qkv_weight: bfloat16 [1088, 3264], P('dp', 'seq'), may hold values from -0.1875 to 0.1875
- query_bias: bfloat16 [1088], P('dp'), may hold values from -3 to 3
- value_bias: bfloat16 [1088], P('dp'), may hold values from -3 to 3
- out_weight: bfloat16 [1088, 1088], P('dp', 'seq'), may hold values from -1.5 to 1.5
- out_bias: bfloat16 [1088], P('dp'), may hold values from -3 to 3
- norm2_gain: bfloat16 [1088], P('dp'), may hold values from 0.5 to 1.5
- norm2_bias: bfloat16 [1088], P('dp'), may hold values from -3 to 3
- up_weight: bfloat16 [1088, 4352], P('dp', 'seq'), may hold values from -0.1875 to 0.1875
- up_bias: bfloat16 [4352], P('dp'), may hold values from -3 to 3
- down_weight: bfloat16 [4352, 1088], P('seq', 'dp'), may hold values from -0.09375 to 0.09375
- down_bias: bfloat16 [1088], P('dp'), may hold values from -3 to 3
Outputs:
- outputs: bfloat16 [8, 1024, 1088], P('dp', 'seq')
- input_grad: float32 [8, 1024, 1088], P('dp', 'seq')
- norm1_gain_grad: float32 [1088], P('dp')
- norm1_bias_grad: float32 [1088], P('dp')
- qkv_weight_grad: float32 [1088, 3264], P('dp', 'seq')
- query_bias_grad: float32 [1088], P('dp')
- value_bias_grad: float32 [1088], P('dp')
- out_weight_grad: float32 [1088, 1088], P('dp', 'seq')
- out_bias_grad: float32 [1088], P('dp')
- norm2_gain_grad: float32 [1088], P('dp')
- norm2_bias_grad: float32 [1088], P('dp')
- up_weight_grad: float32 [1088, 4352], P('dp', 'seq')
- up_bias_grad: float32 [4352], P('dp')
- down_weight_grad: float32 [4352, 1088], P('seq', 'dp')
- down_bias_grad: float32 [1088], P('dp')
Inputs may be any that keep to these rules, and one draw needn't show every extreme that they name: `lengths`: each of the 8 sequences has its live tokens at the front of its slot, 5734 in all; the longest fills its slot.
All inputs are finite; a program needn't handle non-finite values. No bound on the sum of `lengths` on one device may be relied on, other than what follows from the above.
Results may differ from a plain program's by a relative error of at most 0.011.
Values may be sent and summed in bfloat16 or wider, within the bound.
No kernel may reach another device: no remote copies, remote signals or barrier semaphores. Data moves between devices by JAX's collectives and lax.ppermute only.
A program may use at most 128 MiB of HBM per device.

v0:
```python
import jax
import jax.numpy as jnp
from jax import lax
from jax.experimental import pallas as pl
from jax.experimental.pallas import tpu as pltpu
from jax.sharding import PartitionSpec as P


HD = 64
LANES = 128
EPS = 1e-05
GELU_C = 0.7978845608028654
MASKED = -1e30
BF = jnp.bfloat16
F32 = jnp.float32


def mm(a, b, dims=((1,), (0,))):
    return lax.dot_general(a, b, (dims, ((), ())), preferred_element_type=F32)


NT = ((1,), (1,))
TN = ((0,), (0,))


def ln_stats(x):
    average = jnp.mean(x, axis=-1, keepdims=True)
    centered = x - average
    variance = jnp.mean(centered * centered, axis=-1, keepdims=True)
    inv = lax.rsqrt(variance + EPS)
    return centered * inv, inv


def ln_back(grad_in, normed, inv, gain):
    scaled = grad_in * gain
    return inv * (
        scaled
        - jnp.mean(scaled, axis=-1, keepdims=True)
        - normed * jnp.mean(scaled * normed, axis=-1, keepdims=True)
    )


def gelu_parts(pre):
    tangent = jnp.tanh(GELU_C * (pre + 0.044715 * pre * pre * pre))
    result = 0.5 * pre * (1.0 + tangent)
    slope = 0.5 * (1.0 + tangent) + 0.5 * pre * (1.0 - tangent * tangent) * GELU_C * (
        1.0 + 3.0 * 0.044715 * pre * pre
    )
    return result, slope


def head_mask(rows, which):
    lane = lax.broadcasted_iota(jnp.int32, (rows, LANES), 1)
    return (lane >= HD) if which else (lane < HD)


def fill_mask(meta, mask_ref):
    key = lax.broadcasted_iota(jnp.int32, mask_ref.shape, 0)
    row = lax.broadcasted_iota(jnp.int32, mask_ref.shape, 1) + meta[0]
    mask_ref[...] = jnp.where((key <= row) & (key < meta[1]), 0.0, MASKED)


def attend_kernel(meta, q_ref, kv_ref, ctx_ref, lse_ref, mask_ref):
    rows = q_ref.shape[0]

    @pl.when(pl.program_id(0) == 0)
    def _():
        fill_mask(meta, mask_ref)

    k = kv_ref[:, :LANES]
    vt = kv_ref[:, LANES:].T
    q = q_ref[...] * jnp.asarray(HD ** -0.5, BF)
    pieces = []
    for which in range(2):
        qm = jnp.where(head_mask(rows, which), q, jnp.zeros_like(q))
        s = mm(k, qm, NT) + mask_ref[...]
        top = jnp.max(s, axis=0, keepdims=True)
        e = jnp.exp(s - top)
        total = jnp.sum(e, axis=0, keepdims=True)
        weights = (e * (1.0 / total)).astype(BF)
        pieces.append(mm(vt[which * HD:(which + 1) * HD], weights))
        lse_ref[0, which:which + 1, :] = top + jnp.log(total)
    ctx_ref[...] = jnp.concatenate(pieces, axis=0).T.astype(BF)


def attend(meta, q, kv):
    rows, width = q.shape
    keys = kv.shape[0]
    pairs = width // LANES
    return pl.pallas_call(
        attend_kernel,
        grid_spec=pltpu.PrefetchScalarGridSpec(
            num_scalar_prefetch=1,
            grid=(pairs,),
            in_specs=[
                pl.BlockSpec((rows, LANES), lambda p, m: (0, p)),
                pl.BlockSpec((keys, 2 * LANES), lambda p, m: (0, p)),
            ],
            out_specs=[
                pl.BlockSpec((rows, LANES), lambda p, m: (0, p)),
                pl.BlockSpec((1, 2, rows), lambda p, m: (p, 0, 0)),
            ],
            scratch_shapes=[pltpu.VMEM((keys, rows), F32)],
        ),
        out_shape=[
            jax.ShapeDtypeStruct((rows, width), BF),
            jax.ShapeDtypeStruct((pairs, 2, rows), F32),
        ],
        cost_estimate=pl.CostEstimate(
            flops=8 * rows * keys * width, transcendentals=2 * pairs * rows * keys, bytes_accessed=6 * keys * width
        ),
        name="attend",
    )(meta, q, kv)


def attend_back_kernel(meta, q_ref, kv_ref, lse_ref, g_ref, dq_ref, dkv_ref, mask_ref):
    rows = q_ref.shape[0]

    @pl.when(pl.program_id(0) == 0)
    def _():
        fill_mask(meta, mask_ref)

    scale = jnp.asarray(HD ** -0.5, BF)
    k = kv_ref[:, :LANES]
    v = kv_ref[:, LANES:]
    kt = k.T
    q = q_ref[...]
    g = g_ref[...]
    dq, weights_all, ds_all, q_all, g_all = [], [], [], [], []
    for which in range(2):
        mask = head_mask(rows, which)
        qm = jnp.where(mask, q, jnp.zeros_like(q))
        gm = jnp.where(mask, g, jnp.zeros_like(g))
        s = mm(k, qm * scale, NT) + mask_ref[...]
        weights = jnp.exp(s - lse_ref[0, which:which + 1, :])
        dprob = mm(v, gm * scale, NT)
        delta = jnp.sum(weights * dprob, axis=0, keepdims=True)
        ds = (weights * (dprob - delta)).astype(BF)
        dq.append(mm(kt[which * HD:(which + 1) * HD], ds))
        weights_all.append(weights.astype(BF))
        ds_all.append(ds)
        q_all.append(qm)
        g_all.append(gm)
    dq_ref[...] = jnp.concatenate(dq, axis=0).T.astype(BF)
    dk = mm(jnp.concatenate(ds_all, axis=1), jnp.concatenate(q_all, axis=0))
    dv = mm(jnp.concatenate(weights_all, axis=1), jnp.concatenate(g_all, axis=0))
    dkv_ref[:, :LANES] = dk.astype(BF)
    dkv_ref[:, LANES:] = dv.astype(BF)


def attend_back(meta, q, kv, lse, g):
    rows, width = q.shape
    keys = kv.shape[0]
    pairs = width // LANES
    return pl.pallas_call(
        attend_back_kernel,
        grid_spec=pltpu.PrefetchScalarGridSpec(
            num_scalar_prefetch=1,
            grid=(pairs,),
            in_specs=[
                pl.BlockSpec((rows, LANES), lambda p, m: (0, p)),
                pl.BlockSpec((keys, 2 * LANES), lambda p, m: (0, p)),
                pl.BlockSpec((1, 2, rows), lambda p, m: (p, 0, 0)),
                pl.BlockSpec((rows, LANES), lambda p, m: (0, p)),
            ],
            out_specs=[
                pl.BlockSpec((rows, LANES), lambda p, m: (0, p)),
                pl.BlockSpec((keys, 2 * LANES), lambda p, m: (0, p)),
            ],
            scratch_shapes=[pltpu.VMEM((keys, rows), F32)],
        ),
        out_shape=[
            jax.ShapeDtypeStruct((rows, width), BF),
            jax.ShapeDtypeStruct((keys, 2 * width), BF),
        ],
        cost_estimate=pl.CostEstimate(
            flops=20 * rows * keys * width, transcendentals=2 * pairs * rows * keys, bytes_accessed=12 * keys * width
        ),
        name="attend_back",
    )(meta, q, kv, lse, g)


def swap(x, bit):
    n = lax.axis_size("dp")
    return lax.ppermute(x, "dp", [(i, i ^ bit) for i in range(n)])


def ring_z(x):
    size = lax.axis_size("seq")
    me = lax.axis_index("seq")
    full = jnp.zeros((size,) + x.shape, x.dtype)
    full = lax.dynamic_update_slice(full, x[None], (me, 0, 0))
    for d in range(1, size):
        got = lax.ppermute(x, "seq", [(i, (i + d) % size) for i in range(size)])
        full = lax.dynamic_update_slice(full, got[None], ((me - d) % size, 0, 0))
    return full


def gather_dp(chunks):
    n = lax.axis_size("dp")
    if n != 8:
        return lax.all_gather(jnp.concatenate(chunks, axis=0), "dp", axis=0)
    me = lax.axis_index("dp")
    group, core = me // 2, me % 2
    rows = sum(x.shape[0] for x in chunks)
    full = jnp.zeros((n // 2, 2, rows, chunks[0].shape[1]), chunks[0].dtype)
    at = 0
    for x in chunks:
        half = jnp.zeros((n // 2,) + x.shape, x.dtype)
        half = lax.dynamic_update_slice(half, x[None], (group, 0, 0))
        for d in range(1, n // 2):
            got = swap(x, 2 * d)
            half = lax.dynamic_update_slice(half, got[None], (group ^ d, 0, 0))
        other = swap(half, 1)
        full = lax.dynamic_update_slice(full, half[:, None], (0, core, at, 0))
        full = lax.dynamic_update_slice(full, other[:, None], (0, 1 - core, at, 0))
        at += x.shape[0]
    return full.reshape(n, rows, chunks[0].shape[1])


def scatter_dp(g):
    n = lax.axis_size("dp")
    if n != 8:
        return lax.psum_scatter(g, "dp", scatter_dimension=0).astype(F32)
    me = lax.axis_index("dp")
    group, core = me // 2, me % 2
    pairs = g.reshape((n // 2, 2) + g.shape[1:])
    keep = lax.dynamic_index_in_dim(pairs, core, 1, keepdims=False)
    send = lax.dynamic_index_in_dim(pairs, 1 - core, 1, keepdims=False)
    got = swap(send, 1)
    summed = (keep.astype(F32) + got.astype(F32)).astype(BF)
    total = lax.dynamic_index_in_dim(summed, group, 0, keepdims=False).astype(F32)
    for d in range(1, n // 2):
        part = lax.dynamic_index_in_dim(summed, group ^ d, 0, keepdims=False)
        total = total + swap(part, 2 * d).astype(F32)
    return total


def gather_z(x):
    return lax.all_gather(x, "seq", axis=0, tiled=True)


def scatter_z(x):
    return lax.psum_scatter(x, "seq", scatter_dimension=0, tiled=True).astype(F32)


def pad_cols(x, width):
    return jnp.pad(x, [(0, 0)] * (x.ndim - 1) + [(0, width - x.shape[-1])])


def pair_up(a, b):
    lead = a.shape[:-1]
    blocks = a.shape[-1] // LANES
    both = jnp.stack([a.reshape(lead + (blocks, LANES)), b.reshape(lead + (blocks, LANES))], axis=-2)
    return both.reshape(lead + (2 * a.shape[-1],))


def pair_split(x):
    lead = x.shape[:-1]
    both = x.reshape(lead + (x.shape[-1] // (2 * LANES), 2, LANES))
    half = lead + (x.shape[-1] // 2,)
    return both[..., 0, :].reshape(half), both[..., 1, :].reshape(half)


def shards(
    inputs,
    lengths,
    cotangent,
    norm1_gain,
    norm1_bias,
    qkv_weight,
    query_bias,
    value_bias,
    out_weight,
    out_bias,
    norm2_gain,
    norm2_bias,
    up_weight,
    up_bias,
    down_weight,
    down_bias,
):
    n = lax.axis_size("dp")
    zs = lax.axis_size("seq")
    z = lax.axis_index("seq")
    rows, width = inputs.shape[1:]
    total_rows = rows * zs
    share = norm1_gain.shape[0]
    wide = -(-width // LANES) * LANES
    qkv_cols = qkv_weight.shape[1]
    ff = up_weight.shape[1]
    ff_total = ff * zs
    length = lengths[0]
    first = z * rows
    meta = jnp.stack([first, length]).astype(jnp.int32)

    thin = jnp.stack(
        [norm1_gain, norm1_bias, query_bias, value_bias, out_bias, norm2_gain, norm2_bias, down_bias]
    ).reshape(1, 8 * share)
    thin_all = gather_dp([jnp.concatenate([thin, up_bias.reshape(1, -1)], axis=1)])
    thin_all = thin_all.reshape(n, 8 * share + up_bias.shape[0])
    vectors = (
        thin_all[:, : 8 * share].reshape(n, 8, share).transpose(1, 0, 2).reshape(8, width).astype(F32)
    )
    up_bias_all = thin_all[:, 8 * share:].reshape(ff_total).astype(F32)
    gain1, shift1, bias_q, bias_v, bias_o, gain2, shift2, bias_d = [vectors[i] for i in range(8)]
    up_shift = lax.dynamic_slice_in_dim(up_bias_all, z * ff, ff)

    x_full = gather_z(inputs[0])
    cot, _ = lax.optimization_barrier((cotangent[0], x_full))
    g_full = gather_z(cot)

    cut = -(-share // 16) * 8
    chunks = []
    for lo, hi in ((0, cut), (cut, share)):
        raw = ring_z(qkv_weight[lo:hi]).transpose(1, 0, 2).reshape(hi - lo, 3 * width)
        wq_s = pad_cols(raw[:, :width], wide)
        wk_s = pad_cols(raw[:, width : 2 * width], wide)
        wv_s = pad_cols(raw[:, 2 * width :], wide)
        chunks.append(jnp.concatenate([wq_s, pair_up(wk_s, wv_s)], axis=1))
    qkv_full = gather_dp(chunks).reshape(width, 3 * wide)
    out_s, _ = lax.optimization_barrier((out_weight, chunks[1]))
    out_rows = ring_z(out_s).transpose(1, 0, 2).reshape(share, width)
    out_rows, up_s, down_s, qkv_full = lax.optimization_barrier((out_rows, up_weight, down_weight, qkv_full))
    wq = qkv_full[:, :wide]
    wkv = qkv_full[:, wide:]

    x_own = inputs[0].astype(F32)
    normed1, inv1 = ln_stats(x_own)
    attn_own = (normed1 * gain1 + shift1).astype(BF)
    normed1_full, _ = ln_stats(x_full.astype(F32))
    attn_full = (normed1_full * gain1 + shift1).astype(BF)
    q = (mm(attn_own, wq) + pad_cols(bias_q, wide)).astype(BF)
    bias_kv = pair_up(jnp.zeros((wide,), F32), pad_cols(bias_v, wide))
    kv = (mm(attn_full, wkv) + bias_kv).astype(BF)
    wo = gather_dp([out_rows]).reshape(width, width)
    mlp_w = gather_dp([jnp.concatenate([up_s, down_s.T], axis=1)]).reshape(width, 2 * ff)
    up_full = mlp_w[:, :ff]
    down_t = mlp_w[:, ff:]
    ctx, lse = attend(meta, q, kv)
    ctx, g_full = lax.optimization_barrier((ctx, g_full))
    ctx = ctx[:, :width]
    resid = x_own + mm(ctx, wo) + bias_o
    normed2, inv2 = ln_stats(resid)
    mlp_in = (normed2 * gain2 + shift2).astype(BF)
    mlp_full = gather_z(mlp_in)
    pre = mm(mlp_full, up_full) + up_shift
    act, slope = gelu_parts(pre)
    hidden = act.astype(BF)

    position = lax.broadcasted_iota(jnp.int32, (total_rows, 1), 0)
    g_full = g_full * (position < length).astype(BF)
    own_position = first + lax.broadcasted_iota(jnp.int32, (rows, 1), 0)
    grad_out = cotangent[0].astype(F32) * (own_position < length).astype(F32)
    grad_pre = mm(g_full, down_t) * slope
    grad_pre_b = grad_pre.astype(BF)
    grad_mlp = scatter_z(mm(grad_pre_b, up_full, NT).astype(BF))
    mlp_part, _ = lax.optimization_barrier((mm(hidden, down_t, NT).astype(BF), grad_mlp))
    mlp_out = scatter_z(mlp_part)
    up_b_block = jnp.sum(grad_pre, axis=0)
    mlp_dw = jnp.concatenate([mm(mlp_full, grad_pre_b, TN), mm(g_full, hidden, TN)], axis=1).astype(BF)
    grad_resid = grad_out + ln_back(grad_mlp, normed2, inv2, gain2)
    grad_resid_b = grad_resid.astype(BF)
    grad_ctx = pad_cols(mm(grad_resid_b, wo, NT).astype(BF), wide)
    dwo = scatter_dp(mm(ctx, grad_resid_b, TN).astype(BF).reshape(n, share, width))
    dq, dkv = attend_back(meta, q, kv, lse, grad_ctx)
    mlp_dw = scatter_dp(mlp_dw.reshape(n, share, 2 * ff))
    dq, dkv, mlp_out = lax.optimization_barrier((dq, dkv, mlp_out))
    outputs = (resid + mlp_out + bias_d).astype(BF)
    up_grad = mlp_dw[:, :ff]
    down_grad = mlp_dw[:, ff:].T
    dw = jnp.concatenate([mm(attn_own, dq, TN), mm(attn_full, dkv, TN)], axis=1).astype(BF)
    dq, dkv, dw = lax.optimization_barrier((dq, dkv, dw))
    dw = scatter_dp(dw.reshape(n, share, 3 * wide))
    part_kv = mm(dkv, wkv, NT)
    part_q = mm(dq, wq, NT)
    grad_attn = scatter_z(part_kv.astype(BF))

    dv_sum = pair_split(jnp.sum(dkv.astype(F32), axis=0))[1][:width]
    vec = jnp.stack(
        [
            jnp.sum(part_kv * normed1_full, axis=0) + jnp.sum(part_q * normed1, axis=0),
            jnp.sum(part_kv, axis=0) + jnp.sum(part_q, axis=0),
            jnp.sum(dq.astype(F32), axis=0)[:width],
            dv_sum,
            jnp.sum(grad_resid, axis=0),
            jnp.sum(grad_mlp * normed2, axis=0),
            jnp.sum(grad_mlp, axis=0),
            jnp.sum(grad_out, axis=0),
        ]
    )
    up_b = lax.dynamic_update_slice_in_dim(jnp.zeros((ff_total,), F32), up_b_block, z * ff, 0)
    thin_grad = jnp.concatenate(
        [vec.reshape(8, n, share).transpose(1, 0, 2).reshape(n, 8 * share), up_b.reshape(n, ff_total // n)],
        axis=1,
    )
    thin_len = thin_grad.shape[1]
    thin_grad = scatter_dp(thin_grad.astype(BF)[:, None, :])

    piece = qkv_cols + width // zs
    dwk, dwv = pair_split(dw[:, wide:])
    dw_cols = jnp.concatenate([dw[:, :width], dwk[:, :width], dwv[:, :width]], axis=1).astype(BF)
    dwo = dwo.astype(BF)
    extra = -(-thin_len // piece)
    thin_rows = pad_cols(thin_grad.astype(BF), extra * piece).reshape(extra, piece)
    lines = -(-(share + extra) // 16) * 16
    thin_rows = jnp.pad(thin_rows, [(0, lines - share - extra), (0, 0)])
    blocks = []
    for j in range(zs):
        blocks.append(
            jnp.concatenate(
                [
                    dw_cols[:, j * qkv_cols : (j + 1) * qkv_cols],
                    dwo[:, j * (width // zs) : (j + 1) * (width // zs)],
                ],
                axis=1,
            )
        )
        blocks.append(thin_rows)
    last, grad_attn = lax.optimization_barrier((jnp.concatenate(blocks, axis=0), grad_attn))
    last = scatter_z(last)
    input_grad = grad_resid + ln_back(grad_attn + part_q, normed1, inv1, gain1)
    attn_dw = last[:share]
    thin_grad = last[share : share + extra].reshape(extra * piece)[:thin_len]
    vec_out = thin_grad[: 8 * share].reshape(8, share)
    return (
        outputs[None],
        input_grad[None],
        vec_out[0],
        vec_out[1],
        attn_dw[:, :qkv_cols],
        vec_out[2],
        vec_out[3],
        attn_dw[:, qkv_cols:],
        vec_out[4],
        vec_out[5],
        vec_out[6],
        up_grad,
        thin_grad[8 * share:],
        down_grad,
        vec_out[7],
    )


def solution(mesh):
    row = P("dp", "seq", None)
    vec = P("dp")
    mat = P("dp", "seq")
    in_specs = (row, vec, row, vec, vec, mat, vec, vec, mat, vec, vec, vec, mat, vec, P("seq", "dp"), vec)
    out_specs = (row, row, vec, vec, mat, vec, vec, mat, vec, vec, vec, mat, vec, P("seq", "dp"), vec)

    return jax.shard_map(shards, mesh=mesh, in_specs=in_specs, out_specs=out_specs, check_vma=False)
```

profile of v0, /device:TPU:0, one launch (start us, length us, event | category | flops | bytes accessed | tf_op | source)
XLA Modules:
  0.0 540.5 jit_solution(2064751240449406992)
XLA Ops:
  14.1 3.0 collective-permute-start.1
  19.6 3.1 collective-permute-start.5
  32.0 3.0 dynamic_update_slice.135
  35.1 3.4 dynamic_update_slice.143
  44.0 3.3 collective-permute-start.12
  47.8 3.0 dynamic_update_slice.136
  50.8 3.0 dynamic_update_slice.137
  53.8 3.0 dynamic_update_slice.138
  59.5 6.5 %collective-permute-start.8 = (bf16[136,272]{1,0:T(8,128)(2,1)}, bf16[136,272]{1,0:T(8,128)(2,1)}, u32[]{:S(2)}, u32[]{:S(2)}) collective-permute-start(bf16[136,272]{1,0:T(8,128)(2,1)} %param.24), channel_id=1, source_target_pairs={{0,2},{1,3},{2,0},{3,1},{4,6},{5,7},{6,4},{7,5},{8,10},{9,11},{10,... | collective-permute-start | bytes 221960 | tf_op jit(solution)/shard_map/ppermute | solution.py:194
  76.6 3.4 dynamic_update_slice.144
  80.0 3.4 dynamic_update_slice.145
  83.3 3.4 dynamic_update_slice.146
  96.7 4.4 dynamic_update_slice.140
  112.6 6.3 %collective-permute-done.15 = bf16[72,3456]{1,0:T(8,128)(2,1)S(1)} collective-permute-done((bf16[72,3456]{1,0:T(8,128)(2,1)}, bf16[72,3456]{1,0:T(8,128)(2,1)S(1)}, u32[]{:S(2)}, u32[]{:S(2)}) %collective-permute-start.15) | collective-permute-done | bytes 497696 | tf_op jit(solution)/shard_map/ppermute | solution.py:185
  136.6 7.4 %collective-permute-done.21 = bf16[136,1088]{1,0:T(8,128)(2,1)S(1)} collective-permute-done((bf16[136,1088]{1,0:T(8,128)(2,1)S(1)}, bf16[136,1088]{1,0:T(8,128)(2,1)S(1)}, u32[]{:S(2)}, u32[]{:S(2)}) %collective-permute-start.21) | collective-permute-done | bytes 295968 | tf_op jit(solution)/shard_map/ppermute | solution.py:185
  147.6 9.1 %collective-permute-done.25 = bf16[136,2176]{1,0:T(8,128)(2,1)S(1)} collective-permute-done((bf16[136,2176]{1,0:T(8,128)(2,1)}, bf16[136,2176]{1,0:T(8,128)(2,1)S(1)}, u32[]{:S(2)}, u32[]{:S(2)}) %collective-permute-start.25) | collective-permute-done | bytes 591904 | tf_op jit(solution)/shard_map/ppermute | solution.py:185
  161.4 10.9 %add_convert_fusion.kv_ref = bf16[1024,2304]{1,0:T(8,128)(2,1)} fusion(f32[2304]{0:T(1024)S(1)} %copy-done.31, bf16[1088,3456]{1,0:T(8,128)(2,1)} %bitcast.275, f32[1088]{0:T(1024)S(1)} %copy-done.26, f32[1088]{0:T(1024)S(1)} %mul.192, f32[1024]{0:T(1024)S(1)} %add_rsqrt_fusion, f32[1024]{0:T(1024)S(1)} %broadcast_multiply_fusion, ...), kind=kOutput, calls=%fused_computation.1 | convolution fusion | flops 5145231360 | bytes 11986432 | tf_op jit(solution)/shard_map/dot_general | solution.py:19
  172.3 19.6 %attend.1 = (bf16[256,1152]{1,0:T(8,128)(2,1)}, f32[9,2,256]{2,1,0:T(2,128)}) custom-call(s32[2]{0:T(128)} %pad_add_fusion.meta, bf16[256,1152]{1,0:T(8,128)(2,1)} %fusion.19.q_ref, bf16[1024,2304]{1,0:T(8,128)(2,1)} %add_convert_fusion.kv_ref), custom_call_target="tpu_custom_call" | custom-call | flops 2415919104 | bytes 7077888 | tf_op jit(solution)/shard_map/attend/pallas_call | solution.py:90
  193.1 3.0 fusion.103
  202.1 3.4 bitcast_dynamic-update-slice_fusion
  205.5 3.3 bitcast_dynamic-update-slice_fusion.1
  208.8 36.1 %all-gather.7.cloned.1.call-done = bf16[1024,1088]{0,1:T(8,128)(2,1)} async-done(((bf16[256,1088]{0,1:T(8,128)(2,1)}), bf16[1024,1088]{0,1:T(8,128)(2,1)}) %all-gather.7.cloned.1.call-update) | async-done | bytes 2228240 | tf_op jit(solution)/shard_map/all_gather | solution.py:240
  244.9 5.7 %convolution_add_fusion = f32[1024,1088]{0,1:T(8,128)S(1)} fusion(bf16[1024,1088]{0,1:T(8,128)(2,1)} %all-gather.7.cloned.1.call-done, f32[1088]{0:T(1024)S(1)} %dynamic_slice.83, bf16[1088,2176]{1,0:T(8,128)(2,1)} %bitcast.58), kind=kOutput, calls=%fused_computation.24 | convolution fusion | flops 2425421824 | bytes 9195776 | tf_op jit(solution)/shard_map/dot_general | solution.py:19
  250.6 11.3 %fusion.104 = (bf16[1088]{0:T(1024)(128)(2,1)S(1)}, bf16[1024,1088]{0,1:T(8,128)(2,1)S(1)}) fusion(f32[1024,1088]{0,1:T(8,128)S(1)} %convolution_add_fusion, bf16[1088,2176]{1,0:T(8,128)(2,1)} %bitcast.58, bf16[1024,1088]{0,1:T(8,128)(2,1)S(1)} %copy-done.35, bf16[1024]{0:T(1024)(128)(2,1)S(1)} %fusion.88), kind=kOutput, calls=%fused_computation.240 | convolution fusion | flops 2447703040 | bytes 11423872 | tf_op jit(solution)/shard_map/dot_general | solution.py:19
  263.3 6.0 %convolution_convert_fusion.6 = bf16[1024,1088]{0,1:T(8,128)(2,1)} fusion(bf16[1088,2176]{1,0:T(8,128)(2,1)} %bitcast.58, bf16[1024,1088]{0,1:T(8,128)(2,1)S(1)} %get-tuple-element.120), kind=kOutput, calls=%fused_computation.39 | convolution fusion | flops 2425421824 | bytes 6963200 | tf_op jit(solution)/shard_map/dot_general | solution.py:19
  269.4 5.5 %convolution_convert_fusion.4 = bf16[1088,1088]{1,0:T(8,128)(2,1)S(1)} fusion(bf16[1024,1088]{0,1:T(8,128)(2,1)} %all-gather.7.cloned.1.call-done, bf16[1024,1088]{0,1:T(8,128)(2,1)} %copy-done.38), kind=kOutput, calls=%fused_computation.5 | convolution fusion | flops 2425491456 | bytes 6823936 | tf_op jit(solution)/shard_map/dot_general | solution.py:19
  275.0 6.4 %convolution_convert_fusion.3 = bf16[1088,1088]{1,0:T(8,128)(2,1)S(1)} fusion(bf16[1024,1088]{0,1:T(8,128)(2,1)S(1)} %copy-done.36, bf16[1024]{0:T(1024)(128)(2,1)S(1)} %fusion.88, f32[1024,1088]{0,1:T(8,128)} %copy-done.37), kind=kOutput, calls=%fused_computation.4 | convolution fusion | flops 2436632576 | bytes 9054208 | tf_op jit(solution)/shard_map/dot_general | solution.py:19
  283.8 7.1 %convolution_convert_fusion.5 = bf16[1024,1088]{0,1:T(8,128)(2,1)} fusion(bf16[1088,2176]{1,0:T(8,128)(2,1)} %bitcast.58, f32[1024,1088]{0,1:T(8,128)S(1)} %bitcast.315), kind=kOutput, calls=%fused_computation.38 | convolution fusion | flops 2435448832 | bytes 9191424 | tf_op jit(solution)/shard_map/dot_general | solution.py:19
  292.0 3.5 fusion.5
  301.7 11.7 %reduce-scatter.5.cloned.1.call-done = bf16[256,1088]{0,1:T(8,128)(2,1)} async-done(((bf16[1024,1088]{0,1:T(8,128)(2,1)}), bf16[256,1088]{0,1:T(8,128)(2,1)}) %reduce-scatter.5.cloned.1.call-update) | async-done | bytes 557072 | tf_op jit(solution)/shard_map/reduce_scatter | solution.py:244
  321.0 3.5 convolution_convert_fusion.1
  324.5 21.4 %attend_back.1 = (bf16[256,1152]{1,0:T(8,128)(2,1)}, bf16[1024,2304]{1,0:T(8,128)(2,1)}) custom-call(s32[2]{0:T(128)} %pad_add_fusion.meta, bf16[256,1152]{1,0:T(8,128)(2,1)} %fusion.19.q_ref, bf16[1024,2304]{1,0:T(8,128)(2,1)} %add_convert_fusion.kv_ref, f32[9,2,256]{2,1,0:T(2,128)} %get-tuple-element.42.lse_ref, bf16[256,1152]{1,0:T(8,128)(2,1)} %pad.48.g_ref), custom_call_target="tpu_custom_call" | custom-call | flops 6039797760 | bytes 14155776 | tf_op jit(solution)/shard_map/attend_back/pallas_call | solution.py:155
  345.9 14.6 %reduce-scatter.7.cloned.1.call-done = bf16[256,1088]{0,1:T(8,128)(2,1)} async-done(((bf16[1024,1088]{0,1:T(8,128)(2,1)}), bf16[256,1088]{0,1:T(8,128)(2,1)}) %reduce-scatter.7.cloned.1.call-update) | async-done | bytes 557072 | tf_op jit(solution)/shard_map/reduce_scatter | solution.py:244
  365.0 10.1 %convolution_convert_fusion = bf16[1088,2304]{1,0:T(8,128)(2,1)} fusion(bf16[1024,2304]{1,0:T(8,128)(2,1)} %get-tuple-element.53, f32[1088]{0:T(1024)S(1)} %copy-done.26, f32[1088]{0:T(1024)S(1)} %mul.192, f32[1024]{0:T(1024)S(1)} %add_rsqrt_fusion, f32[1024]{0:T(1024)S(1)} %broadcast_multiply_fusion, bf16[1,1024,1088]{1,2,0:T(8,128)(2,1)S(1)} %copy-done.7), kind=kOutput, calls=%fused_computation | convolution fusion | flops 5143019520 | bytes 11977216 | tf_op jit(solution)/shard_map/dot_general | solution.py:19
  375.1 6.1 %pad_maximum_fusion = bf16[1088,3456]{1,0:T(8,128)(2,1)} fusion(bf16[1088,2304]{1,0:T(8,128)(2,1)} %convolution_convert_fusion, bf16[1088,1152]{1,0:T(8,128)(2,1)S(1)} %convolution_convert_fusion.2), kind=kLoop, calls=%fused_computation.6 | loop fusion | flops 15040512 | bytes 15040512 | tf_op jit(solution)/shard_map/concatenate | solution.py:372
  381.3 3.9 fusion.95
  388.3 3.0 reduce.1
  391.5 4.3 dynamic-slice_bitcast_fusion
  396.4 10.3 %fusion.93 = (f32[1088]{0:T(1024)S(1)}, f32[1088]{0:T(1024)S(1)}, bf16[1024,1088]{0,1:T(8,128)(2,1)}) fusion(f32[1024]{0:T(1024)S(1)} %add_rsqrt_fusion, f32[1024]{0:T(1024)S(1)} %broadcast_multiply_fusion, bf16[1,1024,1088]{1,2,0:T(8,128)(2,1)S(1)} %copy-done.8, bf16[1024,2304]{1,0:T(8,128)(2,1)} %get-tuple-element.53, bf16[1088,3456]{1,0:T(8,128)(2,1)} %bitcast.277), kind=kOutput, calls=%fused_computation.229 | convolution fusion | flops 5141624832 | bytes 14205440 | tf_op jit(solution)/shard_map/dot_general | solution.py:19
  407.4 3.1 fusion.44
  419.7 4.1 fusion
  430.9 3.9 collective-permute-done.36
  434.8 5.5 %collective-permute-done.35 = bf16[136,1088]{1,0:T(8,128)(2,1)} collective-permute-done((bf16[136,1088]{1,0:T(8,128)(2,1)}, bf16[136,1088]{1,0:T(8,128)(2,1)}, u32[]{:S(2)}, u32[]{:S(2)}) %collective-permute-start.35) | collective-permute-done | bytes 295968 | tf_op jit(solution)/shard_map/ppermute | solution.py:185
  442.3 9.7 %reduce-scatter.9.cloned.1.call-done = bf16[256,1088]{0,1:T(8,128)(2,1)} async-done(((bf16[1024,1088]{0,1:T(8,128)(2,1)}), bf16[256,1088]{0,1:T(8,128)(2,1)}) %reduce-scatter.9.cloned.1.call-update) | async-done | bytes 557072 | tf_op jit(solution)/shard_map/reduce_scatter | solution.py:244
  454.2 19.7 %collective-permute-done.32 = bf16[136,3456]{1,0:T(8,128)(2,1)} collective-permute-done((bf16[136,3456]{1,0:T(8,128)(2,1)}, bf16[136,3456]{1,0:T(8,128)(2,1)}, u32[]{:S(2)}, u32[]{:S(2)}) %collective-permute-start.32) | collective-permute-done | bytes 940064 | tf_op jit(solution)/shard_map/ppermute | solution.py:185
  473.8 6.6 %collective-permute-done.31 = bf16[136,3456]{1,0:T(8,128)(2,1)} collective-permute-done((bf16[136,3456]{1,0:T(8,128)(2,1)}, bf16[136,3456]{1,0:T(8,128)(2,1)}, u32[]{:S(2)}, u32[]{:S(2)}) %collective-permute-start.31) | collective-permute-done | bytes 940064 | tf_op jit(solution)/shard_map/ppermute | solution.py:185
  486.8 3.4 slice_reduce_fusion
  501.9 25.2 %reduce-scatter.11.cloned.1.call-done = bf16[144,1088]{1,0:T(8,128)(2,1)} async-done(((bf16[576,1088]{1,0:T(8,128)(2,1)}), bf16[144,1088]{1,0:T(8,128)(2,1)}) %reduce-scatter.11.cloned.1.call-update) | async-done | bytes 313360 | tf_op jit(solution)/shard_map/reduce_scatter | solution.py:244
  (389 shorter events, 163.5 us)
Async XLA Ops:
  7.2 151.2 %all-gather.9.cloned.1.call-start = ((), (), s32[]{:S(2)}) async-start(), calls=%async_computation.10 | async-start | bytes 2785280 | tf_op jit(solution)/shard_map/all_gather | solution.py:240
  7.9 184.0 %all-gather.5.cloned.1.call-start = ((), (), s32[]{:S(2)}) async-start(), calls=%async_computation.4 | async-start | bytes 2785280 | tf_op jit(solution)/shard_map/all_gather | solution.py:240
  14.1 16.4 %collective-permute-start.1 = (bf16[1,1632]{1,0:T(2,128)(2,1)S(1)}, bf16[1,1632]{1,0:T(2,128)(2,1)S(1)}, u32[]{:S(2)}, u32[]{:S(2)}) collective-permute-start(bf16[1,1632]{1,0:T(2,128)(2,1)S(1)} %pad_maximum_fusion.6), channel_id=1, source_target_pairs={{0,16},{4,20},{8,24},{12,28},{16,0},{20,4},{24,8},{28,12},{1,17},{... | collective-permute-start | bytes 9800 | tf_op jit(solution)/shard_map/ppermute | solution.py:185
  17.1 11.0 %collective-permute-start = (bf16[1,1632]{1,0:T(2,128)(2,1)S(1)}, bf16[1,1632]{1,0:T(2,128)(2,1)S(1)}, u32[]{:S(2)}, u32[]{:S(2)}) collective-permute-start(bf16[1,1632]{1,0:T(2,128)(2,1)S(1)} %pad_maximum_fusion.6), channel_id=1, source_target_pairs={{0,8},{4,12},{8,0},{12,4},{16,24},{20,28},{24,16},{28,20},{1,9},{5... | collective-permute-start | bytes 9800 | tf_op jit(solution)/shard_map/ppermute | solution.py:185
  18.6 12.0 %collective-permute-start.2 = (bf16[1,1632]{1,0:T(2,128)(2,1)S(1)}, bf16[1,1632]{1,0:T(2,128)(2,1)S(1)}, u32[]{:S(2)}, u32[]{:S(2)}) collective-permute-start(bf16[1,1632]{1,0:T(2,128)(2,1)S(1)} %pad_maximum_fusion.6), channel_id=1, source_target_pairs={{0,24},{4,28},{8,16},{12,20},{16,8},{20,12},{24,0},{28,4},{1,25},{... | collective-permute-start | bytes 9800 | tf_op jit(solution)/shard_map/ppermute | solution.py:185
  19.6 24.4 %collective-permute-start.5 = (bf16[64,816]{1,0:T(8,128)(2,1)S(1)}, bf16[64,816]{1,0:T(8,128)(2,1)S(1)}, u32[]{:S(2)}, u32[]{:S(2)}) collective-permute-start(bf16[64,816]{1,0:T(8,128)(2,1)S(1)} %get-tuple-element.112), channel_id=1, source_target_pairs={{0,2},{1,3},{2,0},{3,1},{4,6},{5,7},{6,4},{7,5},{8,10},{9,11},{10,... | collective-permute-start | bytes 313352 | tf_op jit(solution)/shard_map/ppermute | solution.py:194
  22.7 24.7 %collective-permute-start.4 = (bf16[64,816]{1,0:T(8,128)(2,1)S(1)}, bf16[64,816]{1,0:T(8,128)(2,1)S(1)}, u32[]{:S(2)}, u32[]{:S(2)}) collective-permute-start(bf16[64,816]{1,0:T(8,128)(2,1)S(1)} %get-tuple-element.112), channel_id=1, source_target_pairs={{0,1},{1,2},{2,3},{3,0},{4,5},{5,6},{6,7},{7,4},{8,9},{9,10},{10,1... | collective-permute-start | bytes 313352 | tf_op jit(solution)/shard_map/ppermute | solution.py:194
  24.3 220.6 %all-gather.7.cloned.1.call-start = ((), (), s32[]{:S(2)}) async-start(), calls=%async_computation.5 | async-start | bytes 2785280 | tf_op jit(solution)/shard_map/all_gather | solution.py:240
  28.1 19.5 %collective-permute-start.6 = (bf16[64,816]{1,0:T(8,128)(2,1)S(1)}, bf16[64,816]{1,0:T(8,128)(2,1)S(1)}, u32[]{:S(2)}, u32[]{:S(2)}) collective-permute-start(bf16[64,816]{1,0:T(8,128)(2,1)S(1)} %get-tuple-element.112), channel_id=1, source_target_pairs={{0,3},{1,0},{2,1},{3,2},{4,7},{5,4},{6,5},{7,6},{8,11},{9,8},{10,9... | collective-permute-start | bytes 313352 | tf_op jit(solution)/shard_map/ppermute | solution.py:194
  30.5 41.7 %collective-permute-start.11 = (bf16[72,816]{1,0:T(8,128)(2,1)S(1)}, bf16[72,816]{1,0:T(8,128)(2,1)S(1)}, u32[]{:S(2)}, u32[]{:S(2)}) collective-permute-start(bf16[72,816]{1,0:T(8,128)(2,1)S(1)} %get-tuple-element.110), channel_id=1, source_target_pairs={{0,2},{1,3},{2,0},{3,1},{4,6},{5,7},{6,4},{7,5},{8,10},{9,11},{10,... | collective-permute-start | bytes 352520 | tf_op jit(solution)/shard_map/ppermute | solution.py:194
  30.8 8.0 %collective-permute-start.3 = (bf16[4,1,1632]{2,0,1:T(4,128)(2,1)S(1)}, bf16[4,1,1632]{2,0,1:T(4,128)(2,1)S(1)}, u32[]{:S(2)}, u32[]{:S(2)}) collective-permute-start(bf16[4,1,1632]{2,0,1:T(4,128)(2,1)S(1)} %dynamic_update_slice.132), channel_id=1, source_target_pairs={{0,4},{4,0},{8,12},{12,8},{16,20},{20,16},{24,28},{28,24},{1,5},{5... | collective-permute-start | bytes 39176 | tf_op jit(solution)/shard_map/ppermute | solution.py:185
  38.7 34.2 %collective-permute-start.10 = (bf16[72,816]{1,0:T(8,128)(2,1)S(1)}, bf16[72,816]{1,0:T(8,128)(2,1)S(1)}, u32[]{:S(2)}, u32[]{:S(2)}) collective-permute-start(bf16[72,816]{1,0:T(8,128)(2,1)S(1)} %get-tuple-element.110), channel_id=1, source_target_pairs={{0,1},{1,2},{2,3},{3,0},{4,5},{5,6},{6,7},{7,4},{8,9},{9,10},{10,1... | collective-permute-start | bytes 352520 | tf_op jit(solution)/shard_map/ppermute | solution.py:194
  44.0 30.8 %collective-permute-start.12 = (bf16[72,816]{1,0:T(8,128)(2,1)S(1)}, bf16[72,816]{1,0:T(8,128)(2,1)S(1)}, u32[]{:S(2)}, u32[]{:S(2)}) collective-permute-start(bf16[72,816]{1,0:T(8,128)(2,1)S(1)} %get-tuple-element.110), channel_id=1, source_target_pairs={{0,3},{1,0},{2,1},{3,2},{4,7},{5,4},{6,5},{7,6},{8,11},{9,8},{10,9... | collective-permute-start | bytes 352520 | tf_op jit(solution)/shard_map/ppermute | solution.py:194
  59.0 30.2 %collective-permute-start.9 = (bf16[136,272]{1,0:T(8,128)(2,1)}, bf16[136,272]{1,0:T(8,128)(2,1)}, u32[]{:S(2)}, u32[]{:S(2)}) collective-permute-start(bf16[136,272]{1,0:T(8,128)(2,1)} %param.24), channel_id=1, source_target_pairs={{0,3},{1,0},{2,1},{3,2},{4,7},{5,4},{6,5},{7,6},{8,11},{9,8},{10,9... | collective-permute-start | bytes 221960 | tf_op jit(solution)/shard_map/ppermute | solution.py:194
  59.5 31.2 %collective-permute-start.8 = (bf16[136,272]{1,0:T(8,128)(2,1)}, bf16[136,272]{1,0:T(8,128)(2,1)}, u32[]{:S(2)}, u32[]{:S(2)}) collective-permute-start(bf16[136,272]{1,0:T(8,128)(2,1)} %param.24), channel_id=1, source_target_pairs={{0,2},{1,3},{2,0},{3,1},{4,6},{5,7},{6,4},{7,5},{8,10},{9,11},{10,... | collective-permute-start | bytes 221960 | tf_op jit(solution)/shard_map/ppermute | solution.py:194
  72.2 21.2 %collective-permute-start.7 = (bf16[136,272]{1,0:T(8,128)(2,1)}, bf16[136,272]{1,0:T(8,128)(2,1)}, u32[]{:S(2)}, u32[]{:S(2)}) collective-permute-start(bf16[136,272]{1,0:T(8,128)(2,1)} %param.24), channel_id=1, source_target_pairs={{0,1},{1,2},{2,3},{3,0},{4,5},{5,6},{6,7},{7,4},{8,9},{9,10},{10,1... | collective-permute-start | bytes 221960 | tf_op jit(solution)/shard_map/ppermute | solution.py:194
  73.0 46.1 %collective-permute-start.18 = (bf16[64,3456]{1,0:T(8,128)(2,1)}, bf16[64,3456]{1,0:T(8,128)(2,1)}, u32[]{:S(2)}, u32[]{:S(2)}) collective-permute-start(bf16[64,3456]{1,0:T(8,128)(2,1)} %pad_maximum_fusion.5), channel_id=1, source_target_pairs={{0,16},{4,20},{8,24},{12,28},{16,0},{20,4},{24,8},{28,12},{1,17},{... | collective-permute-start | bytes 1327112 | tf_op jit(solution)/shard_map/ppermute | solution.py:185
  74.8 32.3 %collective-permute-start.17 = (bf16[64,3456]{1,0:T(8,128)(2,1)}, bf16[64,3456]{1,0:T(8,128)(2,1)}, u32[]{:S(2)}, u32[]{:S(2)}) collective-permute-start(bf16[64,3456]{1,0:T(8,128)(2,1)} %pad_maximum_fusion.5), channel_id=1, source_target_pairs={{0,8},{4,12},{8,0},{12,4},{16,24},{20,28},{24,16},{28,20},{1,9},{5... | collective-permute-start | bytes 1327112 | tf_op jit(solution)/shard_map/ppermute | solution.py:185
  89.2 31.7 %collective-permute-start.19 = (bf16[64,3456]{1,0:T(8,128)(2,1)}, bf16[64,3456]{1,0:T(8,128)(2,1)}, u32[]{:S(2)}, u32[]{:S(2)}) collective-permute-start(bf16[64,3456]{1,0:T(8,128)(2,1)} %pad_maximum_fusion.5), channel_id=1, source_target_pairs={{0,24},{4,28},{8,16},{12,20},{16,8},{20,12},{24,0},{28,4},{1,25},{... | collective-permute-start | bytes 1327112 | tf_op jit(solution)/shard_map/ppermute | solution.py:185
  90.7 20.8 %collective-permute-start.14 = (bf16[72,3456]{1,0:T(8,128)(2,1)}, bf16[72,3456]{1,0:T(8,128)(2,1)}, u32[]{:S(2)}, u32[]{:S(2)}) collective-permute-start(bf16[72,3456]{1,0:T(8,128)(2,1)} %pad_maximum_fusion.4), channel_id=1, source_target_pairs={{0,16},{4,20},{8,24},{12,28},{16,0},{20,4},{24,8},{28,12},{1,17},{... | collective-permute-start | bytes 1493000 | tf_op jit(solution)/shard_map/ppermute | solution.py:185
  93.4 17.0 %collective-permute-start.13 = (bf16[72,3456]{1,0:T(8,128)(2,1)}, bf16[72,3456]{1,0:T(8,128)(2,1)}, u32[]{:S(2)}, u32[]{:S(2)}) collective-permute-start(bf16[72,3456]{1,0:T(8,128)(2,1)} %pad_maximum_fusion.4), channel_id=1, source_target_pairs={{0,8},{4,12},{8,0},{12,4},{16,24},{20,28},{24,16},{28,20},{1,9},{5... | collective-permute-start | bytes 1493000 | tf_op jit(solution)/shard_map/ppermute | solution.py:185
  107.1 11.8 %collective-permute-start.15 = (bf16[72,3456]{1,0:T(8,128)(2,1)}, bf16[72,3456]{1,0:T(8,128)(2,1)S(1)}, u32[]{:S(2)}, u32[]{:S(2)}) collective-permute-start(bf16[72,3456]{1,0:T(8,128)(2,1)} %pad_maximum_fusion.4), channel_id=1, source_target_pairs={{0,24},{4,28},{8,16},{12,20},{16,8},{20,12},{24,0},{28,4},{1,25},{... | collective-permute-start | bytes 1493000 | tf_op jit(solution)/shard_map/ppermute | solution.py:185
  127.0 18.6 %collective-permute-start.23 = (bf16[136,1088]{1,0:T(8,128)(2,1)S(1)}, bf16[136,1088]{1,0:T(8,128)(2,1)S(1)}, u32[]{:S(2)}, u32[]{:S(2)}) collective-permute-start(bf16[136,1088]{1,0:T(8,128)(2,1)S(1)} %reshape.331), channel_id=1, source_target_pairs={{0,24},{4,28},{8,16},{12,20},{16,8},{20,12},{24,0},{28,4},{1,25},{... | collective-permute-start | bytes 887816 | tf_op jit(solution)/shard_map/ppermute | solution.py:185
  127.5 18.1 %collective-permute-start.22 = (bf16[136,1088]{1,0:T(8,128)(2,1)S(1)}, bf16[136,1088]{1,0:T(8,128)(2,1)S(1)}, u32[]{:S(2)}, u32[]{:S(2)}) collective-permute-start(bf16[136,1088]{1,0:T(8,128)(2,1)S(1)} %reshape.331), channel_id=1, source_target_pairs={{0,16},{4,20},{8,24},{12,28},{16,0},{20,4},{24,8},{28,12},{1,17},{... | collective-permute-start | bytes 887816 | tf_op jit(solution)/shard_map/ppermute | solution.py:185
  129.1 14.9 %collective-permute-start.21 = (bf16[136,1088]{1,0:T(8,128)(2,1)S(1)}, bf16[136,1088]{1,0:T(8,128)(2,1)S(1)}, u32[]{:S(2)}, u32[]{:S(2)}) collective-permute-start(bf16[136,1088]{1,0:T(8,128)(2,1)S(1)} %reshape.331), channel_id=1, source_target_pairs={{0,8},{4,12},{8,0},{12,4},{16,24},{20,28},{24,16},{28,20},{1,9},{5... | collective-permute-start | bytes 887816 | tf_op jit(solution)/shard_map/ppermute | solution.py:185
  133.4 24.2 %collective-permute-start.26 = (bf16[136,2176]{1,0:T(8,128)(2,1)}, bf16[136,2176]{1,0:T(8,128)(2,1)S(1)}, u32[]{:S(2)}, u32[]{:S(2)}) collective-permute-start(bf16[136,2176]{1,0:T(8,128)(2,1)} %get-tuple-element.80), channel_id=1, source_target_pairs={{0,16},{4,20},{8,24},{12,28},{16,0},{20,4},{24,8},{28,12},{1,17},{... | collective-permute-start | bytes 1775624 | tf_op jit(solution)/shard_map/ppermute | solution.py:185
  133.8 22.9 %collective-permute-start.25 = (bf16[136,2176]{1,0:T(8,128)(2,1)}, bf16[136,2176]{1,0:T(8,128)(2,1)S(1)}, u32[]{:S(2)}, u32[]{:S(2)}) collective-permute-start(bf16[136,2176]{1,0:T(8,128)(2,1)} %get-tuple-element.80), channel_id=1, source_target_pairs={{0,8},{4,12},{8,0},{12,4},{16,24},{20,28},{24,16},{28,20},{1,9},{5... | collective-permute-start | bytes 1775624 | tf_op jit(solution)/shard_map/ppermute | solution.py:185
  144.0 53.5 %collective-permute-start.27 = (bf16[136,2176]{1,0:T(8,128)(2,1)}, bf16[136,2176]{1,0:T(8,128)(2,1)}, u32[]{:S(2)}, u32[]{:S(2)}) collective-permute-start(bf16[136,2176]{1,0:T(8,128)(2,1)} %get-tuple-element.80), channel_id=1, source_target_pairs={{0,24},{4,28},{8,16},{12,20},{16,8},{20,12},{24,0},{28,4},{1,25},{... | collective-permute-start | bytes 1775624 | tf_op jit(solution)/shard_map/ppermute | solution.py:185
  145.7 46.2 %collective-permute-start.24 = (bf16[4,136,1088]{2,1,0:T(8,128)(2,1)S(1)}, bf16[4,136,1088]{2,1,0:T(8,128)(2,1)S(1)}, u32[]{:S(2)}, u32[]{:S(2)}) collective-permute-start(bf16[4,136,1088]{2,1,0:T(8,128)(2,1)S(1)} %bitcast_dynamic-update-slice_fusion.20), channel_id=1, source_target_pairs={{0,4},{4,0},{8,12},{12,8},{16,20},{20,16},{24,28},{28,24},{1,5},{5... | collective-permute-start | bytes 3551240 | tf_op jit(solution)/shard_map/ppermute | solution.py:185
  197.4 115.9 %reduce-scatter.5.cloned.1.call-start = ((), (), s32[]{:S(2)}) async-start(), calls=%async_computation.6 | async-start | bytes 2785280 | tf_op jit(solution)/shard_map/reduce_scatter | solution.py:244
  269.4 91.2 %reduce-scatter.7.cloned.1.call-start = ((), (), s32[]{:S(2)}) async-start(), calls=%async_computation.7 | async-start | bytes 2785280 | tf_op jit(solution)/shard_map/reduce_scatter | solution.py:244
  283.7 8.3 %collective-permute-start.41 = (bf16[4,136,2176]{2,1,0:T(8,128)(2,1)}, bf16[4,136,2176]{2,1,0:T(8,128)(2,1)}, u32[]{:S(2)}, u32[]{:S(2)}) collective-permute-start(bf16[4,136,2176]{2,1,0:T(8,128)(2,1)} %fusion.22), channel_id=1, source_target_pairs={{0,4},{4,0},{8,12},{12,8},{16,20},{20,16},{24,28},{28,24},{1,5},{5... | collective-permute-start | bytes 7102472 | tf_op jit(solution)/shard_map/ppermute | solution.py:185
  290.9 161.2 %reduce-scatter.9.cloned.1.call-start = ((), (), s32[]{:S(2)}) async-start(), calls=%async_computation.8 | async-start | bytes 2785280 | tf_op jit(solution)/shard_map/reduce_scatter | solution.py:244
  298.2 109.1 %collective-permute-start.42 = (bf16[136,2176]{1,0:T(8,128)(2,1)}, bf16[136,2176]{1,0:T(8,128)(2,1)}, u32[]{:S(2)}, u32[]{:S(2)}) collective-permute-start(bf16[136,2176]{1,0:T(8,128)(2,1)} %get-tuple-element.85), channel_id=1, source_target_pairs={{0,8},{4,12},{8,0},{12,4},{16,24},{20,28},{24,16},{28,20},{1,9},{5... | collective-permute-start | bytes 1775624 | tf_op jit(solution)/shard_map/ppermute | solution.py:185
  299.7 107.7 %collective-permute-start.44 = (bf16[136,2176]{1,0:T(8,128)(2,1)}, bf16[136,2176]{1,0:T(8,128)(2,1)}, u32[]{:S(2)}, u32[]{:S(2)}) collective-permute-start(bf16[136,2176]{1,0:T(8,128)(2,1)} %get-tuple-element.86), channel_id=1, source_target_pairs={{0,24},{4,28},{8,16},{12,20},{16,8},{20,12},{24,0},{28,4},{1,25},{... | collective-permute-start | bytes 1775624 | tf_op jit(solution)/shard_map/ppermute | solution.py:185
  301.1 106.3 %collective-permute-start.43 = (bf16[136,2176]{1,0:T(8,128)(2,1)}, bf16[136,2176]{1,0:T(8,128)(2,1)}, u32[]{:S(2)}, u32[]{:S(2)}) collective-permute-start(bf16[136,2176]{1,0:T(8,128)(2,1)} %get-tuple-element.87), channel_id=1, source_target_pairs={{0,16},{4,20},{8,24},{12,28},{16,0},{20,4},{24,8},{28,12},{1,17},{... | collective-permute-start | bytes 1775624 | tf_op jit(solution)/shard_map/ppermute | solution.py:185
  388.2 25.9 %collective-permute-start.33 = (bf16[4,136,1088]{2,1,0:T(8,128)(2,1)}, bf16[4,136,1088]{2,1,0:T(8,128)(2,1)}, u32[]{:S(2)}, u32[]{:S(2)}) collective-permute-start(bf16[4,136,1088]{2,1,0:T(8,128)(2,1)} %dynamic-slice_bitcast_fusion.1), channel_id=1, source_target_pairs={{0,4},{4,0},{8,12},{12,8},{16,20},{20,16},{24,28},{28,24},{1,5},{5... | collective-permute-start | bytes 3551240 | tf_op jit(solution)/shard_map/ppermute | solution.py:185
  395.9 22.5 %collective-permute-start.29 = (bf16[4,136,3456]{2,1,0:T(8,128)(2,1)}, bf16[4,136,3456]{2,1,0:T(8,128)(2,1)}, u32[]{:S(2)}, u32[]{:S(2)}) collective-permute-start(bf16[4,136,3456]{2,1,0:T(8,128)(2,1)} %dynamic-slice_bitcast_fusion), channel_id=1, source_target_pairs={{0,4},{4,0},{8,12},{12,8},{16,20},{20,16},{24,28},{28,24},{1,5},{5... | collective-permute-start | bytes 11280392 | tf_op jit(solution)/shard_map/ppermute | solution.py:185
  406.9 120.2 %reduce-scatter.11.cloned.1.call-start = ((), (), s32[]{:S(2)}) async-start(), calls=%async_computation.9 | async-start | bytes 1658880 | tf_op jit(solution)/shard_map/reduce_scatter | solution.py:244
  410.6 16.0 %collective-permute-start.38 = (bf16[1,1632]{1,0:T(2,128)(2,1)S(1)}, bf16[1,1632]{1,0:T(2,128)(2,1)S(1)}, u32[]{:S(2)}, u32[]{:S(2)}) collective-permute-start(bf16[1,1632]{1,0:T(2,128)(2,1)S(1)} %get-tuple-element.114), channel_id=1, source_target_pairs={{0,8},{4,12},{8,0},{12,4},{16,24},{20,28},{24,16},{28,20},{1,9},{5... | collective-permute-start | bytes 9800 | tf_op jit(solution)/shard_map/ppermute | solution.py:185
  412.1 15.1 %collective-permute-start.40 = (bf16[1,1632]{1,0:T(2,128)(2,1)S(1)}, bf16[1,1632]{1,0:T(2,128)(2,1)S(1)}, u32[]{:S(2)}, u32[]{:S(2)}) collective-permute-start(bf16[1,1632]{1,0:T(2,128)(2,1)S(1)} %get-tuple-element.115), channel_id=1, source_target_pairs={{0,24},{4,28},{8,16},{12,20},{16,8},{20,12},{24,0},{28,4},{1,25},{... | collective-permute-start | bytes 9800 | tf_op jit(solution)/shard_map/ppermute | solution.py:185
  413.6 15.1 %collective-permute-start.39 = (bf16[1,1632]{1,0:T(2,128)(2,1)S(1)}, bf16[1,1632]{1,0:T(2,128)(2,1)S(1)}, u32[]{:S(2)}, u32[]{:S(2)}) collective-permute-start(bf16[1,1632]{1,0:T(2,128)(2,1)S(1)} %get-tuple-element.116), channel_id=1, source_target_pairs={{0,16},{4,20},{8,24},{12,28},{16,0},{20,4},{24,8},{28,12},{1,17},{... | collective-permute-start | bytes 9800 | tf_op jit(solution)/shard_map/ppermute | solution.py:185
  416.9 13.2 %collective-permute-start.34 = (bf16[136,1088]{1,0:T(8,128)(2,1)S(1)}, bf16[136,1088]{1,0:T(8,128)(2,1)S(1)}, u32[]{:S(2)}, u32[]{:S(2)}) collective-permute-start(bf16[136,1088]{1,0:T(8,128)(2,1)S(1)} %get-tuple-element.88), channel_id=1, source_target_pairs={{0,8},{4,12},{8,0},{12,4},{16,24},{20,28},{24,16},{28,20},{1,9},{5... | collective-permute-start | bytes 887816 | tf_op jit(solution)/shard_map/ppermute | solution.py:185
  418.4 16.4 %collective-permute-start.36 = (bf16[136,1088]{1,0:T(8,128)(2,1)}, bf16[136,1088]{1,0:T(8,128)(2,1)S(1)}, u32[]{:S(2)}, u32[]{:S(2)}) collective-permute-start(bf16[136,1088]{1,0:T(8,128)(2,1)} %get-tuple-element.89), channel_id=1, source_target_pairs={{0,24},{4,28},{8,16},{12,20},{16,8},{20,12},{24,0},{28,4},{1,25},{... | collective-permute-start | bytes 887816 | tf_op jit(solution)/shard_map/ppermute | solution.py:185
  426.6 13.6 %collective-permute-start.35 = (bf16[136,1088]{1,0:T(8,128)(2,1)}, bf16[136,1088]{1,0:T(8,128)(2,1)}, u32[]{:S(2)}, u32[]{:S(2)}) collective-permute-start(bf16[136,1088]{1,0:T(8,128)(2,1)} %get-tuple-element.90), channel_id=1, source_target_pairs={{0,16},{4,20},{8,24},{12,28},{16,0},{20,4},{24,8},{28,12},{1,17},{... | collective-permute-start | bytes 887816 | tf_op jit(solution)/shard_map/ppermute | solution.py:185
  427.2 26.9 %collective-permute-start.30 = (bf16[136,3456]{1,0:T(8,128)(2,1)}, bf16[136,3456]{1,0:T(8,128)(2,1)}, u32[]{:S(2)}, u32[]{:S(2)}) collective-permute-start(bf16[136,3456]{1,0:T(8,128)(2,1)} %get-tuple-element.82), channel_id=1, source_target_pairs={{0,8},{4,12},{8,0},{12,4},{16,24},{20,28},{24,16},{28,20},{1,9},{5... | collective-permute-start | bytes 2820104 | tf_op jit(solution)/shard_map/ppermute | solution.py:185
  428.7 45.1 %collective-permute-start.32 = (bf16[136,3456]{1,0:T(8,128)(2,1)}, bf16[136,3456]{1,0:T(8,128)(2,1)}, u32[]{:S(2)}, u32[]{:S(2)}) collective-permute-start(bf16[136,3456]{1,0:T(8,128)(2,1)} %get-tuple-element.83), channel_id=1, source_target_pairs={{0,24},{4,28},{8,16},{12,20},{16,8},{20,12},{24,0},{28,4},{1,25},{... | collective-permute-start | bytes 2820104 | tf_op jit(solution)/shard_map/ppermute | solution.py:185
  430.1 50.3 %collective-permute-start.31 = (bf16[136,3456]{1,0:T(8,128)(2,1)}, bf16[136,3456]{1,0:T(8,128)(2,1)}, u32[]{:S(2)}, u32[]{:S(2)}) collective-permute-start(bf16[136,3456]{1,0:T(8,128)(2,1)} %get-tuple-element.84), channel_id=1, source_target_pairs={{0,16},{4,20},{8,24},{12,28},{16,0},{20,4},{24,8},{28,12},{1,17},{... | collective-permute-start | bytes 2820104 | tf_op jit(solution)/shard_map/ppermute | solution.py:185
  (47 other events, 251.4 us)
Sparse Core Ops, SparseCore 0:
  9.6 78.8 all-gather.8
  90.0 48.4 all-gather.4
  197.6 47.2 all-gather.6
  269.5 43.8 reduce-scatter.4
  315.5 44.9 reduce-scatter.6
  407.0 44.9 reduce-scatter.8
  496.6 30.4 reduce-scatter.10
where the time goes:
time: 549 us; the launch traced here: 541 us
  waiting for transfers between devices  158 us (29%)
  local copies, waits for them, and re-layouts  130 us (24%)
  matrix products  89.7 us (16%)
  other arithmetic  53 us (10%)
  starting transfers between devices  52 us (9%)
  Pallas kernels  41 us (7%)
  between operations  16.6 us (3%)
    dot_general x15, matrix products, mm(): return lax.dot_general(a, b, (dims, ((), ())), preferred_element_type=F32)  89.7 us
    reduce_scatter x4, waiting for transfers between devices, scatter_z(): lax.psum_scatter(x, 'seq', scatter_dimension=0, tiled=True).astype(F32)  61.2 us
    ppermute x36, waiting for transfers between devices, swap(): return lax.ppermute(x, 'dp', [(i, i ^ bit) for i in range(n)])  60.2 us
    all_gather x3, waiting for transfers between devices, gather_z(): return lax.all_gather(x, 'seq', axis=0, tiled=True)  36.1 us
    ppermute x36, starting transfers between devices, swap(): return lax.ppermute(x, 'dp', [(i, i ^ bit) for i in range(n)])  33.3 us
    dynamic_update_slice x9, local copies, waits for them, and re-layouts, ring_z(): full = lax.dynamic_update_slice(full, got[None], ((me - d) % size, 0, 0))  29.2 us
    pallas_call x1, Pallas kernels, attend_back(): pl.pallas_call(attend_back_kernel, grid_spec=pltpu.PrefetchScalarGridSpec...  21.4 us
    pallas_call x1, Pallas kernels, attend(): pl.pallas_call(attend_kernel, grid_spec=pltpu.PrefetchScalarGridSpec(num_...  19.6 us
  transfers between devices with their start and end apart: 52, of which 14 were waited for; matrix products, arithmetic and copies ran while one was open for 41% of the time, Pallas kernels for 8%

commit v1 on v0

--- a/solution.py
+++ b/solution.py
@@ -188,34 +188,61 @@
 def ring_z(x):
     size = lax.axis_size("seq")
     me = lax.axis_index("seq")
-    full = jnp.zeros((size,) + x.shape, x.dtype)
-    full = lax.dynamic_update_slice(full, x[None], (me, 0, 0))
+    parts = [x]
     for d in range(1, size):
-        got = lax.ppermute(x, "seq", [(i, (i + d) % size) for i in range(size)])
-        full = lax.dynamic_update_slice(full, got[None], ((me - d) % size, 0, 0))
-    return full
+        parts.append(lax.ppermute(x, "seq", [(i, (i + d) % size) for i in range(size)]))
+    blocks = []
+    for j in range(size):
+        block = parts[0]
+        for d in range(1, size):
+            block = jnp.where((me - j) % size == d, parts[d], block)
+        blocks.append(block)
+    return blocks
+
+
+def place_kernel(meta, *refs):
+    pieces, out, sems = refs[:-2], refs[-2], refs[-1]
+    count = out.shape[0]
+    copies = []
+    at = 0
+    for c in range(len(pieces) // count):
+        rows = pieces[c * count].shape[0]
+        for e in range(count):
+            piece = pieces[c * count + e]
+            spot = out.at[meta[0] ^ e, pl.ds(at, rows), :]
+            copies.append(pltpu.make_async_copy(piece, spot, sems.at[c * count + e]))
+        at += rows
+    for copy in copies:
+        copy.start()
+    for copy in copies:
+        copy.wait()
+
+
+def place(me, pieces, count, rows):
+    return pl.pallas_call(
+        place_kernel,
+        grid_spec=pltpu.PrefetchScalarGridSpec(
+            num_scalar_prefetch=1,
+            grid=(1,),
+            in_specs=[pl.BlockSpec(memory_space=pl.ANY)] * len(pieces),
+            out_specs=pl.BlockSpec(memory_space=pl.ANY),
+            scratch_shapes=[pltpu.SemaphoreType.DMA((len(pieces),))],
+        ),
+        out_shape=jax.ShapeDtypeStruct((count, rows, pieces[0].shape[1]), pieces[0].dtype),
+        name="place",
+    )(me.reshape(1).astype(jnp.int32), *pieces)
 
 
 def gather_dp(chunks):
     n = lax.axis_size("dp")
     if n != 8:
         return lax.all_gather(jnp.concatenate(chunks, axis=0), "dp", axis=0)
-    me = lax.axis_index("dp")
-    group, core = me // 2, me % 2
-    rows = sum(x.shape[0] for x in chunks)
-    full = jnp.zeros((n // 2, 2, rows, chunks[0].shape[1]), chunks[0].dtype)
-    at = 0
+    pieces = []
     for x in chunks:
-        half = jnp.zeros((n // 2,) + x.shape, x.dtype)
-        half = lax.dynamic_update_slice(half, x[None], (group, 0, 0))
-        for d in range(1, n // 2):
-            got = swap(x, 2 * d)
-            half = lax.dynamic_update_slice(half, got[None], (group ^ d, 0, 0))
-        other = swap(half, 1)
-        full = lax.dynamic_update_slice(full, half[:, None], (0, core, at, 0))
-        full = lax.dynamic_update_slice(full, other[:, None], (0, 1 - core, at, 0))
-        at += x.shape[0]
-    return full.reshape(n, rows, chunks[0].shape[1])
+        for d in range(n // 2):
+            got = swap(x, 2 * d) if d else x
+            pieces += [got, swap(got, 1)]
+    return place(lax.axis_index("dp"), pieces, n, sum(x.shape[0] for x in chunks))
 
 
 def scatter_dp(g):
@@ -313,14 +340,13 @@
     cut = -(-share // 16) * 8
     chunks = []
     for lo, hi in ((0, cut), (cut, share)):
-        raw = ring_z(qkv_weight[lo:hi]).transpose(1, 0, 2).reshape(hi - lo, 3 * width)
+        raw = jnp.concatenate(ring_z(qkv_weight[lo:hi]), axis=1)
         wq_s = pad_cols(raw[:, :width], wide)
         wk_s = pad_cols(raw[:, width : 2 * width], wide)
         wv_s = pad_cols(raw[:, 2 * width :], wide)
         chunks.append(jnp.concatenate([wq_s, pair_up(wk_s, wv_s)], axis=1))
     qkv_full = gather_dp(chunks).reshape(width, 3 * wide)
-    out_s, _ = lax.optimization_barrier((out_weight, chunks[1]))
-    out_rows = ring_z(out_s).transpose(1, 0, 2).reshape(share, width)
+    out_rows = jnp.concatenate(ring_z(out_weight), axis=1)
     out_rows, up_s, down_s, qkv_full = lax.optimization_barrier((out_rows, up_weight, down_weight, qkv_full))
     wq = qkv_full[:, :wide]
     wkv = qkv_full[:, wide:]
@@ -371,7 +397,8 @@
     down_grad = mlp_dw[:, ff:].T
     dw = jnp.concatenate([mm(attn_own, dq, TN), mm(attn_full, dkv, TN)], axis=1).astype(BF)
     dq, dkv, dw = lax.optimization_barrier((dq, dkv, dw))
-    dw = scatter_dp(dw.reshape(n, share, 3 * wide))
+    dw = dw.reshape(n, share, 3 * wide)
+    dw_parts = [scatter_dp(dw[:, :cut]), scatter_dp(dw[:, cut:])]
     part_kv = mm(dkv, wkv, NT)
     part_q = mm(dq, wq, NT)
     grad_attn = scatter_z(part_kv.astype(BF))
@@ -398,30 +425,28 @@
     thin_grad = scatter_dp(thin_grad.astype(BF)[:, None, :])
 
     piece = qkv_cols + width // zs
-    dwk, dwv = pair_split(dw[:, wide:])
-    dw_cols = jnp.concatenate([dw[:, :width], dwk[:, :width], dwv[:, :width]], axis=1).astype(BF)
     dwo = dwo.astype(BF)
     extra = -(-thin_len // piece)
     thin_rows = pad_cols(thin_grad.astype(BF), extra * piece).reshape(extra, piece)
-    lines = -(-(share + extra) // 16) * 16
-    thin_rows = jnp.pad(thin_rows, [(0, lines - share - extra), (0, 0)])
-    blocks = []
-    for j in range(zs):
-        blocks.append(
-            jnp.concatenate(
-                [
-                    dw_cols[:, j * qkv_cols : (j + 1) * qkv_cols],
-                    dwo[:, j * (width // zs) : (j + 1) * (width // zs)],
-                ],
-                axis=1,
-            )
-        )
-        blocks.append(thin_rows)
-    last, grad_attn = lax.optimization_barrier((jnp.concatenate(blocks, axis=0), grad_attn))
-    last = scatter_z(last)
+    sums = []
+    for part, lo, hi in ((dw_parts[0], 0, cut), (dw_parts[1], cut, share)):
+        part = part.astype(BF)
+        dwk, dwv = pair_split(part[:, wide:])
+        cols = jnp.concatenate([part[:, :width], dwk[:, :width], dwv[:, :width]], axis=1)
+        blocks = []
+        for j in range(zs):
+            out_part = dwo[lo:hi, j * (width // zs) : (j + 1) * (width // zs)]
+            blocks.append(jnp.concatenate([cols[:, j * qkv_cols : (j + 1) * qkv_cols], out_part], axis=1))
+            if lo:
+                lines = -(-(hi - lo + extra) // 16) * 16
+                blocks.append(jnp.pad(thin_rows, [(0, lines - (hi - lo) - extra), (0, 0)]))
+        block = jnp.concatenate(blocks, axis=0)
+        if lo:
+            block, grad_attn = lax.optimization_barrier((block, grad_attn))
+        sums.append(scatter_z(block))
     input_grad = grad_resid + ln_back(grad_attn + part_q, normed1, inv1, gain1)
-    attn_dw = last[:share]
-    thin_grad = last[share : share + extra].reshape(extra * piece)[:thin_len]
+    attn_dw = jnp.concatenate([sums[0], sums[1][: share - cut]], axis=0)
+    thin_grad = sums[1][share - cut : share - cut + extra].reshape(extra * piece)[:thin_len]
     vec_out = thin_grad[: 8 * share].reshape(8, share)
     return (
         outputs[None],

time: 549 us -> 988 us (1.80)
  Pallas kernels: 41 us -> 495 us
  local copies, waits for them, and re-layouts: 130 us -> 61.9 us
  waiting for transfers between devices: 158 us -> 199 us
  starting transfers between devices: 52 us -> 69.7 us
    pallas_call x0 -> x4, Pallas kernels: none -> 454 us  [place(): pl.pallas_call(place_kernel, grid_spec=pltpu.PrefetchScalarGridSpec(num_s...]
    ppermute x36 -> x55, waiting for transfers between devices: 60.2 us -> 140 us  [swap(): return lax.ppermute(x, 'dp', [(i, i ^ bit) for i in range(n)])]
    dynamic_update_slice x39 -> x0, local copies, waits for them, and re-layouts: 61 us -> none  [the longest x9 29.2 us: ring_z(): full = lax.dynamic_update_slice(full, got[None], ((me - d) % size, 0, 0))]
    all_gather x3, waiting for transfers between devices: 36.1 us -> 0.04 us  [gather_z(): return lax.all_gather(x, 'seq', axis=0, tiled=True)]
    reduce_scatter x4, waiting for transfers between devices: 61.2 us -> 42.7 us  [scatter_z(): lax.psum_scatter(x, 'seq', scatter_dimension=0, tiled=True).astype(F32)]
    ppermute x9, waiting for transfers between devices: 0.02 us -> 15.7 us  [ring_z(): lax.ppermute(x, 'seq', [(i, (i + d) % size) for i in range(size)])]
    broadcast_in_dim x26 -> x0, local copies, waits for them, and re-layouts: 13.2 us -> none  [the longest x9 4.98 us: ring_z(): full = lax.dynamic_update_slice(full, got[None], ((me - d) % size, 0, 0))]
    ppermute x36 -> x55, starting transfers between devices: 33.3 us -> 41.1 us  [swap(): return lax.ppermute(x, 'dp', [(i, i ^ bit) for i in range(n)])]
  transfers between devices with their start and end apart: 52 -> 72, of which waited for: 14 -> 26; matrix products, arithmetic and copies ran while one was open for 41% -> 16% of each run, Pallas kernels for 8% -> 50%
where the time goes in v1:
time: 988 us; the launch traced here: 980 us
  Pallas kernels  495 us (50%)
  waiting for transfers between devices  199 us (20%)
  matrix products  83.9 us (8%)
  starting transfers between devices  69.7 us (7%)
  local copies, waits for them, and re-layouts  61.9 us (6%)
  other arithmetic  53.7 us (5%)
  between operations  16.8 us (2%)
    pallas_call x4, Pallas kernels, place(): pl.pallas_call(place_kernel, grid_spec=pltpu.PrefetchScalarGridSpec(num_s...  454 us
    ppermute x55, waiting for transfers between devices, swap(): return lax.ppermute(x, 'dp', [(i, i ^ bit) for i in range(n)])  140 us
    dot_general x15, matrix products, mm(): return lax.dot_general(a, b, (dims, ((), ())), preferred_element_type=F32)  83.9 us
    reduce_scatter x4, waiting for transfers between devices, scatter_z(): lax.psum_scatter(x, 'seq', scatter_dimension=0, tiled=True).astype(F32)  42.7 us
    ppermute x55, starting transfers between devices, swap(): return lax.ppermute(x, 'dp', [(i, i ^ bit) for i in range(n)])  41.1 us
    ppermute x9, starting transfers between devices, ring_z(): lax.ppermute(x, 'seq', [(i, (i + d) % size) for i in range(size)])  27.9 us
    pallas_call x1, Pallas kernels, attend_back(): pl.pallas_call(attend_back_kernel, grid_spec=pltpu.PrefetchScalarGridSpec...  21.4 us
  transfers between devices with their start and end apart: 72, of which 26 were waited for; matrix products, arithmetic and copies ran while one was open for 16% of the time, Pallas kernels for 50%

profile of v1, /device:TPU:0, one launch (start us, length us, event | category | flops | bytes accessed | tf_op | source)
XLA Modules:
  0.0 979.8 jit_solution(17860189715433617329)
XLA Ops:
  8.9 3.1 collective-permute-start.22
  27.2 8.7 collective-permute-start.10
  42.0 4.9 collective-permute-done.10
  46.9 6.3 collective-permute-start.8
  53.7 4.1 collective-permute-start.7
  63.3 3.1 collective-permute-done.7
  67.2 5.0 collective-permute-done.9
  75.1 8.3 collective-permute-done.26.refs_12_
  86.5 7.5 collective-permute-done.18.refs_6_
  94.0 9.7 collective-permute-done.16.refs_4_
  105.9 2.8 place.4
  112.7 229.1 %place.5 = bf16[8,136,3456]{2,1,0:T(8,128)(2,1)} custom-call(s32[1]{0:T(128)} %bitcast.2.meta, bf16[72,3456]{1,0:T(8,128)(2,1)} %copy-done.19, bf16[72,3456]{1,0:T(8,128)(2,1)} %copy-done.30, bf16[72,3456]{1,0:T(8,128)(2,1)} %copy-done.29, bf16[72,3456]{1,0:T(8,128)(2,1)} %collective-permute-done.15.refs_3_, bf16[72,3456]{1,0:T(8,128)(2,1)} %copy-done.28, ...), custom_call_target="tpu_custom_call" | custom-call | tf_op jit(solution)/shard_map/place/pallas_call | solution.py:222
  346.9 6.2 collective-permute-done.35.refs_6_
  353.1 5.8 collective-permute-done.33.refs_4_
  359.4 3.8 fusion.20.q_ref
  364.9 77.1 %place.6 = bf16[8,136,1088]{2,1,0:T(8,128)(2,1)} custom-call(s32[1]{0:T(128)} %bitcast.2.meta, bf16[136,1088]{1,0:T(8,128)(2,1)} %copy-done.23, bf16[136,1088]{1,0:T(8,128)(2,1)} %copy-done.40, bf16[136,1088]{1,0:T(8,128)(2,1)} %copy-done.39, bf16[136,1088]{1,0:T(8,128)(2,1)} %copy-done.43, bf16[136,1088]{1,0:T(8,128)(2,1)} %copy-done.38, ...), custom_call_target="tpu_custom_call" | custom-call | tf_op jit(solution)/shard_map/place/pallas_call | solution.py:222
  445.0 10.9 %add_convert_fusion.kv_ref = bf16[1024,2304]{1,0:T(8,128)(2,1)} fusion(f32[2304]{0:T(1024)S(1)} %add.385, bf16[1088,3456]{1,0:T(8,128)(2,1)} %bitcast.226, f32[1088]{0:T(1024)S(1)} %add.372, f32[1088]{0:T(1024)S(1)} %mul.192, f32[1024]{0:T(1024)S(1)} %add_rsqrt_fusion, f32[1024]{0:T(1024)S(1)} %broadcast_multiply_fusion, bf16[1,1024,1088]{1,2,0:T(8,128)(2,1)S(1)} %copy-done.7), kind=kOutput, calls=%fused_computation.1 | convolution fusion | flops 5145231360 | bytes 11986432 | tf_op jit(solution)/shard_map/dot_general | solution.py:19
  455.9 19.6 %attend.1 = (bf16[256,1152]{1,0:T(8,128)(2,1)}, f32[9,2,256]{2,1,0:T(2,128)}) custom-call(s32[2]{0:T(128)} %pad_add_fusion.meta, bf16[256,1152]{1,0:T(8,128)(2,1)} %fusion.20.q_ref, bf16[1024,2304]{1,0:T(8,128)(2,1)} %add_convert_fusion.kv_ref), custom_call_target="tpu_custom_call" | custom-call | flops 2415919104 | bytes 7077888 | tf_op jit(solution)/shard_map/attend/pallas_call | solution.py:90
  475.5 3.1 fusion.129
  483.9 13.7 %collective-permute-done.42.refs_6_ = bf16[136,2176]{1,0:T(8,128)(2,1)S(1)} collective-permute-done((bf16[136,2176]{1,0:T(8,128)(2,1)S(1)}, bf16[136,2176]{1,0:T(8,128)(2,1)S(1)}, u32[]{:S(2)}, u32[]{:S(2)}) %collective-permute-start.42) | collective-permute-done | bytes 591904 | tf_op jit(solution)/shard_map/ppermute | solution.py:185
  497.6 11.8 %collective-permute-done.40.refs_4_ = bf16[136,2176]{1,0:T(8,128)(2,1)S(1)} collective-permute-done((bf16[136,2176]{1,0:T(8,128)(2,1)S(1)}, bf16[136,2176]{1,0:T(8,128)(2,1)S(1)}, u32[]{:S(2)}, u32[]{:S(2)}) %collective-permute-start.40) | collective-permute-done | bytes 591904 | tf_op jit(solution)/shard_map/ppermute | solution.py:185
  512.4 144.6 %place.7 = bf16[8,136,2176]{2,1,0:T(8,128)(2,1)} custom-call(s32[1]{0:T(128)} %bitcast.2.meta, bf16[136,2176]{1,0:T(8,128)(2,1)} %copy-done.16, bf16[136,2176]{1,0:T(8,128)(2,1)} %collective-permute-done.37.refs_1_, bf16[136,2176]{1,0:T(8,128)(2,1)} %collective-permute-done.38.refs_2_, bf16[136,2176]{1,0:T(8,128)(2,1)} %collective-permute-done.39.refs_3_, ...), custom_call_target="tpu_custom_call" | custom-call | tf_op jit(solution)/shard_map/place/pallas_call | solution.py:222
  657.1 5.7 convolution_add_fusion
  662.8 8.4 fusion.130
  672.6 4.3 convolution_convert_fusion.6
  677.0 5.5 convolution_convert_fusion.4
  682.6 6.4 convolution_convert_fusion.3
  691.4 7.8 convolution_convert_fusion.5
  699.4 3.5 fusion.4
  709.0 11.9 %collective-permute-done.61 = bf16[136,2176]{1,0:T(8,128)(2,1)} collective-permute-done((bf16[136,2176]{1,0:T(8,128)(2,1)S(1)}, bf16[136,2176]{1,0:T(8,128)(2,1)}, u32[]{:S(2)}, u32[]{:S(2)}) %collective-permute-start.61) | collective-permute-done | bytes 591904 | tf_op jit(solution)/shard_map/ppermute | solution.py:185
  720.8 12.9 %collective-permute-done.63 = bf16[136,2176]{1,0:T(8,128)(2,1)} collective-permute-done((bf16[136,2176]{1,0:T(8,128)(2,1)S(1)}, bf16[136,2176]{1,0:T(8,128)(2,1)}, u32[]{:S(2)}, u32[]{:S(2)}) %collective-permute-start.63) | collective-permute-done | bytes 591904 | tf_op jit(solution)/shard_map/ppermute | solution.py:185
  745.8 3.5 convolution_convert_fusion.1
  749.3 21.4 %attend_back.1 = (bf16[256,1152]{1,0:T(8,128)(2,1)}, bf16[1024,2304]{1,0:T(8,128)(2,1)}) custom-call(s32[2]{0:T(128)} %pad_add_fusion.meta, bf16[256,1152]{1,0:T(8,128)(2,1)} %fusion.20.q_ref, bf16[1024,2304]{1,0:T(8,128)(2,1)} %add_convert_fusion.kv_ref, f32[9,2,256]{2,1,0:T(2,128)} %get-tuple-element.40.lse_ref, bf16[256,1152]{1,0:T(8,128)(2,1)} %pad.51.g_ref), custom_call_target="tpu_custom_call" | custom-call | flops 6039797760 | bytes 14155776 | tf_op jit(solution)/shard_map/attend_back/pallas_call | solution.py:155
  777.1 7.8 convolution_convert_fusion
  784.9 6.0 pad_maximum_fusion
  790.9 3.0 reduce.1
  793.9 3.6 fusion.124
  803.4 10.3 %fusion.122 = (f32[1088]{0:T(1024)S(1)}, f32[1088]{0:T(1024)S(1)}, bf16[1024,1088]{0,1:T(8,128)(2,1)}) fusion(f32[1024]{0:T(1024)S(1)} %copy-done.71, f32[1024]{0:T(1024)S(1)} %copy-done.61, bf16[1,1024,1088]{1,2,0:T(8,128)(2,1)S(1)} %copy-done.9, bf16[1024,2304]{1,0:T(8,128)(2,1)} %get-tuple-element.51, bf16[1088,3456]{1,0:T(8,128)(2,1)} %bitcast.228), kind=kOutput, calls=%fused_computation.262 | convolution fusion | flops 5141624832 | bytes 14205440 | tf_op jit(solution)/shard_map/dot_general | solution.py:19
  813.8 4.1 slice.377
  821.4 3.1 dynamic-slice_bitcast_fusion.1
  833.9 3.4 collective-permute-done.49
  838.9 5.3 collective-permute-done.51
  846.4 8.3 collective-permute-done.57
  854.7 10.0 %collective-permute-done.59 = bf16[72,3456]{1,0:T(8,128)(2,1)S(1)} collective-permute-done((bf16[72,3456]{1,0:T(8,128)(2,1)S(1)}, bf16[72,3456]{1,0:T(8,128)(2,1)S(1)}, u32[]{:S(2)}, u32[]{:S(2)}) %collective-permute-start.59) | collective-permute-done | bytes 497696 | tf_op jit(solution)/shard_map/ppermute | solution.py:185
  890.5 9.5 collective-permute-done.45
  900.0 9.0 collective-permute-done.47
  920.3 22.1 %reduce-scatter.12.cloned.1.call-done = bf16[256,1088]{0,1:T(8,128)(2,1)} async-done(((bf16[1024,1088]{0,1:T(8,128)(2,1)}), bf16[256,1088]{0,1:T(8,128)(2,1)}) %reduce-scatter.12.cloned.1.call-update) | async-done | bytes 557072 | tf_op jit(solution)/shard_map/reduce_scatter | solution.py:271
  946.4 20.6 %reduce-scatter.14.cloned.1.call-done = bf16[80,1088]{1,0:T(8,128)(2,1)} async-done(((bf16[320,1088]{1,0:T(8,128)(2,1)}), bf16[80,1088]{1,0:T(8,128)(2,1)}) %reduce-scatter.14.cloned.1.call-update) | async-done | bytes 174096 | tf_op jit(solution)/shard_map/reduce_scatter | solution.py:271
  (449 shorter events, 156.7 us)
Async XLA Ops:
  7.2 434.8 %all-gather.9.cloned.1.call-start = ((), (), s32[]{:S(2)}) async-start(), calls=%async_computation.11 | async-start | bytes 2785280 | tf_op jit(solution)/shard_map/all_gather | solution.py:267
  7.9 467.6 %all-gather.5.cloned.1.call-start = ((), (), s32[]{:S(2)}) async-start(), calls=%async_computation.5 | async-start | bytes 2785280 | tf_op jit(solution)/shard_map/all_gather | solution.py:267
  8.9 17.3 %collective-permute-start.22 = (bf16[64,816]{1,0:T(8,128)(2,1)S(1)}, bf16[64,816]{1,0:T(8,128)(2,1)S(1)}, u32[]{:S(2)}, u32[]{:S(2)}) collective-permute-start(bf16[64,816]{1,0:T(8,128)(2,1)S(1)} %slice.293), channel_id=1, source_target_pairs={{0,1},{1,2},{2,3},{3,0},{4,5},{5,6},{6,7},{7,4},{8,9},{9,10},{10,1... | collective-permute-start | bytes 313352 | tf_op jit(solution)/shard_map/ppermute | solution.py:193
  12.0 14.9 %collective-permute-start.21 = (bf16[64,816]{1,0:T(8,128)(2,1)S(1)}, bf16[64,816]{1,0:T(8,128)(2,1)S(1)}, u32[]{:S(2)}, u32[]{:S(2)}) collective-permute-start(bf16[64,816]{1,0:T(8,128)(2,1)S(1)} %slice.293), channel_id=1, source_target_pairs={{0,2},{1,3},{2,0},{3,1},{4,6},{5,7},{6,4},{7,5},{8,10},{9,11},{10,... | collective-permute-start | bytes 313352 | tf_op jit(solution)/shard_map/ppermute | solution.py:193
  22.1 31.6 %collective-permute-start.5 = (bf16[1,1632]{1,0:T(2,128)(2,1)S(1)}, bf16[1,1632]{1,0:T(2,128)(2,1)S(1)}, u32[]{:S(2)}, u32[]{:S(2)}) collective-permute-start(bf16[1,1632]{1,0:T(2,128)(2,1)S(1)} %pad_maximum_fusion.11.refs_0_), channel_id=1, source_target_pairs={{0,24},{4,28},{8,16},{12,20},{16,8},{20,12},{24,0},{28,4},{1,25},{... | collective-permute-start | bytes 9800 | tf_op jit(solution)/shard_map/ppermute | solution.py:185
  24.6 33.2 %collective-permute-start.3 = (bf16[1,1632]{1,0:T(2,128)(2,1)S(1)}, bf16[1,1632]{1,0:T(2,128)(2,1)S(1)}, u32[]{:S(2)}, u32[]{:S(2)}) collective-permute-start(bf16[1,1632]{1,0:T(2,128)(2,1)S(1)} %pad_maximum_fusion.11.refs_0_), channel_id=1, source_target_pairs={{0,16},{4,20},{8,24},{12,28},{16,0},{20,4},{24,8},{28,12},{1,17},{... | collective-permute-start | bytes 9800 | tf_op jit(solution)/shard_map/ppermute | solution.py:185
  25.1 631.9 %all-gather.7.cloned.1.call-start = ((), (), s32[]{:S(2)}) async-start(), calls=%async_computation.6 | async-start | bytes 2785280 | tf_op jit(solution)/shard_map/all_gather | solution.py:267
  26.9 15.1 %collective-permute-start.11 = (bf16[72,816]{1,0:T(8,128)(2,1)S(1)}, bf16[72,816]{1,0:T(8,128)(2,1)S(1)}, u32[]{:S(2)}, u32[]{:S(2)}) collective-permute-start(bf16[72,816]{1,0:T(8,128)(2,1)S(1)} %slice.289), channel_id=1, source_target_pairs={{0,2},{1,3},{2,0},{3,1},{4,6},{5,7},{6,4},{7,5},{8,10},{9,11},{10,... | collective-permute-start | bytes 352520 | tf_op jit(solution)/shard_map/ppermute | solution.py:193
  27.2 19.7 %collective-permute-start.10 = (bf16[72,816]{1,0:T(8,128)(2,1)S(1)}, bf16[72,816]{1,0:T(8,128)(2,1)S(1)}, u32[]{:S(2)}, u32[]{:S(2)}) collective-permute-start(bf16[72,816]{1,0:T(8,128)(2,1)S(1)} %slice.289), channel_id=1, source_target_pairs={{0,3},{1,0},{2,1},{3,2},{4,7},{5,4},{6,5},{7,6},{8,11},{9,8},{10,9... | collective-permute-start | bytes 352520 | tf_op jit(solution)/shard_map/ppermute | solution.py:193
  38.0 20.0 %collective-permute-start.1 = (bf16[1,1632]{1,0:T(2,128)(2,1)S(1)}, bf16[1,1632]{1,0:T(2,128)(2,1)S(1)}, u32[]{:S(2)}, u32[]{:S(2)}) collective-permute-start(bf16[1,1632]{1,0:T(2,128)(2,1)S(1)} %pad_maximum_fusion.11.refs_0_), channel_id=1, source_target_pairs={{0,8},{4,12},{8,0},{12,4},{16,24},{20,28},{24,16},{28,20},{1,9},{5... | collective-permute-start | bytes 9800 | tf_op jit(solution)/shard_map/ppermute | solution.py:185
  42.0 16.3 %collective-permute-start = (bf16[1,1632]{1,0:T(2,128)(2,1)S(1)}, bf16[1,1632]{1,0:T(2,128)(2,1)S(1)}, u32[]{:S(2)}, u32[]{:S(2)}) collective-permute-start(bf16[1,1632]{1,0:T(2,128)(2,1)S(1)} %pad_maximum_fusion.11.refs_0_), channel_id=1, source_target_pairs={{0,4},{4,0},{8,12},{12,8},{16,20},{20,16},{24,28},{28,24},{1,5},{5... | collective-permute-start | bytes 9800 | tf_op jit(solution)/shard_map/ppermute | solution.py:185
  46.9 15.6 %collective-permute-start.8 = (bf16[136,272]{1,0:T(8,128)(2,1)S(1)}, bf16[136,272]{1,0:T(8,128)(2,1)S(1)}, u32[]{:S(2)}, u32[]{:S(2)}) collective-permute-start(bf16[136,272]{1,0:T(8,128)(2,1)S(1)} %copy-done.46), channel_id=1, source_target_pairs={{0,2},{1,3},{2,0},{3,1},{4,6},{5,7},{6,4},{7,5},{8,10},{9,11},{10,... | collective-permute-start | bytes 221960 | tf_op jit(solution)/shard_map/ppermute | solution.py:193
  59.1 13.0 %collective-permute-start.9 = (bf16[136,272]{1,0:T(8,128)(2,1)S(1)}, bf16[136,272]{1,0:T(8,128)(2,1)S(1)}, u32[]{:S(2)}, u32[]{:S(2)}) collective-permute-start(bf16[136,272]{1,0:T(8,128)(2,1)S(1)} %copy-done.46), channel_id=1, source_target_pairs={{0,1},{1,2},{2,3},{3,0},{4,5},{5,6},{6,7},{7,4},{8,9},{9,10},{10,1... | collective-permute-start | bytes 221960 | tf_op jit(solution)/shard_map/ppermute | solution.py:193
  59.8 14.5 %collective-permute-start.28 = (bf16[64,3456]{1,0:T(8,128)(2,1)S(1)}, bf16[64,3456]{1,0:T(8,128)(2,1)S(1)}, u32[]{:S(2)}, u32[]{:S(2)}) collective-permute-start(bf16[64,3456]{1,0:T(8,128)(2,1)S(1)} %pad_maximum_fusion.7.refs_8_), channel_id=1, source_target_pairs={{0,24},{4,28},{8,16},{12,20},{16,8},{20,12},{24,0},{28,4},{1,25},{... | collective-permute-start | bytes 1327112 | tf_op jit(solution)/shard_map/ppermute | solution.py:185
  62.1 21.3 %collective-permute-start.26 = (bf16[64,3456]{1,0:T(8,128)(2,1)S(1)}, bf16[64,3456]{1,0:T(8,128)(2,1)S(1)}, u32[]{:S(2)}, u32[]{:S(2)}) collective-permute-start(bf16[64,3456]{1,0:T(8,128)(2,1)S(1)} %pad_maximum_fusion.7.refs_8_), channel_id=1, source_target_pairs={{0,16},{4,20},{8,24},{12,28},{16,0},{20,4},{24,8},{28,12},{1,17},{... | collective-permute-start | bytes 1327112 | tf_op jit(solution)/shard_map/ppermute | solution.py:185
  62.5 22.1 %collective-permute-start.24 = (bf16[64,3456]{1,0:T(8,128)(2,1)S(1)}, bf16[64,3456]{1,0:T(8,128)(2,1)S(1)}, u32[]{:S(2)}, u32[]{:S(2)}) collective-permute-start(bf16[64,3456]{1,0:T(8,128)(2,1)S(1)} %pad_maximum_fusion.7.refs_8_), channel_id=1, source_target_pairs={{0,8},{4,12},{8,0},{12,4},{16,24},{20,28},{24,16},{28,20},{1,9},{5... | collective-permute-start | bytes 1327112 | tf_op jit(solution)/shard_map/ppermute | solution.py:185
  66.5 19.7 %collective-permute-start.23 = (bf16[64,3456]{1,0:T(8,128)(2,1)S(1)}, bf16[64,3456]{1,0:T(8,128)(2,1)}, u32[]{:S(2)}, u32[]{:S(2)}) collective-permute-start(bf16[64,3456]{1,0:T(8,128)(2,1)S(1)} %pad_maximum_fusion.7.refs_8_), channel_id=1, source_target_pairs={{0,4},{4,0},{8,12},{12,8},{16,20},{20,16},{24,28},{28,24},{1,5},{5... | collective-permute-start | bytes 1327112 | tf_op jit(solution)/shard_map/ppermute | solution.py:185
  72.1 21.9 %collective-permute-start.18 = (bf16[72,3456]{1,0:T(8,128)(2,1)S(1)}, bf16[72,3456]{1,0:T(8,128)(2,1)S(1)}, u32[]{:S(2)}, u32[]{:S(2)}) collective-permute-start(bf16[72,3456]{1,0:T(8,128)(2,1)S(1)} %pad_maximum_fusion.6.refs_0_), channel_id=1, source_target_pairs={{0,24},{4,28},{8,16},{12,20},{16,8},{20,12},{24,0},{28,4},{1,25},{... | collective-permute-start | bytes 1493000 | tf_op jit(solution)/shard_map/ppermute | solution.py:185
  74.4 29.3 %collective-permute-start.16 = (bf16[72,3456]{1,0:T(8,128)(2,1)S(1)}, bf16[72,3456]{1,0:T(8,128)(2,1)S(1)}, u32[]{:S(2)}, u32[]{:S(2)}) collective-permute-start(bf16[72,3456]{1,0:T(8,128)(2,1)S(1)} %pad_maximum_fusion.6.refs_0_), channel_id=1, source_target_pairs={{0,16},{4,20},{8,24},{12,28},{16,0},{20,4},{24,8},{28,12},{1,17},{... | collective-permute-start | bytes 1493000 | tf_op jit(solution)/shard_map/ppermute | solution.py:185
  83.4 20.5 %collective-permute-start.14 = (bf16[72,3456]{1,0:T(8,128)(2,1)S(1)}, bf16[72,3456]{1,0:T(8,128)(2,1)S(1)}, u32[]{:S(2)}, u32[]{:S(2)}) collective-permute-start(bf16[72,3456]{1,0:T(8,128)(2,1)S(1)} %pad_maximum_fusion.6.refs_0_), channel_id=1, source_target_pairs={{0,8},{4,12},{8,0},{12,4},{16,24},{20,28},{24,16},{28,20},{1,9},{5... | collective-permute-start | bytes 1493000 | tf_op jit(solution)/shard_map/ppermute | solution.py:185
  84.6 20.2 %collective-permute-start.13 = (bf16[72,3456]{1,0:T(8,128)(2,1)S(1)}, bf16[72,3456]{1,0:T(8,128)(2,1)S(1)}, u32[]{:S(2)}, u32[]{:S(2)}) collective-permute-start(bf16[72,3456]{1,0:T(8,128)(2,1)S(1)} %pad_maximum_fusion.6.refs_0_), channel_id=1, source_target_pairs={{0,4},{4,0},{8,12},{12,8},{16,20},{20,16},{24,28},{28,24},{1,5},{5... | collective-permute-start | bytes 1493000 | tf_op jit(solution)/shard_map/ppermute | solution.py:185
  86.2 18.7 %collective-permute-start.29 = (bf16[64,3456]{1,0:T(8,128)(2,1)}, bf16[64,3456]{1,0:T(8,128)(2,1)S(1)}, u32[]{:S(2)}, u32[]{:S(2)}) collective-permute-start(bf16[64,3456]{1,0:T(8,128)(2,1)} %copy-done.31), channel_id=1, source_target_pairs={{0,4},{4,0},{8,12},{12,8},{16,20},{20,16},{24,28},{28,24},{1,5},{5... | collective-permute-start | bytes 1327112 | tf_op jit(solution)/shard_map/ppermute | solution.py:185
  94.0 18.6 %collective-permute-start.19 = (bf16[72,3456]{1,0:T(8,128)(2,1)S(1)}, bf16[72,3456]{1,0:T(8,128)(2,1)}, u32[]{:S(2)}, u32[]{:S(2)}) collective-permute-start(bf16[72,3456]{1,0:T(8,128)(2,1)S(1)} %collective-permute-done.18.refs_6_), channel_id=1, source_target_pairs={{0,4},{4,0},{8,12},{12,8},{16,20},{20,16},{24,28},{28,24},{1,5},{5... | collective-permute-start | bytes 1493000 | tf_op jit(solution)/shard_map/ppermute | solution.py:185
  343.6 15.3 %collective-permute-start.33 = (bf16[136,1088]{1,0:T(8,128)(2,1)S(1)}, bf16[136,1088]{1,0:T(8,128)(2,1)S(1)}, u32[]{:S(2)}, u32[]{:S(2)}) collective-permute-start(bf16[136,1088]{1,0:T(8,128)(2,1)S(1)} %concatenate.113.refs_0_), channel_id=1, source_target_pairs={{0,16},{4,20},{8,24},{12,28},{16,0},{20,4},{24,8},{28,12},{1,17},{... | collective-permute-start | bytes 887816 | tf_op jit(solution)/shard_map/ppermute | solution.py:185
  344.5 14.4 %collective-permute-start.31 = (bf16[136,1088]{1,0:T(8,128)(2,1)S(1)}, bf16[136,1088]{1,0:T(8,128)(2,1)S(1)}, u32[]{:S(2)}, u32[]{:S(2)}) collective-permute-start(bf16[136,1088]{1,0:T(8,128)(2,1)S(1)} %concatenate.113.refs_0_), channel_id=1, source_target_pairs={{0,8},{4,12},{8,0},{12,4},{16,24},{20,28},{24,16},{28,20},{1,9},{5... | collective-permute-start | bytes 887816 | tf_op jit(solution)/shard_map/ppermute | solution.py:185
  346.8 16.4 %collective-permute-start.30 = (bf16[136,1088]{1,0:T(8,128)(2,1)S(1)}, bf16[136,1088]{1,0:T(8,128)(2,1)S(1)}, u32[]{:S(2)}, u32[]{:S(2)}) collective-permute-start(bf16[136,1088]{1,0:T(8,128)(2,1)S(1)} %concatenate.113.refs_0_), channel_id=1, source_target_pairs={{0,4},{4,0},{8,12},{12,8},{16,20},{20,16},{24,28},{28,24},{1,5},{5... | collective-permute-start | bytes 887816 | tf_op jit(solution)/shard_map/ppermute | solution.py:185
  480.1 258.1 %reduce-scatter.8.cloned.1.call-start = ((), (), s32[]{:S(2)}) async-start(), calls=%async_computation.7 | async-start | bytes 2785280 | tf_op jit(solution)/shard_map/reduce_scatter | solution.py:271
  480.3 17.2 %collective-permute-start.42 = (bf16[136,2176]{1,0:T(8,128)(2,1)S(1)}, bf16[136,2176]{1,0:T(8,128)(2,1)S(1)}, u32[]{:S(2)}, u32[]{:S(2)}) collective-permute-start(bf16[136,2176]{1,0:T(8,128)(2,1)S(1)} %pad_maximum_fusion.3.refs_0_), channel_id=1, source_target_pairs={{0,24},{4,28},{8,16},{12,20},{16,8},{20,12},{24,0},{28,4},{1,25},{... | collective-permute-start | bytes 1775624 | tf_op jit(solution)/shard_map/ppermute | solution.py:185
  482.1 27.2 %collective-permute-start.40 = (bf16[136,2176]{1,0:T(8,128)(2,1)S(1)}, bf16[136,2176]{1,0:T(8,128)(2,1)S(1)}, u32[]{:S(2)}, u32[]{:S(2)}) collective-permute-start(bf16[136,2176]{1,0:T(8,128)(2,1)S(1)} %pad_maximum_fusion.3.refs_0_), channel_id=1, source_target_pairs={{0,16},{4,20},{8,24},{12,28},{16,0},{20,4},{24,8},{28,12},{1,17},{... | collective-permute-start | bytes 1775624 | tf_op jit(solution)/shard_map/ppermute | solution.py:185
  483.1 26.4 %collective-permute-start.38 = (bf16[136,2176]{1,0:T(8,128)(2,1)S(1)}, bf16[136,2176]{1,0:T(8,128)(2,1)}, u32[]{:S(2)}, u32[]{:S(2)}) collective-permute-start(bf16[136,2176]{1,0:T(8,128)(2,1)S(1)} %pad_maximum_fusion.3.refs_0_), channel_id=1, source_target_pairs={{0,8},{4,12},{8,0},{12,4},{16,24},{20,28},{24,16},{28,20},{1,9},{5... | collective-permute-start | bytes 1775624 | tf_op jit(solution)/shard_map/ppermute | solution.py:185
  483.9 26.3 %collective-permute-start.37 = (bf16[136,2176]{1,0:T(8,128)(2,1)S(1)}, bf16[136,2176]{1,0:T(8,128)(2,1)}, u32[]{:S(2)}, u32[]{:S(2)}) collective-permute-start(bf16[136,2176]{1,0:T(8,128)(2,1)S(1)} %pad_maximum_fusion.3.refs_0_), channel_id=1, source_target_pairs={{0,4},{4,0},{8,12},{12,8},{16,20},{20,16},{24,28},{28,24},{1,5},{5... | collective-permute-start | bytes 1775624 | tf_op jit(solution)/shard_map/ppermute | solution.py:185
  676.9 93.8 %reduce-scatter.10.cloned.1.call-start = ((), (), s32[]{:S(2)}) async-start(), calls=%async_computation.8 | async-start | bytes 2785280 | tf_op jit(solution)/shard_map/reduce_scatter | solution.py:271
  699.2 220.2 %reduce-scatter.16.cloned.1.call-start = ((), (), s32[]{:S(2)}) async-start(), calls=%async_computation.12 | async-start | bytes 829440
  704.4 16.4 %collective-permute-start.61 = (bf16[136,2176]{1,0:T(8,128)(2,1)S(1)}, bf16[136,2176]{1,0:T(8,128)(2,1)}, u32[]{:S(2)}, u32[]{:S(2)}) collective-permute-start(bf16[136,2176]{1,0:T(8,128)(2,1)S(1)} %get-tuple-element.80), channel_id=1, source_target_pairs={{0,8},{4,12},{8,0},{12,4},{16,24},{20,28},{24,16},{28,20},{1,9},{5... | collective-permute-start | bytes 1775624 | tf_op jit(solution)/shard_map/ppermute | solution.py:185
  705.8 27.9 %collective-permute-start.63 = (bf16[136,2176]{1,0:T(8,128)(2,1)S(1)}, bf16[136,2176]{1,0:T(8,128)(2,1)}, u32[]{:S(2)}, u32[]{:S(2)}) collective-permute-start(bf16[136,2176]{1,0:T(8,128)(2,1)S(1)} %get-tuple-element.81), channel_id=1, source_target_pairs={{0,24},{4,28},{8,16},{12,20},{16,8},{20,12},{24,0},{28,4},{1,25},{... | collective-permute-start | bytes 1775624 | tf_op jit(solution)/shard_map/ppermute | solution.py:185
  707.2 27.9 %collective-permute-start.62 = (bf16[136,2176]{1,0:T(8,128)(2,1)S(1)}, bf16[136,2176]{1,0:T(8,128)(2,1)}, u32[]{:S(2)}, u32[]{:S(2)}) collective-permute-start(bf16[136,2176]{1,0:T(8,128)(2,1)S(1)} %get-tuple-element.82), channel_id=1, source_target_pairs={{0,16},{4,20},{8,24},{12,28},{16,0},{20,4},{24,8},{28,12},{1,17},{... | collective-permute-start | bytes 1775624 | tf_op jit(solution)/shard_map/ppermute | solution.py:185
  775.5 49.5 %collective-permute-start.48 = (bf16[4,136,1088]{2,1,0:T(8,128)(2,1)}, bf16[4,136,1088]{2,1,0:T(8,128)(2,1)}, u32[]{:S(2)}, u32[]{:S(2)}) collective-permute-start(bf16[4,136,1088]{2,1,0:T(8,128)(2,1)} %dynamic-slice_bitcast_fusion.2), channel_id=1, source_target_pairs={{0,4},{4,0},{8,12},{12,8},{16,20},{20,16},{24,28},{28,24},{1,5},{5... | collective-permute-start | bytes 3551240 | tf_op jit(solution)/shard_map/ppermute | solution.py:185
  824.5 57.5 %collective-permute-start.44 = (bf16[4,64,3456]{2,1,0:T(8,128)(2,1)}, bf16[4,64,3456]{2,1,0:T(8,128)(2,1)}, u32[]{:S(2)}, u32[]{:S(2)}) collective-permute-start(bf16[4,64,3456]{2,1,0:T(8,128)(2,1)} %dynamic-slice_bitcast_fusion.1), channel_id=1, source_target_pairs={{0,4},{4,0},{8,12},{12,8},{16,20},{20,16},{24,28},{28,24},{1,5},{5... | collective-permute-start | bytes 5308424 | tf_op jit(solution)/shard_map/ppermute | solution.py:185
  828.1 16.1 %collective-permute-start.51 = (bf16[136,1088]{1,0:T(8,128)(2,1)S(1)}, bf16[136,1088]{1,0:T(8,128)(2,1)S(1)}, u32[]{:S(2)}, u32[]{:S(2)}) collective-permute-start(bf16[136,1088]{1,0:T(8,128)(2,1)S(1)} %get-tuple-element.90), channel_id=1, source_target_pairs={{0,24},{4,28},{8,16},{12,20},{16,8},{20,12},{24,0},{28,4},{1,25},{... | collective-permute-start | bytes 887816 | tf_op jit(solution)/shard_map/ppermute | solution.py:185
  829.2 16.3 %collective-permute-start.50 = (bf16[136,1088]{1,0:T(8,128)(2,1)S(1)}, bf16[136,1088]{1,0:T(8,128)(2,1)S(1)}, u32[]{:S(2)}, u32[]{:S(2)}) collective-permute-start(bf16[136,1088]{1,0:T(8,128)(2,1)S(1)} %get-tuple-element.91), channel_id=1, source_target_pairs={{0,16},{4,20},{8,24},{12,28},{16,0},{20,4},{24,8},{28,12},{1,17},{... | collective-permute-start | bytes 887816 | tf_op jit(solution)/shard_map/ppermute | solution.py:185
  832.6 22.0 %collective-permute-start.57 = (bf16[72,3456]{1,0:T(8,128)(2,1)S(1)}, bf16[72,3456]{1,0:T(8,128)(2,1)S(1)}, u32[]{:S(2)}, u32[]{:S(2)}) collective-permute-start(bf16[72,3456]{1,0:T(8,128)(2,1)S(1)} %get-tuple-element.83), channel_id=1, source_target_pairs={{0,8},{4,12},{8,0},{12,4},{16,24},{20,28},{24,16},{28,20},{1,9},{5... | collective-permute-start | bytes 1493000 | tf_op jit(solution)/shard_map/ppermute | solution.py:185
  837.2 27.4 %collective-permute-start.59 = (bf16[72,3456]{1,0:T(8,128)(2,1)S(1)}, bf16[72,3456]{1,0:T(8,128)(2,1)S(1)}, u32[]{:S(2)}, u32[]{:S(2)}) collective-permute-start(bf16[72,3456]{1,0:T(8,128)(2,1)S(1)} %get-tuple-element.84), channel_id=1, source_target_pairs={{0,24},{4,28},{8,16},{12,20},{16,8},{20,12},{24,0},{28,4},{1,25},{... | collective-permute-start | bytes 1493000 | tf_op jit(solution)/shard_map/ppermute | solution.py:185
  844.2 22.1 %collective-permute-start.58 = (bf16[72,3456]{1,0:T(8,128)(2,1)S(1)}, bf16[72,3456]{1,0:T(8,128)(2,1)S(1)}, u32[]{:S(2)}, u32[]{:S(2)}) collective-permute-start(bf16[72,3456]{1,0:T(8,128)(2,1)S(1)} %get-tuple-element.85), channel_id=1, source_target_pairs={{0,16},{4,20},{8,24},{12,28},{16,0},{20,4},{24,8},{28,12},{1,17},{... | collective-permute-start | bytes 1493000 | tf_op jit(solution)/shard_map/ppermute | solution.py:185
  872.6 69.8 %reduce-scatter.12.cloned.1.call-start = ((), (), s32[]{:S(2)}) async-start(), calls=%async_computation.9 | async-start | bytes 2785280 | tf_op jit(solution)/shard_map/reduce_scatter | solution.py:271
  877.9 89.1 %reduce-scatter.14.cloned.1.call-start = ((), (), s32[]{:S(2)}) async-start(), calls=%async_computation.10 | async-start | bytes 921600 | tf_op jit(solution)/shard_map/reduce_scatter | solution.py:271
  886.7 13.2 %collective-permute-start.45 = (bf16[64,3456]{1,0:T(8,128)(2,1)}, bf16[64,3456]{1,0:T(8,128)(2,1)S(1)}, u32[]{:S(2)}, u32[]{:S(2)}) collective-permute-start(bf16[64,3456]{1,0:T(8,128)(2,1)} %get-tuple-element.86), channel_id=1, source_target_pairs={{0,8},{4,12},{8,0},{12,4},{16,24},{20,28},{24,16},{28,20},{1,9},{5... | collective-permute-start | bytes 1327112 | tf_op jit(solution)/shard_map/ppermute | solution.py:185
  888.2 20.8 %collective-permute-start.47 = (bf16[64,3456]{1,0:T(8,128)(2,1)}, bf16[64,3456]{1,0:T(8,128)(2,1)S(1)}, u32[]{:S(2)}, u32[]{:S(2)}) collective-permute-start(bf16[64,3456]{1,0:T(8,128)(2,1)} %get-tuple-element.87), channel_id=1, source_target_pairs={{0,24},{4,28},{8,16},{12,20},{16,8},{20,12},{24,0},{28,4},{1,25},{... | collective-permute-start | bytes 1327112 | tf_op jit(solution)/shard_map/ppermute | solution.py:185
  889.5 21.0 %collective-permute-start.46 = (bf16[64,3456]{1,0:T(8,128)(2,1)}, bf16[64,3456]{1,0:T(8,128)(2,1)}, u32[]{:S(2)}, u32[]{:S(2)}) collective-permute-start(bf16[64,3456]{1,0:T(8,128)(2,1)} %get-tuple-element.88), channel_id=1, source_target_pairs={{0,16},{4,20},{8,24},{12,28},{16,0},{20,4},{24,8},{28,12},{1,17},{... | collective-permute-start | bytes 1327112 | tf_op jit(solution)/shard_map/ppermute | solution.py:185
  (102 other events, 1314.7 us)
Sparse Core Ops, SparseCore 0:
  9.6 70.9 all-gather.8
  82.2 48.5 all-gather.4
  480.2 48.5 all-gather.6
  677.0 45.7 reduce-scatter.7
  725.0 44.9 reduce-scatter.9
  872.7 22.7 reduce-scatter.15
  897.8 44.4 reduce-scatter.11
  944.6 22.3 reduce-scatter.13

commit v2 on v1

--- a/solution.py
+++ b/solution.py
@@ -224,7 +224,7 @@
         grid_spec=pltpu.PrefetchScalarGridSpec(
             num_scalar_prefetch=1,
             grid=(1,),
-            in_specs=[pl.BlockSpec(memory_space=pl.ANY)] * len(pieces),
+            in_specs=[pl.BlockSpec(memory_space=pltpu.VMEM)] * len(pieces),
             out_specs=pl.BlockSpec(memory_space=pl.ANY),
             scratch_shapes=[pltpu.SemaphoreType.DMA((len(pieces),))],
         ),
@@ -245,17 +245,23 @@
     return place(lax.axis_index("dp"), pieces, n, sum(x.shape[0] for x in chunks))
 
 
-def scatter_dp(g):
+def core_half(grads, mine):
+    n = lax.axis_size("dp")
+    core = lax.axis_index("dp") % 2
+    which = core if mine else 1 - core
+    cut_out = [
+        lax.dynamic_index_in_dim(g.reshape((n // 2, 2) + g.shape[1:]), which, 1, keepdims=False) for g in grads
+    ]
+    return jnp.concatenate(cut_out, axis=2)
+
+
+def scatter_dp(grads, send=None):
     n = lax.axis_size("dp")
     if n != 8:
-        return lax.psum_scatter(g, "dp", scatter_dimension=0).astype(F32)
-    me = lax.axis_index("dp")
-    group, core = me // 2, me % 2
-    pairs = g.reshape((n // 2, 2) + g.shape[1:])
-    keep = lax.dynamic_index_in_dim(pairs, core, 1, keepdims=False)
-    send = lax.dynamic_index_in_dim(pairs, 1 - core, 1, keepdims=False)
-    got = swap(send, 1)
-    summed = (keep.astype(F32) + got.astype(F32)).astype(BF)
+        return lax.psum_scatter(jnp.concatenate(grads, axis=2), "dp", scatter_dimension=0).astype(F32)
+    group = lax.axis_index("dp") // 2
+    got = swap(core_half(grads, False) if send is None else send, 1)
+    summed = (core_half(grads, True).astype(F32) + got.astype(F32)).astype(BF)
     total = lax.dynamic_index_in_dim(summed, group, 0, keepdims=False).astype(F32)
     for d in range(1, n // 2):
         part = lax.dynamic_index_in_dim(summed, group ^ d, 0, keepdims=False)
@@ -326,26 +332,24 @@
     ).reshape(1, 8 * share)
     thin_all = gather_dp([jnp.concatenate([thin, up_bias.reshape(1, -1)], axis=1)])
     thin_all = thin_all.reshape(n, 8 * share + up_bias.shape[0])
+    cut = -(-share // 16) * 8
+    raw = ring_z(qkv_weight)
+    raw, own_x, thin_all = lax.optimization_barrier((raw, inputs[0], thin_all))
     vectors = (
         thin_all[:, : 8 * share].reshape(n, 8, share).transpose(1, 0, 2).reshape(8, width).astype(F32)
     )
     up_bias_all = thin_all[:, 8 * share:].reshape(ff_total).astype(F32)
     gain1, shift1, bias_q, bias_v, bias_o, gain2, shift2, bias_d = [vectors[i] for i in range(8)]
     up_shift = lax.dynamic_slice_in_dim(up_bias_all, z * ff, ff)
-
-    x_full = gather_z(inputs[0])
+    x_full = gather_z(own_x)
     cot, _ = lax.optimization_barrier((cotangent[0], x_full))
     g_full = gather_z(cot)
-
-    cut = -(-share // 16) * 8
-    chunks = []
-    for lo, hi in ((0, cut), (cut, share)):
-        raw = jnp.concatenate(ring_z(qkv_weight[lo:hi]), axis=1)
-        wq_s = pad_cols(raw[:, :width], wide)
-        wk_s = pad_cols(raw[:, width : 2 * width], wide)
-        wv_s = pad_cols(raw[:, 2 * width :], wide)
-        chunks.append(jnp.concatenate([wq_s, pair_up(wk_s, wv_s)], axis=1))
-    qkv_full = gather_dp(chunks).reshape(width, 3 * wide)
+    raw = jnp.concatenate(raw, axis=1)
+    wq_s = pad_cols(raw[:, :width], wide)
+    wk_s = pad_cols(raw[:, width : 2 * width], wide)
+    wv_s = pad_cols(raw[:, 2 * width :], wide)
+    qkv_s = jnp.concatenate([wq_s, pair_up(wk_s, wv_s)], axis=1)
+    qkv_full = gather_dp([qkv_s]).reshape(width, 3 * wide)
     out_rows = jnp.concatenate(ring_z(out_weight), axis=1)
     out_rows, up_s, down_s, qkv_full = lax.optimization_barrier((out_rows, up_weight, down_weight, qkv_full))
     wq = qkv_full[:, :wide]
@@ -384,21 +388,27 @@
     mlp_part, _ = lax.optimization_barrier((mm(hidden, down_t, NT).astype(BF), grad_mlp))
     mlp_out = scatter_z(mlp_part)
     up_b_block = jnp.sum(grad_pre, axis=0)
-    mlp_dw = jnp.concatenate([mm(mlp_full, grad_pre_b, TN), mm(g_full, hidden, TN)], axis=1).astype(BF)
+    up_dw = mm(mlp_full, grad_pre_b, TN).astype(BF).reshape(n, share, ff)
+    down_dw = mm(g_full, hidden, TN).astype(BF).reshape(n, share, ff)
+
     grad_resid = grad_out + ln_back(grad_mlp, normed2, inv2, gain2)
     grad_resid_b = grad_resid.astype(BF)
     grad_ctx = pad_cols(mm(grad_resid_b, wo, NT).astype(BF), wide)
-    dwo = scatter_dp(mm(ctx, grad_resid_b, TN).astype(BF).reshape(n, share, width))
+    dwo = scatter_dp([mm(ctx, grad_resid_b, TN).astype(BF).reshape(n, share, width)])
     dq, dkv = attend_back(meta, q, kv, lse, grad_ctx)
-    mlp_dw = scatter_dp(mlp_dw.reshape(n, share, 2 * ff))
+    mlp_dw = scatter_dp([up_dw, down_dw])
     dq, dkv, mlp_out = lax.optimization_barrier((dq, dkv, mlp_out))
     outputs = (resid + mlp_out + bias_d).astype(BF)
     up_grad = mlp_dw[:, :ff]
     down_grad = mlp_dw[:, ff:].T
-    dw = jnp.concatenate([mm(attn_own, dq, TN), mm(attn_full, dkv, TN)], axis=1).astype(BF)
-    dq, dkv, dw = lax.optimization_barrier((dq, dkv, dw))
-    dw = dw.reshape(n, share, 3 * wide)
-    dw_parts = [scatter_dp(dw[:, :cut]), scatter_dp(dw[:, cut:])]
+    dwq = mm(attn_own, dq, TN).astype(BF).reshape(n, share, wide)
+    dwkv = mm(attn_full, dkv, TN).astype(BF).reshape(n, share, 2 * wide)
+    dw_a = [dwq[:, :cut], dwkv[:, :cut]]
+    dw_b = [dwq[:, cut:], dwkv[:, cut:]]
+    dq, dkv, send_a, send_b = lax.optimization_barrier(
+        (dq, dkv, core_half(dw_a, False), core_half(dw_b, False))
+    )
+    dw_parts = [scatter_dp(dw_a, send_a), scatter_dp(dw_b, send_b)]
     part_kv = mm(dkv, wkv, NT)
     part_q = mm(dq, wq, NT)
     grad_attn = scatter_z(part_kv.astype(BF))
@@ -422,7 +432,7 @@
         axis=1,
     )
     thin_len = thin_grad.shape[1]
-    thin_grad = scatter_dp(thin_grad.astype(BF)[:, None, :])
+    thin_grad = scatter_dp([thin_grad.astype(BF)[:, None, :]])
 
     piece = qkv_cols + width // zs
     dwo = dwo.astype(BF)

time: 988 us -> 535 us (0.54)
  Pallas kernels: 495 us -> 56.8 us
  starting transfers between devices: 69.7 us -> 51.1 us
  waiting for transfers between devices: 199 us -> 217 us
    pallas_call x4, Pallas kernels: 454 us -> 15.5 us  [place(): pl.pallas_call(place_kernel, grid_spec=pltpu.PrefetchScalarGridSpec(num_s...]
    ppermute x55 -> x48, waiting for transfers between devices: 140 us -> 157 us  [swap(): return lax.ppermute(x, 'dp', [(i, i ^ bit) for i in range(n)])]
    ppermute x9 -> x6, starting transfers between devices: 27.9 us -> 12.7 us  [ring_z(): lax.ppermute(x, 'seq', [(i, (i + d) % size) for i in range(size)])]
    ppermute x55 -> x48, starting transfers between devices: 41.1 us -> 36.8 us  [swap(): return lax.ppermute(x, 'dp', [(i, i ^ bit) for i in range(n)])]
  transfers between devices with their start and end apart: 72 -> 62, of which waited for: 26 -> 30; matrix products, arithmetic and copies ran while one was open for 16% -> 24% of each run, Pallas kernels for 50% -> 11%
where the time goes in v2:
time: 535 us; the launch traced here: 529 us
  waiting for transfers between devices  217 us (41%)
  matrix products  82.6 us (15%)
  local copies, waits for them, and re-layouts  58 us (11%)
  Pallas kernels  56.8 us (11%)
  starting transfers between devices  51.1 us (10%)
  other arithmetic  47.1 us (9%)
  between operations  16.2 us (3%)
    ppermute x48, waiting for transfers between devices, swap(): return lax.ppermute(x, 'dp', [(i, i ^ bit) for i in range(n)])  157 us
    dot_general x15, matrix products, mm(): return lax.dot_general(a, b, (dims, ((), ())), preferred_element_type=F32)  82.6 us
    reduce_scatter x4, waiting for transfers between devices, scatter_z(): lax.psum_scatter(x, 'seq', scatter_dimension=0, tiled=True).astype(F32)  41 us
    ppermute x48, starting transfers between devices, swap(): return lax.ppermute(x, 'dp', [(i, i ^ bit) for i in range(n)])  36.8 us
    pallas_call x1, Pallas kernels, attend_back(): pl.pallas_call(attend_back_kernel, grid_spec=pltpu.PrefetchScalarGridSpec...  21.6 us
    pallas_call x1, Pallas kernels, attend(): pl.pallas_call(attend_kernel, grid_spec=pltpu.PrefetchScalarGridSpec(num_...  19.8 us
    pallas_call x4, Pallas kernels, place(): pl.pallas_call(place_kernel, grid_spec=pltpu.PrefetchScalarGridSpec(num_s...  15.5 us
    unnamed x135, local copies, waits for them, and re-layouts  14.3 us
  transfers between devices with their start and end apart: 62, of which 30 were waited for; matrix products, arithmetic and copies ran while one was open for 24% of the time, Pallas kernels for 11%

profile of v2, /device:TPU:0, one launch (start us, length us, event | category | flops | bytes accessed | tf_op | source)
XLA Modules:
  0.0 529.3 jit_solution(9401682743856034680)
XLA Ops:
  7.2 4.1 collective-permute-start.1
  19.6 2.5 collective-permute-start.8
  36.5 2.5 collective-permute-start.18
  40.0 2.8 collective-permute-start.11
  43.1 18.1 %collective-permute-done.18.refs_6_ = bf16[136,3456]{1,0:T(8,128)(2,1)S(1)} collective-permute-done((bf16[136,3456]{1,0:T(8,128)(2,1)S(1)}, bf16[136,3456]{1,0:T(8,128)(2,1)S(1)}, u32[]{:S(2)}, u32[]{:S(2)}) %collective-permute-start.18) | collective-permute-done | bytes 940064 | tf_op jit(solution)/shard_map/ppermute | solution.py:185
  61.2 19.4 %collective-permute-done.16.refs_4_ = bf16[136,3456]{1,0:T(8,128)(2,1)} collective-permute-done((bf16[136,3456]{1,0:T(8,128)(2,1)S(1)}, bf16[136,3456]{1,0:T(8,128)(2,1)}, u32[]{:S(2)}, u32[]{:S(2)}) %collective-permute-start.16) | collective-permute-done | bytes 940064 | tf_op jit(solution)/shard_map/ppermute | solution.py:185
  81.3 3.2 collective-permute-start.10
  85.2 4.6 collective-permute-done.10
  91.0 5.6 %collective-permute-done.12 = bf16[136,272]{1,0:T(8,128)(2,1)S(1)} collective-permute-done((bf16[136,272]{1,0:T(8,128)(2,1)S(1)}, bf16[136,272]{1,0:T(8,128)(2,1)S(1)}, u32[]{:S(2)}, u32[]{:S(2)}) %collective-permute-start.12) | collective-permute-done | bytes 74016 | tf_op jit(solution)/shard_map/ppermute | solution.py:193
  97.0 6.2 %place.5 = bf16[8,136,3456]{2,1,0:T(8,128)(2,1)} custom-call(s32[1]{0:T(128)} %bitcast.2.meta, bf16[136,3456]{1,0:T(8,128)(2,1)} %copy-done.13, bf16[136,3456]{1,0:T(8,128)(2,1)} %collective-permute-done.13.refs_1_, bf16[136,3456]{1,0:T(8,128)(2,1)} %collective-permute-done.14.refs_2_, bf16[136,3456]{1,0:T(8,128)(2,1)} %collective-permute-done.15.refs_3_, ...), custom_call_target="tpu_custom_call" | custom-call | tf_op jit(solution)/shard_map/place/pallas_call | solution.py:222
  108.7 5.8 %collective-permute-done.25.refs_6_ = bf16[136,1088]{1,0:T(8,128)(2,1)S(1)} collective-permute-done((bf16[136,1088]{1,0:T(8,128)(2,1)S(1)}, bf16[136,1088]{1,0:T(8,128)(2,1)S(1)}, u32[]{:S(2)}, u32[]{:S(2)}) %collective-permute-start.25) | collective-permute-done | bytes 295968 | tf_op jit(solution)/shard_map/ppermute | solution.py:185
  114.5 5.1 collective-permute-done.23.refs_4_
  120.1 3.7 fusion.17.q_ref
  126.0 3.1 place.6
  130.3 10.7 %add_convert_fusion.kv_ref = bf16[1024,2304]{1,0:T(8,128)(2,1)} fusion(f32[2304]{0:T(1024)S(1)} %add.381, bf16[1088,3456]{1,0:T(8,128)(2,1)} %bitcast.208, bf16[1024,1088]{0,1:T(8,128)(2,1)S(1)} %copy-done.4, f32[1088]{0:T(1024)S(1)} %add.372, f32[1088]{0:T(1024)S(1)} %mul.192, f32[1024]{0:T(1024)S(1)} %add_rsqrt_fusion, f32[1024]{0:T(1024)S(1)} %broadcast_multiply_fusion), kind=kOutput, calls=%fused_computation.1 | convolution fusion | flops 5145231360 | bytes 11986432 | tf_op jit(solution)/shard_map/dot_general | solution.py:19
  141.0 19.8 %attend.1 = (bf16[256,1152]{1,0:T(8,128)(2,1)}, f32[9,2,256]{2,1,0:T(2,128)}) custom-call(s32[2]{0:T(128)} %pad_add_fusion.meta, bf16[256,1152]{1,0:T(8,128)(2,1)} %fusion.17.q_ref, bf16[1024,2304]{1,0:T(8,128)(2,1)} %add_convert_fusion.kv_ref), custom_call_target="tpu_custom_call" | custom-call | flops 2415919104 | bytes 7077888 | tf_op jit(solution)/shard_map/attend/pallas_call | solution.py:90
  160.8 3.1 fusion.114
  169.4 13.7 %collective-permute-done.32.refs_6_ = bf16[136,2176]{1,0:T(8,128)(2,1)S(1)} collective-permute-done((bf16[136,2176]{1,0:T(8,128)(2,1)S(1)}, bf16[136,2176]{1,0:T(8,128)(2,1)S(1)}, u32[]{:S(2)}, u32[]{:S(2)}) %collective-permute-start.32) | collective-permute-done | bytes 591904 | tf_op jit(solution)/shard_map/ppermute | solution.py:185
  183.1 11.7 %collective-permute-done.30.refs_4_ = bf16[136,2176]{1,0:T(8,128)(2,1)S(1)} collective-permute-done((bf16[136,2176]{1,0:T(8,128)(2,1)S(1)}, bf16[136,2176]{1,0:T(8,128)(2,1)S(1)}, u32[]{:S(2)}, u32[]{:S(2)}) %collective-permute-start.30) | collective-permute-done | bytes 591904 | tf_op jit(solution)/shard_map/ppermute | solution.py:185
  197.8 4.6 place.7
  202.4 9.0 %all-gather.8.cloned.1.call-done = bf16[1024,1088]{0,1:T(8,128)(2,1)} async-done(((bf16[256,1088]{0,1:T(8,128)(2,1)}), bf16[1024,1088]{0,1:T(8,128)(2,1)}) %all-gather.8.cloned.1.call-update) | async-done | bytes 2228240 | tf_op jit(solution)/shard_map/all_gather | solution.py:273
  211.4 5.7 %convolution_add_fusion = f32[1024,1088]{0,1:T(8,128)S(1)} fusion(bf16[1024,1088]{0,1:T(8,128)(2,1)} %all-gather.8.cloned.1.call-done, f32[1088]{0:T(1024)S(1)} %dynamic_slice.122, bf16[1088,2176]{1,0:T(8,128)(2,1)} %bitcast.214), kind=kOutput, calls=%fused_computation.16 | convolution fusion | flops 2425421824 | bytes 9195776 | tf_op jit(solution)/shard_map/dot_general | solution.py:19
  217.2 8.0 %fusion.115 = (bf16[1088]{0:T(1024)(128)(2,1)S(1)}, bf16[1024,1088]{0,1:T(8,128)(2,1)S(1)}) fusion(f32[1024,1088]{0,1:T(8,128)S(1)} %convolution_add_fusion, bf16[1088,2176]{1,0:T(8,128)(2,1)S(1)} %bitcast.216, bf16[1024,1088]{0,1:T(8,128)(2,1)S(1)} %copy-done.56, bf16[1024]{0:T(1024)(128)(2,1)S(1)} %fusion.102), kind=kOutput, calls=%fused_computation.255 | convolution fusion | flops 2447703040 | bytes 11423872 | tf_op jit(solution)/shard_map/dot_general | solution.py:19
  226.6 4.2 convolution_convert_fusion.6
  231.3 5.5 %convolution_convert_fusion.4 = bf16[1088,1088]{1,0:T(8,128)(2,1)S(1)} fusion(bf16[1024,1088]{0,1:T(8,128)(2,1)} %all-gather.8.cloned.1.call-done, bf16[1024,1088]{0,1:T(8,128)(2,1)} %copy-done.59), kind=kOutput, calls=%fused_computation.5 | convolution fusion | flops 2425491456 | bytes 6823936 | tf_op jit(solution)/shard_map/dot_general | solution.py:19
  236.8 5.5 %convolution_convert_fusion.3 = bf16[1088,1088]{1,0:T(8,128)(2,1)S(1)} fusion(bf16[1024,1088]{0,1:T(8,128)(2,1)S(1)} %copy-done.57, bf16[1024]{0:T(1024)(128)(2,1)S(1)} %fusion.102, f32[1024,1088]{0,1:T(8,128)} %copy-done.58), kind=kOutput, calls=%fused_computation.4 | convolution fusion | flops 2436632576 | bytes 9054208 | tf_op jit(solution)/shard_map/dot_general | solution.py:19
  245.9 7.8 %convolution_convert_fusion.5 = bf16[1024,1088]{0,1:T(8,128)(2,1)} fusion(bf16[1088,2176]{1,0:T(8,128)(2,1)} %bitcast.215, f32[1024,1088]{0,1:T(8,128)} %copy-done.58), kind=kOutput, calls=%fused_computation.31 | convolution fusion | flops 2435448832 | bytes 9191424 | tf_op jit(solution)/shard_map/dot_general | solution.py:19
  254.0 3.1 add_convert_fusion.1
  263.2 11.9 %collective-permute-done.51 = bf16[136,2176]{1,0:T(8,128)(2,1)} collective-permute-done((bf16[136,2176]{1,0:T(8,128)(2,1)S(1)}, bf16[136,2176]{1,0:T(8,128)(2,1)}, u32[]{:S(2)}, u32[]{:S(2)}) %collective-permute-start.51) | collective-permute-done | bytes 591904 | tf_op jit(solution)/shard_map/ppermute | solution.py:185
  275.1 13.2 %collective-permute-done.53 = bf16[136,2176]{1,0:T(8,128)(2,1)} collective-permute-done((bf16[136,2176]{1,0:T(8,128)(2,1)S(1)}, bf16[136,2176]{1,0:T(8,128)(2,1)}, u32[]{:S(2)}, u32[]{:S(2)}) %collective-permute-start.53) | collective-permute-done | bytes 591904 | tf_op jit(solution)/shard_map/ppermute | solution.py:185
  300.3 3.5 convolution_convert_fusion.1
  303.8 21.6 %attend_back.1 = (bf16[256,1152]{1,0:T(8,128)(2,1)}, bf16[1024,2304]{1,0:T(8,128)(2,1)}) custom-call(s32[2]{0:T(128)} %pad_add_fusion.meta, bf16[256,1152]{1,0:T(8,128)(2,1)} %fusion.17.q_ref, bf16[1024,2304]{1,0:T(8,128)(2,1)} %add_convert_fusion.kv_ref, f32[9,2,256]{2,1,0:T(2,128)} %get-tuple-element.53.lse_ref, bf16[256,1152]{1,0:T(8,128)(2,1)} %pad.38.g_ref), custom_call_target="tpu_custom_call" | custom-call | flops 6039797760 | bytes 14155776 | tf_op jit(solution)/shard_map/attend_back/pallas_call | solution.py:155
  327.5 2.3 convolution_convert_fusion.2
  332.1 6.4 %convolution_convert_fusion = bf16[1088,2304]{1,0:T(8,128)(2,1)S(1)} fusion(bf16[1024,2304]{1,0:T(8,128)(2,1)S(1)} %copy-done.12, bf16[1024,1088]{0,1:T(8,128)(2,1)S(1)} %copy-done.5, f32[1088]{0:T(1024)S(1)} %add.372, f32[1088]{0:T(1024)S(1)} %mul.192, f32[1024]{0:T(1024)S(1)} %copy-done.54, f32[1024]{0:T(1024)S(1)} %copy-done.44), kind=kOutput, calls=%fused_computation | convolution fusion | flops 5143019520 | bytes 11977216 | tf_op jit(solution)/shard_map/dot_general | solution.py:19
  344.8 2.6 dynamic-slice_bitcast_fusion.6
  356.9 3.0 reduce.1
  360.7 10.6 %fusion.107 = (f32[1088]{0:T(1024)S(1)}, f32[1088]{0:T(1024)S(1)}, bf16[1024,1088]{0,1:T(8,128)(2,1)}) fusion(f32[1024]{0:T(1024)S(1)} %copy-done.54, f32[1024]{0:T(1024)S(1)} %copy-done.44, bf16[1024,1088]{0,1:T(8,128)(2,1)} %all-gather.4.cloned.1.call-done, bf16[1024,2304]{1,0:T(8,128)(2,1)} %get-tuple-element.64, bf16[1088,3456]{1,0:T(8,128)(2,1)} %bitcast.209), kind=kOutput, calls=%fused_computation.247 | convolution fusion | flops 5141624832 | bytes 14205440 | tf_op jit(solution)/shard_map/dot_general | solution.py:19
  371.3 3.7 fusion.109
  384.9 3.0 collective-permute-done.39
  389.5 5.3 collective-permute-done.41
  397.1 8.2 %collective-permute-done.47 = bf16[72,3456]{1,0:T(8,128)(2,1)S(1)} collective-permute-done((bf16[72,3456]{1,0:T(8,128)(2,1)S(1)}, bf16[72,3456]{1,0:T(8,128)(2,1)S(1)}, u32[]{:S(2)}, u32[]{:S(2)}) %collective-permute-start.47) | collective-permute-done | bytes 497696 | tf_op jit(solution)/shard_map/ppermute | solution.py:185
  405.4 10.3 %collective-permute-done.49 = bf16[72,3456]{1,0:T(8,128)(2,1)S(1)} collective-permute-done((bf16[72,3456]{1,0:T(8,128)(2,1)S(1)}, bf16[72,3456]{1,0:T(8,128)(2,1)S(1)}, u32[]{:S(2)}, u32[]{:S(2)}) %collective-permute-start.49) | collective-permute-done | bytes 497696 | tf_op jit(solution)/shard_map/ppermute | solution.py:185
  427.0 2.3 fusion.66
  433.4 2.2 add_convert_fusion.3
  441.8 9.5 %collective-permute-done.35 = bf16[64,3456]{1,0:T(8,128)(2,1)S(1)} collective-permute-done((bf16[64,3456]{1,0:T(8,128)(2,1)}, bf16[64,3456]{1,0:T(8,128)(2,1)S(1)}, u32[]{:S(2)}, u32[]{:S(2)}) %collective-permute-start.35) | collective-permute-done | bytes 442400 | tf_op jit(solution)/shard_map/ppermute | solution.py:185
  451.2 9.1 %collective-permute-done.37 = bf16[64,3456]{1,0:T(8,128)(2,1)S(1)} collective-permute-done((bf16[64,3456]{1,0:T(8,128)(2,1)}, bf16[64,3456]{1,0:T(8,128)(2,1)S(1)}, u32[]{:S(2)}, u32[]{:S(2)}) %collective-permute-start.37) | collective-permute-done | bytes 442400 | tf_op jit(solution)/shard_map/ppermute | solution.py:185
  471.6 20.4 %reduce-scatter.12.cloned.1.call-done = bf16[256,1088]{0,1:T(8,128)(2,1)} async-done(((bf16[1024,1088]{0,1:T(8,128)(2,1)}), bf16[256,1088]{0,1:T(8,128)(2,1)}) %reduce-scatter.12.cloned.1.call-update) | async-done | bytes 557072 | tf_op jit(solution)/shard_map/reduce_scatter | solution.py:277
  496.1 20.6 %reduce-scatter.14.cloned.1.call-done = bf16[80,1088]{1,0:T(8,128)(2,1)} async-done(((bf16[320,1088]{1,0:T(8,128)(2,1)}), bf16[80,1088]{1,0:T(8,128)(2,1)}) %reduce-scatter.14.cloned.1.call-update) | async-done | bytes 174096 | tf_op jit(solution)/shard_map/reduce_scatter | solution.py:277
  (393 shorter events, 143.9 us)
Async XLA Ops:
  7.2 99.6 %all-gather.4.cloned.1.call-start = ((), (), s32[]{:S(2)}) async-start(), calls=%async_computation.5 | async-start | bytes 2785280 | tf_op jit(solution)/shard_map/all_gather | solution.py:273
  7.2 25.8 %collective-permute-start.1 = (bf16[136,816]{1,0:T(8,128)(2,1)}, bf16[136,816]{1,0:T(8,128)(2,1)S(1)}, u32[]{:S(2)}, u32[]{:S(2)}) collective-permute-start(bf16[136,816]{1,0:T(8,128)(2,1)} %param.21), channel_id=1, source_target_pairs={{0,2},{1,3},{2,0},{3,1},{4,6},{5,7},{6,4},{7,5},{8,10},{9,11},{10,... | collective-permute-start | bytes 665864 | tf_op jit(solution)/shard_map/ppermute | solution.py:193
  11.4 21.7 %collective-permute-start = (bf16[136,816]{1,0:T(8,128)(2,1)}, bf16[136,816]{1,0:T(8,128)(2,1)S(1)}, u32[]{:S(2)}, u32[]{:S(2)}) collective-permute-start(bf16[136,816]{1,0:T(8,128)(2,1)} %param.21), channel_id=1, source_target_pairs={{0,3},{1,0},{2,1},{3,2},{4,7},{5,4},{6,5},{7,6},{8,11},{9,8},{10,9... | collective-permute-start | bytes 665864 | tf_op jit(solution)/shard_map/ppermute | solution.py:193
  12.7 20.3 %collective-permute-start.2 = (bf16[136,816]{1,0:T(8,128)(2,1)}, bf16[136,816]{1,0:T(8,128)(2,1)S(1)}, u32[]{:S(2)}, u32[]{:S(2)}) collective-permute-start(bf16[136,816]{1,0:T(8,128)(2,1)} %param.21), channel_id=1, source_target_pairs={{0,1},{1,2},{2,3},{3,0},{4,5},{5,6},{6,7},{7,4},{8,9},{9,10},{10,1... | collective-permute-start | bytes 665864 | tf_op jit(solution)/shard_map/ppermute | solution.py:193
  34.1 126.6 %all-gather.6.cloned.1.call-start = ((), (), s32[]{:S(2)}) async-start(), calls=%async_computation.6 | async-start | bytes 2785280 | tf_op jit(solution)/shard_map/all_gather | solution.py:273
  36.5 24.7 %collective-permute-start.18 = (bf16[136,3456]{1,0:T(8,128)(2,1)S(1)}, bf16[136,3456]{1,0:T(8,128)(2,1)S(1)}, u32[]{:S(2)}, u32[]{:S(2)}) collective-permute-start(bf16[136,3456]{1,0:T(8,128)(2,1)S(1)} %pad_maximum_fusion.4.refs_0_), channel_id=1, source_target_pairs={{0,24},{4,28},{8,16},{12,20},{16,8},{20,12},{24,0},{28,4},{1,25},{... | collective-permute-start | bytes 2820104 | tf_op jit(solution)/shard_map/ppermute | solution.py:185
  39.0 41.6 %collective-permute-start.16 = (bf16[136,3456]{1,0:T(8,128)(2,1)S(1)}, bf16[136,3456]{1,0:T(8,128)(2,1)}, u32[]{:S(2)}, u32[]{:S(2)}) collective-permute-start(bf16[136,3456]{1,0:T(8,128)(2,1)S(1)} %pad_maximum_fusion.4.refs_0_), channel_id=1, source_target_pairs={{0,16},{4,20},{8,24},{12,28},{16,0},{20,4},{24,8},{28,12},{1,17},{... | collective-permute-start | bytes 2820104 | tf_op jit(solution)/shard_map/ppermute | solution.py:185
  39.5 41.2 %collective-permute-start.14 = (bf16[136,3456]{1,0:T(8,128)(2,1)S(1)}, bf16[136,3456]{1,0:T(8,128)(2,1)}, u32[]{:S(2)}, u32[]{:S(2)}) collective-permute-start(bf16[136,3456]{1,0:T(8,128)(2,1)S(1)} %pad_maximum_fusion.4.refs_0_), channel_id=1, source_target_pairs={{0,8},{4,12},{8,0},{12,4},{16,24},{20,28},{24,16},{28,20},{1,9},{5... | collective-permute-start | bytes 2820104 | tf_op jit(solution)/shard_map/ppermute | solution.py:185
  40.0 41.3 %collective-permute-start.11 = (bf16[136,272]{1,0:T(8,128)(2,1)S(1)}, bf16[136,272]{1,0:T(8,128)(2,1)S(1)}, u32[]{:S(2)}, u32[]{:S(2)}) collective-permute-start(bf16[136,272]{1,0:T(8,128)(2,1)S(1)} %copy-done.34), channel_id=1, source_target_pairs={{0,2},{1,3},{2,0},{3,1},{4,6},{5,7},{6,4},{7,5},{8,10},{9,11},{10,... | collective-permute-start | bytes 221960 | tf_op jit(solution)/shard_map/ppermute | solution.py:193
  43.0 53.9 %collective-permute-start.13 = (bf16[136,3456]{1,0:T(8,128)(2,1)S(1)}, bf16[136,3456]{1,0:T(8,128)(2,1)}, u32[]{:S(2)}, u32[]{:S(2)}) collective-permute-start(bf16[136,3456]{1,0:T(8,128)(2,1)S(1)} %pad_maximum_fusion.4.refs_0_), channel_id=1, source_target_pairs={{0,4},{4,0},{8,12},{12,8},{16,20},{20,16},{24,28},{28,24},{1,5},{5... | collective-permute-start | bytes 2820104 | tf_op jit(solution)/shard_map/ppermute | solution.py:185
  61.2 35.7 %collective-permute-start.19 = (bf16[136,3456]{1,0:T(8,128)(2,1)S(1)}, bf16[136,3456]{1,0:T(8,128)(2,1)}, u32[]{:S(2)}, u32[]{:S(2)}) collective-permute-start(bf16[136,3456]{1,0:T(8,128)(2,1)S(1)} %collective-permute-done.18.refs_6_), channel_id=1, source_target_pairs={{0,4},{4,0},{8,12},{12,8},{16,20},{20,16},{24,28},{28,24},{1,5},{5... | collective-permute-start | bytes 2820104 | tf_op jit(solution)/shard_map/ppermute | solution.py:185
  80.6 16.3 %collective-permute-start.17 = (bf16[136,3456]{1,0:T(8,128)(2,1)}, bf16[136,3456]{1,0:T(8,128)(2,1)}, u32[]{:S(2)}, u32[]{:S(2)}) collective-permute-start(bf16[136,3456]{1,0:T(8,128)(2,1)} %collective-permute-done.16.refs_4_), channel_id=1, source_target_pairs={{0,4},{4,0},{8,12},{12,8},{16,20},{20,16},{24,28},{28,24},{1,5},{5... | collective-permute-start | bytes 2820104 | tf_op jit(solution)/shard_map/ppermute | solution.py:185
  80.7 16.2 %collective-permute-start.15 = (bf16[136,3456]{1,0:T(8,128)(2,1)}, bf16[136,3456]{1,0:T(8,128)(2,1)}, u32[]{:S(2)}, u32[]{:S(2)}) collective-permute-start(bf16[136,3456]{1,0:T(8,128)(2,1)} %collective-permute-done.14.refs_2_), channel_id=1, source_target_pairs={{0,4},{4,0},{8,12},{12,8},{16,20},{20,16},{24,28},{28,24},{1,5},{5... | collective-permute-start | bytes 2820104 | tf_op jit(solution)/shard_map/ppermute | solution.py:185
  81.3 8.5 %collective-permute-start.10 = (bf16[136,272]{1,0:T(8,128)(2,1)S(1)}, bf16[136,272]{1,0:T(8,128)(2,1)S(1)}, u32[]{:S(2)}, u32[]{:S(2)}) collective-permute-start(bf16[136,272]{1,0:T(8,128)(2,1)S(1)} %copy-done.34), channel_id=1, source_target_pairs={{0,3},{1,0},{2,1},{3,2},{4,7},{5,4},{6,5},{7,6},{8,11},{9,8},{10,9... | collective-permute-start | bytes 221960 | tf_op jit(solution)/shard_map/ppermute | solution.py:193
  103.2 11.3 %collective-permute-start.25 = (bf16[136,1088]{1,0:T(8,128)(2,1)S(1)}, bf16[136,1088]{1,0:T(8,128)(2,1)S(1)}, u32[]{:S(2)}, u32[]{:S(2)}) collective-permute-start(bf16[136,1088]{1,0:T(8,128)(2,1)S(1)} %concatenate.105.refs_0_), channel_id=1, source_target_pairs={{0,24},{4,28},{8,16},{12,20},{16,8},{20,12},{24,0},{28,4},{1,25},{... | collective-permute-start | bytes 887816 | tf_op jit(solution)/shard_map/ppermute | solution.py:185
  105.2 14.4 %collective-permute-start.23 = (bf16[136,1088]{1,0:T(8,128)(2,1)S(1)}, bf16[136,1088]{1,0:T(8,128)(2,1)}, u32[]{:S(2)}, u32[]{:S(2)}) collective-permute-start(bf16[136,1088]{1,0:T(8,128)(2,1)S(1)} %concatenate.105.refs_0_), channel_id=1, source_target_pairs={{0,16},{4,20},{8,24},{12,28},{16,0},{20,4},{24,8},{28,12},{1,17},{... | collective-permute-start | bytes 887816 | tf_op jit(solution)/shard_map/ppermute | solution.py:185
  106.3 13.4 %collective-permute-start.21 = (bf16[136,1088]{1,0:T(8,128)(2,1)S(1)}, bf16[136,1088]{1,0:T(8,128)(2,1)}, u32[]{:S(2)}, u32[]{:S(2)}) collective-permute-start(bf16[136,1088]{1,0:T(8,128)(2,1)S(1)} %concatenate.105.refs_0_), channel_id=1, source_target_pairs={{0,8},{4,12},{8,0},{12,4},{16,24},{20,28},{24,16},{28,20},{1,9},{5... | collective-permute-start | bytes 887816 | tf_op jit(solution)/shard_map/ppermute | solution.py:185
  106.8 104.6 %all-gather.8.cloned.1.call-start = ((), (), s32[]{:S(2)}) async-start(), calls=%async_computation.7 | async-start | bytes 2785280 | tf_op jit(solution)/shard_map/all_gather | solution.py:273
  108.6 15.3 %collective-permute-start.20 = (bf16[136,1088]{1,0:T(8,128)(2,1)S(1)}, bf16[136,1088]{1,0:T(8,128)(2,1)S(1)}, u32[]{:S(2)}, u32[]{:S(2)}) collective-permute-start(bf16[136,1088]{1,0:T(8,128)(2,1)S(1)} %concatenate.105.refs_0_), channel_id=1, source_target_pairs={{0,4},{4,0},{8,12},{12,8},{16,20},{20,16},{24,28},{28,24},{1,5},{5... | collective-permute-start | bytes 887816 | tf_op jit(solution)/shard_map/ppermute | solution.py:185
  114.5 9.4 %collective-permute-start.26 = (bf16[136,1088]{1,0:T(8,128)(2,1)S(1)}, bf16[136,1088]{1,0:T(8,128)(2,1)S(1)}, u32[]{:S(2)}, u32[]{:S(2)}) collective-permute-start(bf16[136,1088]{1,0:T(8,128)(2,1)S(1)} %collective-permute-done.25.refs_6_), channel_id=1, source_target_pairs={{0,4},{4,0},{8,12},{12,8},{16,20},{20,16},{24,28},{28,24},{1,5},{5... | collective-permute-start | bytes 887816 | tf_op jit(solution)/shard_map/ppermute | solution.py:185
  165.3 127.4 %reduce-scatter.8.cloned.1.call-start = ((), (), s32[]{:S(2)}) async-start(), calls=%async_computation.8 | async-start | bytes 2785280 | tf_op jit(solution)/shard_map/reduce_scatter | solution.py:277
  165.8 17.3 %collective-permute-start.32 = (bf16[136,2176]{1,0:T(8,128)(2,1)S(1)}, bf16[136,2176]{1,0:T(8,128)(2,1)S(1)}, u32[]{:S(2)}, u32[]{:S(2)}) collective-permute-start(bf16[136,2176]{1,0:T(8,128)(2,1)S(1)} %pad_maximum_fusion.7.refs_0_), channel_id=1, source_target_pairs={{0,24},{4,28},{8,16},{12,20},{16,8},{20,12},{24,0},{28,4},{1,25},{... | collective-permute-start | bytes 1775624 | tf_op jit(solution)/shard_map/ppermute | solution.py:185
  167.6 27.2 %collective-permute-start.30 = (bf16[136,2176]{1,0:T(8,128)(2,1)S(1)}, bf16[136,2176]{1,0:T(8,128)(2,1)S(1)}, u32[]{:S(2)}, u32[]{:S(2)}) collective-permute-start(bf16[136,2176]{1,0:T(8,128)(2,1)S(1)} %pad_maximum_fusion.7.refs_0_), channel_id=1, source_target_pairs={{0,16},{4,20},{8,24},{12,28},{16,0},{20,4},{24,8},{28,12},{1,17},{... | collective-permute-start | bytes 1775624 | tf_op jit(solution)/shard_map/ppermute | solution.py:185
  168.8 26.1 %collective-permute-start.28 = (bf16[136,2176]{1,0:T(8,128)(2,1)S(1)}, bf16[136,2176]{1,0:T(8,128)(2,1)}, u32[]{:S(2)}, u32[]{:S(2)}) collective-permute-start(bf16[136,2176]{1,0:T(8,128)(2,1)S(1)} %pad_maximum_fusion.7.refs_0_), channel_id=1, source_target_pairs={{0,8},{4,12},{8,0},{12,4},{16,24},{20,28},{24,16},{28,20},{1,9},{5... | collective-permute-start | bytes 1775624 | tf_op jit(solution)/shard_map/ppermute | solution.py:185
  169.4 26.2 %collective-permute-start.27 = (bf16[136,2176]{1,0:T(8,128)(2,1)S(1)}, bf16[136,2176]{1,0:T(8,128)(2,1)}, u32[]{:S(2)}, u32[]{:S(2)}) collective-permute-start(bf16[136,2176]{1,0:T(8,128)(2,1)S(1)} %pad_maximum_fusion.7.refs_0_), channel_id=1, source_target_pairs={{0,4},{4,0},{8,12},{12,8},{16,20},{20,16},{24,28},{28,24},{1,5},{5... | collective-permute-start | bytes 1775624 | tf_op jit(solution)/shard_map/ppermute | solution.py:185
  183.0 12.5 %collective-permute-start.33 = (bf16[136,2176]{1,0:T(8,128)(2,1)S(1)}, bf16[136,2176]{1,0:T(8,128)(2,1)}, u32[]{:S(2)}, u32[]{:S(2)}) collective-permute-start(bf16[136,2176]{1,0:T(8,128)(2,1)S(1)} %collective-permute-done.32.refs_6_), channel_id=1, source_target_pairs={{0,4},{4,0},{8,12},{12,8},{16,20},{20,16},{24,28},{28,24},{1,5},{5... | collective-permute-start | bytes 1775624 | tf_op jit(solution)/shard_map/ppermute | solution.py:185
  230.8 94.5 %reduce-scatter.10.cloned.1.call-start = ((), (), s32[]{:S(2)}) async-start(), calls=%async_computation.9 | async-start | bytes 2785280 | tf_op jit(solution)/shard_map/reduce_scatter | solution.py:277
  253.8 216.9 %reduce-scatter.16.cloned.1.call-start = ((), (), s32[]{:S(2)}) async-start(), calls=%async_computation.12 | async-start | bytes 829440
  258.6 16.4 %collective-permute-start.51 = (bf16[136,2176]{1,0:T(8,128)(2,1)S(1)}, bf16[136,2176]{1,0:T(8,128)(2,1)}, u32[]{:S(2)}, u32[]{:S(2)}) collective-permute-start(bf16[136,2176]{1,0:T(8,128)(2,1)S(1)} %get-tuple-element.100), channel_id=1, source_target_pairs={{0,8},{4,12},{8,0},{12,4},{16,24},{20,28},{24,16},{28,20},{1,9},{5... | collective-permute-start | bytes 1775624 | tf_op jit(solution)/shard_map/ppermute | solution.py:185
  260.2 28.1 %collective-permute-start.53 = (bf16[136,2176]{1,0:T(8,128)(2,1)S(1)}, bf16[136,2176]{1,0:T(8,128)(2,1)}, u32[]{:S(2)}, u32[]{:S(2)}) collective-permute-start(bf16[136,2176]{1,0:T(8,128)(2,1)S(1)} %get-tuple-element.101), channel_id=1, source_target_pairs={{0,24},{4,28},{8,16},{12,20},{16,8},{20,12},{24,0},{28,4},{1,25},{... | collective-permute-start | bytes 1775624 | tf_op jit(solution)/shard_map/ppermute | solution.py:185
  261.6 28.0 %collective-permute-start.52 = (bf16[136,2176]{1,0:T(8,128)(2,1)S(1)}, bf16[136,2176]{1,0:T(8,128)(2,1)}, u32[]{:S(2)}, u32[]{:S(2)}) collective-permute-start(bf16[136,2176]{1,0:T(8,128)(2,1)S(1)} %get-tuple-element.102), channel_id=1, source_target_pairs={{0,16},{4,20},{8,24},{12,28},{16,0},{20,4},{24,8},{28,12},{1,17},{... | collective-permute-start | bytes 1775624 | tf_op jit(solution)/shard_map/ppermute | solution.py:185
  347.4 28.0 %collective-permute-start.38 = (bf16[4,136,1088]{2,1,0:T(8,128)(2,1)}, bf16[4,136,1088]{2,1,0:T(8,128)(2,1)}, u32[]{:S(2)}, u32[]{:S(2)}) collective-permute-start(bf16[4,136,1088]{2,1,0:T(8,128)(2,1)} %dynamic-slice_bitcast_fusion.6), channel_id=1, source_target_pairs={{0,4},{4,0},{8,12},{12,8},{16,20},{20,16},{24,28},{28,24},{1,5},{5... | collective-permute-start | bytes 3551240 | tf_op jit(solution)/shard_map/ppermute | solution.py:185
  360.1 21.1 %collective-permute-start.46 = (bf16[4,72,3456]{2,1,0:T(8,128)(2,1)}, bf16[4,72,3456]{2,1,0:T(8,128)(2,1)}, u32[]{:S(2)}, u32[]{:S(2)}) collective-permute-start(bf16[4,72,3456]{2,1,0:T(8,128)(2,1)} %pad_maximum_fusion.1), channel_id=1, source_target_pairs={{0,4},{4,0},{8,12},{12,8},{16,20},{20,16},{24,28},{28,24},{1,5},{5... | collective-permute-start | bytes 5971976 | tf_op jit(solution)/shard_map/ppermute | solution.py:185
  375.2 58.2 %collective-permute-start.34 = (bf16[4,64,3456]{2,1,0:T(8,128)(2,1)}, bf16[4,64,3456]{2,1,0:T(8,128)(2,1)}, u32[]{:S(2)}, u32[]{:S(2)}) collective-permute-start(bf16[4,64,3456]{2,1,0:T(8,128)(2,1)} %pad_maximum_fusion.2), channel_id=1, source_target_pairs={{0,4},{4,0},{8,12},{12,8},{16,20},{20,16},{24,28},{28,24},{1,5},{5... | collective-permute-start | bytes 5308424 | tf_op jit(solution)/shard_map/ppermute | solution.py:185
  377.6 10.3 %collective-permute-start.39 = (bf16[136,1088]{1,0:T(8,128)(2,1)S(1)}, bf16[136,1088]{1,0:T(8,128)(2,1)S(1)}, u32[]{:S(2)}, u32[]{:S(2)}) collective-permute-start(bf16[136,1088]{1,0:T(8,128)(2,1)S(1)} %get-tuple-element.113), channel_id=1, source_target_pairs={{0,8},{4,12},{8,0},{12,4},{16,24},{20,28},{24,16},{28,20},{1,9},{5... | collective-permute-start | bytes 887816 | tf_op jit(solution)/shard_map/ppermute | solution.py:185
  379.2 15.6 %collective-permute-start.41 = (bf16[136,1088]{1,0:T(8,128)(2,1)S(1)}, bf16[136,1088]{1,0:T(8,128)(2,1)S(1)}, u32[]{:S(2)}, u32[]{:S(2)}) collective-permute-start(bf16[136,1088]{1,0:T(8,128)(2,1)S(1)} %get-tuple-element.114), channel_id=1, source_target_pairs={{0,24},{4,28},{8,16},{12,20},{16,8},{20,12},{24,0},{28,4},{1,25},{... | collective-permute-start | bytes 887816 | tf_op jit(solution)/shard_map/ppermute | solution.py:185
  379.7 16.4 %collective-permute-start.40 = (bf16[136,1088]{1,0:T(8,128)(2,1)S(1)}, bf16[136,1088]{1,0:T(8,128)(2,1)S(1)}, u32[]{:S(2)}, u32[]{:S(2)}) collective-permute-start(bf16[136,1088]{1,0:T(8,128)(2,1)S(1)} %get-tuple-element.115), channel_id=1, source_target_pairs={{0,16},{4,20},{8,24},{12,28},{16,0},{20,4},{24,8},{28,12},{1,17},{... | collective-permute-start | bytes 887816 | tf_op jit(solution)/shard_map/ppermute | solution.py:185
  383.3 22.0 %collective-permute-start.47 = (bf16[72,3456]{1,0:T(8,128)(2,1)S(1)}, bf16[72,3456]{1,0:T(8,128)(2,1)S(1)}, u32[]{:S(2)}, u32[]{:S(2)}) collective-permute-start(bf16[72,3456]{1,0:T(8,128)(2,1)S(1)} %get-tuple-element.105), channel_id=1, source_target_pairs={{0,8},{4,12},{8,0},{12,4},{16,24},{20,28},{24,16},{28,20},{1,9},{5... | collective-permute-start | bytes 1493000 | tf_op jit(solution)/shard_map/ppermute | solution.py:185
  387.9 27.7 %collective-permute-start.49 = (bf16[72,3456]{1,0:T(8,128)(2,1)S(1)}, bf16[72,3456]{1,0:T(8,128)(2,1)S(1)}, u32[]{:S(2)}, u32[]{:S(2)}) collective-permute-start(bf16[72,3456]{1,0:T(8,128)(2,1)S(1)} %get-tuple-element.106), channel_id=1, source_target_pairs={{0,24},{4,28},{8,16},{12,20},{16,8},{20,12},{24,0},{28,4},{1,25},{... | collective-permute-start | bytes 1493000 | tf_op jit(solution)/shard_map/ppermute | solution.py:185
  394.7 23.0 %collective-permute-start.48 = (bf16[72,3456]{1,0:T(8,128)(2,1)S(1)}, bf16[72,3456]{1,0:T(8,128)(2,1)S(1)}, u32[]{:S(2)}, u32[]{:S(2)}) collective-permute-start(bf16[72,3456]{1,0:T(8,128)(2,1)S(1)} %get-tuple-element.107), channel_id=1, source_target_pairs={{0,16},{4,20},{8,24},{12,28},{16,0},{20,4},{24,8},{28,12},{1,17},{... | collective-permute-start | bytes 1493000 | tf_op jit(solution)/shard_map/ppermute | solution.py:185
  423.9 68.0 %reduce-scatter.12.cloned.1.call-start = ((), (), s32[]{:S(2)}) async-start(), calls=%async_computation.10 | async-start | bytes 2785280 | tf_op jit(solution)/shard_map/reduce_scatter | solution.py:277
  429.4 87.3 %reduce-scatter.14.cloned.1.call-start = ((), (), s32[]{:S(2)}) async-start(), calls=%async_computation.11 | async-start | bytes 921600 | tf_op jit(solution)/shard_map/reduce_scatter | solution.py:277
  429.8 11.0 %collective-permute-start.43 = (bf16[1,1632]{1,0:T(2,128)(2,1)S(1)}, bf16[1,1632]{1,0:T(2,128)(2,1)S(1)}, u32[]{:S(2)}, u32[]{:S(2)}) collective-permute-start(bf16[1,1632]{1,0:T(2,128)(2,1)S(1)} %get-tuple-element.150), channel_id=1, source_target_pairs={{0,8},{4,12},{8,0},{12,4},{16,24},{20,28},{24,16},{28,20},{1,9},{5... | collective-permute-start | bytes 9800 | tf_op jit(solution)/shard_map/ppermute | solution.py:185
  431.4 10.1 %collective-permute-start.45 = (bf16[1,1632]{1,0:T(2,128)(2,1)S(1)}, bf16[1,1632]{1,0:T(2,128)(2,1)S(1)}, u32[]{:S(2)}, u32[]{:S(2)}) collective-permute-start(bf16[1,1632]{1,0:T(2,128)(2,1)S(1)} %get-tuple-element.151), channel_id=1, source_target_pairs={{0,24},{4,28},{8,16},{12,20},{16,8},{20,12},{24,0},{28,4},{1,25},{... | collective-permute-start | bytes 9800 | tf_op jit(solution)/shard_map/ppermute | solution.py:185
  432.8 8.7 %collective-permute-start.44 = (bf16[1,1632]{1,0:T(2,128)(2,1)S(1)}, bf16[1,1632]{1,0:T(2,128)(2,1)S(1)}, u32[]{:S(2)}, u32[]{:S(2)}) collective-permute-start(bf16[1,1632]{1,0:T(2,128)(2,1)S(1)} %get-tuple-element.152), channel_id=1, source_target_pairs={{0,16},{4,20},{8,24},{12,28},{16,0},{20,4},{24,8},{28,12},{1,17},{... | collective-permute-start | bytes 9800 | tf_op jit(solution)/shard_map/ppermute | solution.py:185
  438.0 13.2 %collective-permute-start.35 = (bf16[64,3456]{1,0:T(8,128)(2,1)}, bf16[64,3456]{1,0:T(8,128)(2,1)S(1)}, u32[]{:S(2)}, u32[]{:S(2)}) collective-permute-start(bf16[64,3456]{1,0:T(8,128)(2,1)} %get-tuple-element.108), channel_id=1, source_target_pairs={{0,8},{4,12},{8,0},{12,4},{16,24},{20,28},{24,16},{28,20},{1,9},{5... | collective-permute-start | bytes 1327112 | tf_op jit(solution)/shard_map/ppermute | solution.py:185
  439.5 20.9 %collective-permute-start.37 = (bf16[64,3456]{1,0:T(8,128)(2,1)}, bf16[64,3456]{1,0:T(8,128)(2,1)S(1)}, u32[]{:S(2)}, u32[]{:S(2)}) collective-permute-start(bf16[64,3456]{1,0:T(8,128)(2,1)} %get-tuple-element.109), channel_id=1, source_target_pairs={{0,24},{4,28},{8,16},{12,20},{16,8},{20,12},{24,0},{28,4},{1,25},{... | collective-permute-start | bytes 1327112 | tf_op jit(solution)/shard_map/ppermute | solution.py:185
  440.9 20.9 %collective-permute-start.36 = (bf16[64,3456]{1,0:T(8,128)(2,1)}, bf16[64,3456]{1,0:T(8,128)(2,1)}, u32[]{:S(2)}, u32[]{:S(2)}) collective-permute-start(bf16[64,3456]{1,0:T(8,128)(2,1)} %get-tuple-element.110), channel_id=1, source_target_pairs={{0,16},{4,20},{8,24},{12,28},{16,0},{20,4},{24,8},{28,12},{1,17},{... | collective-permute-start | bytes 1327112 | tf_op jit(solution)/shard_map/ppermute | solution.py:185
  (76 other events, 611.5 us)
Sparse Core Ops, SparseCore 0:
  34.3 55.6 all-gather.3
  106.9 46.0 all-gather.5
  165.5 45.8 all-gather.7
  230.9 43.8 reduce-scatter.7
  277.0 44.9 reduce-scatter.9
  424.1 20.9 reduce-scatter.15
  447.4 44.5 reduce-scatter.11
  494.3 22.3 reduce-scatter.13

commit v3 on v2

--- a/solution.py
+++ b/solution.py
@@ -233,16 +233,20 @@
     )(me.reshape(1).astype(jnp.int32), *pieces)
 
 
-def gather_dp(chunks):
+def gather_dp(chunks, after=None):
     n = lax.axis_size("dp")
     if n != 8:
-        return lax.all_gather(jnp.concatenate(chunks, axis=0), "dp", axis=0)
+        full = lax.all_gather(jnp.concatenate(chunks, axis=0), "dp", axis=0)
+        return full if after is None else (full, after)
     pieces = []
     for x in chunks:
         for d in range(n // 2):
             got = swap(x, 2 * d) if d else x
             pieces += [got, swap(got, 1)]
-    return place(lax.axis_index("dp"), pieces, n, sum(x.shape[0] for x in chunks))
+    if after is not None:
+        pieces[-1], after = lax.optimization_barrier((pieces[-1], after))
+    full = place(lax.axis_index("dp"), pieces, n, sum(x.shape[0] for x in chunks))
+    return full if after is None else (full, after)
 
 
 def core_half(grads, mine):
@@ -256,12 +260,21 @@
 
 
 def scatter_dp(grads, send=None):
+    return spread(core_sum(grads, send))
+
+
+def core_sum(grads, send=None):
+    if lax.axis_size("dp") != 8:
+        return jnp.concatenate(grads, axis=2)
+    got = swap(core_half(grads, False) if send is None else send, 1)
+    return (core_half(grads, True).astype(F32) + got.astype(F32)).astype(BF)
+
+
+def spread(summed):
     n = lax.axis_size("dp")
     if n != 8:
-        return lax.psum_scatter(jnp.concatenate(grads, axis=2), "dp", scatter_dimension=0).astype(F32)
+        return lax.psum_scatter(summed, "dp", scatter_dimension=0).astype(F32)
     group = lax.axis_index("dp") // 2
-    got = swap(core_half(grads, False) if send is None else send, 1)
-    summed = (core_half(grads, True).astype(F32) + got.astype(F32)).astype(BF)
     total = lax.dynamic_index_in_dim(summed, group, 0, keepdims=False).astype(F32)
     for d in range(1, n // 2):
         part = lax.dynamic_index_in_dim(summed, group ^ d, 0, keepdims=False)
@@ -342,14 +355,19 @@
     gain1, shift1, bias_q, bias_v, bias_o, gain2, shift2, bias_d = [vectors[i] for i in range(8)]
     up_shift = lax.dynamic_slice_in_dim(up_bias_all, z * ff, ff)
     x_full = gather_z(own_x)
-    cot, _ = lax.optimization_barrier((cotangent[0], x_full))
-    g_full = gather_z(cot)
     raw = jnp.concatenate(raw, axis=1)
     wq_s = pad_cols(raw[:, :width], wide)
     wk_s = pad_cols(raw[:, width : 2 * width], wide)
     wv_s = pad_cols(raw[:, 2 * width :], wide)
     qkv_s = jnp.concatenate([wq_s, pair_up(wk_s, wv_s)], axis=1)
-    qkv_full = gather_dp([qkv_s]).reshape(width, 3 * wide)
+    x_wide = x_full.astype(F32)
+    mean_full = jnp.mean(x_wide, axis=-1, keepdims=True)
+    inv_full = lax.rsqrt(jnp.mean((x_wide - mean_full) * (x_wide - mean_full), axis=-1, keepdims=True) + EPS)
+    qkv_full, (mean_full, inv_full) = gather_dp([qkv_s], (mean_full, inv_full))
+    normed1_full = (x_wide - mean_full) * inv_full
+    qkv_full = qkv_full.reshape(width, 3 * wide)
+    cot, qkv_full = lax.optimization_barrier((cotangent[0], qkv_full))
+    g_full = gather_z(cot)
     out_rows = jnp.concatenate(ring_z(out_weight), axis=1)
     out_rows, up_s, down_s, qkv_full = lax.optimization_barrier((out_rows, up_weight, down_weight, qkv_full))
     wq = qkv_full[:, :wide]
@@ -358,7 +376,6 @@
     x_own = inputs[0].astype(F32)
     normed1, inv1 = ln_stats(x_own)
     attn_own = (normed1 * gain1 + shift1).astype(BF)
-    normed1_full, _ = ln_stats(x_full.astype(F32))
     attn_full = (normed1_full * gain1 + shift1).astype(BF)
     q = (mm(attn_own, wq) + pad_cols(bias_q, wide)).astype(BF)
     bias_kv = pair_up(jnp.zeros((wide,), F32), pad_cols(bias_v, wide))
@@ -408,10 +425,14 @@
     dq, dkv, send_a, send_b = lax.optimization_barrier(
         (dq, dkv, core_half(dw_a, False), core_half(dw_b, False))
     )
-    dw_parts = [scatter_dp(dw_a, send_a), scatter_dp(dw_b, send_b)]
+    sum_a = core_sum(dw_a, send_a)
+    sum_b = core_sum(dw_b, send_b)
     part_kv = mm(dkv, wkv, NT)
+    part_b, part_kv = lax.optimization_barrier((part_kv.astype(BF), part_kv))
     part_q = mm(dq, wq, NT)
-    grad_attn = scatter_z(part_kv.astype(BF))
+    grad_attn = scatter_z(part_b)
+    part_kv, part_q, dq, dkv, sum_a, sum_b = lax.optimization_barrier((part_kv, part_q, dq, dkv, sum_a, sum_b))
+    dw_parts = [spread(sum_a), spread(sum_b)]
 
     dv_sum = pair_split(jnp.sum(dkv.astype(F32), axis=0))[1][:width]
     vec = jnp.stack(

time: 535 us -> 504 us (0.942)
  waiting for transfers between devices: 217 us -> 203 us
  local copies, waits for them, and re-layouts: 58 us -> 46.8 us
  matrix products: 82.6 us -> 74.7 us
    ppermute x48, waiting for transfers between devices: 157 us -> 129 us  [swap(): return lax.ppermute(x, 'dp', [(i, i ^ bit) for i in range(n)])]
    reduce_scatter x4, waiting for transfers between devices: 41 us -> 56.7 us  [scatter_z(): lax.psum_scatter(x, 'seq', scatter_dimension=0, tiled=True).astype(F32)]
    ppermute x6, waiting for transfers between devices: 10.3 us -> 0.02 us  [ring_z(): lax.ppermute(x, 'seq', [(i, (i + d) % size) for i in range(size)])]
    all_gather x3, waiting for transfers between devices: 9.03 us -> 17.3 us  [gather_z(): return lax.all_gather(x, 'seq', axis=0, tiled=True)]
    dot_general x15, matrix products: 82.6 us -> 74.7 us  [mm(): return lax.dot_general(a, b, (dims, ((), ())), preferred_element_type=F32)]
    reduce_sum x0 -> x4, other arithmetic: none -> 7.75 us  [the longest x1 3.32 us: shards(): jnp.sum(part_kv, axis=0) + jnp.sum(part_q, axis=0)]
    unnamed x135 -> x161, local copies, waits for them, and re-layouts: 14.3 us -> 15.7 us
  transfers between devices with their start and end apart: 62 -> 62, of which waited for: 30 -> 31; matrix products, arithmetic and copies ran while one was open for 24% -> 26% of each run, Pallas kernels for 11% -> 11%
where the time goes in v3:
time: 504 us; the launch traced here: 498 us
  waiting for transfers between devices  203 us (40%)
  matrix products  74.7 us (15%)
  Pallas kernels  56.6 us (11%)
  starting transfers between devices  50.1 us (10%)
  other arithmetic  50 us (10%)
  local copies, waits for them, and re-layouts  46.8 us (9%)
  between operations  16.6 us (3%)
    ppermute x48, waiting for transfers between devices, swap(): return lax.ppermute(x, 'dp', [(i, i ^ bit) for i in range(n)])  129 us
    dot_general x15, matrix products, mm(): return lax.dot_general(a, b, (dims, ((), ())), preferred_element_type=F32)  74.7 us
    reduce_scatter x4, waiting for transfers between devices, scatter_z(): lax.psum_scatter(x, 'seq', scatter_dimension=0, tiled=True).astype(F32)  56.7 us
    ppermute x48, starting transfers between devices, swap(): return lax.ppermute(x, 'dp', [(i, i ^ bit) for i in range(n)])  37.5 us
    pallas_call x1, Pallas kernels, attend_back(): pl.pallas_call(attend_back_kernel, grid_spec=pltpu.PrefetchScalarGridSpec...  21.4 us
    pallas_call x1, Pallas kernels, attend(): pl.pallas_call(attend_kernel, grid_spec=pltpu.PrefetchScalarGridSpec(num_...  19.6 us
    all_gather x3, waiting for transfers between devices, gather_z(): return lax.all_gather(x, 'seq', axis=0, tiled=True)  17.3 us
    unnamed x161, local copies, waits for them, and re-layouts  15.7 us
  transfers between devices with their start and end apart: 62, of which 31 were waited for; matrix products, arithmetic and copies ran while one was open for 26% of the time, Pallas kernels for 11%

profile of v3, /device:TPU:0, one launch (start us, length us, event | category | flops | bytes accessed | tf_op | source)
XLA Modules:
  0.0 498.0 jit_solution(175305664871453049)
XLA Ops:
  7.2 4.1 collective-permute-start.1
  19.6 2.5 collective-permute-start.8
  37.4 2.4 collective-permute-start.18
  40.9 2.8 collective-permute-start.11
  43.9 18.4 %collective-permute-done.18.refs_6_ = bf16[136,3456]{1,0:T(8,128)(2,1)} collective-permute-done((bf16[136,3456]{1,0:T(8,128)(2,1)}, bf16[136,3456]{1,0:T(8,128)(2,1)}, u32[]{:S(2)}, u32[]{:S(2)}) %collective-permute-start.18) | collective-permute-done | bytes 940064 | tf_op jit(solution)/shard_map/ppermute | solution.py:185
  62.4 19.3 %collective-permute-done.16.refs_4_ = bf16[136,3456]{1,0:T(8,128)(2,1)} collective-permute-done((bf16[136,3456]{1,0:T(8,128)(2,1)}, bf16[136,3456]{1,0:T(8,128)(2,1)}, u32[]{:S(2)}, u32[]{:S(2)}) %collective-permute-start.16) | collective-permute-done | bytes 940064 | tf_op jit(solution)/shard_map/ppermute | solution.py:185
  82.2 6.5 %all-gather.4.cloned.1.call-done = bf16[1024,1088]{0,1:T(8,128)(2,1)} async-done(((bf16[256,1088]{0,1:T(8,128)(2,1)}), bf16[1024,1088]{0,1:T(8,128)(2,1)}) %all-gather.4.cloned.1.call-update) | async-done | bytes 2228240 | tf_op jit(solution)/shard_map/all_gather | solution.py:286
  88.7 2.1 convert_reduce_fusion
  94.3 6.2 %place.5 = bf16[8,136,3456]{2,1,0:T(8,128)(2,1)} custom-call(s32[1]{0:T(128)} %bitcast.2.meta, bf16[136,3456]{1,0:T(8,128)(2,1)} %pad_maximum_fusion.4.refs_0_, bf16[136,3456]{1,0:T(8,128)(2,1)} %collective-permute-done.13.refs_1_, bf16[136,3456]{1,0:T(8,128)(2,1)} %collective-permute-done.14.refs_2_, bf16[136,3456]{1,0:T(8,128)(2,1)} %collective-permute-done.15.refs_3_, ...), custom_call_target="tpu_custom_call" | custom-call | tf_op jit(solution)/shard_map/place/pallas_call | solution.py:222
  106.2 2.5 collective-permute-start.25
  109.7 10.8 %add_convert_fusion.kv_ref = bf16[1024,2304]{1,0:T(8,128)(2,1)} fusion(f32[2304]{0:T(1024)S(1)} %add.385, bf16[1088,3456]{1,0:T(8,128)(2,1)} %bitcast.211, bf16[1024,1088]{0,1:T(8,128)(2,1)S(1)} %copy-done.1, f32[1088]{0:T(1024)S(1)} %add.376, f32[1088]{0:T(1024)S(1)} %mul.194, f32[1024]{0:T(1024)} %add_rsqrt_fusion, f32[1024]{0:T(1024)} %copy-done.39), kind=kOutput, calls=%fused_computation.1 | convolution fusion | flops 5145231360 | bytes 11986432 | tf_op jit(solution)/shard_map/dot_general | solution.py:19
  123.1 3.7 fusion.17.q_ref
  126.8 19.6 %attend.1 = (bf16[256,1152]{1,0:T(8,128)(2,1)}, f32[9,2,256]{2,1,0:T(2,128)}) custom-call(s32[2]{0:T(128)} %pad_add_fusion.meta, bf16[256,1152]{1,0:T(8,128)(2,1)} %fusion.17.q_ref, bf16[1024,2304]{1,0:T(8,128)(2,1)} %add_convert_fusion.kv_ref), custom_call_target="tpu_custom_call" | custom-call | flops 2415919104 | bytes 7077888 | tf_op jit(solution)/shard_map/attend/pallas_call | solution.py:90
  148.0 3.2 place.6
  151.2 2.9 fusion.114
  159.6 13.7 %collective-permute-done.32.refs_6_ = bf16[136,2176]{1,0:T(8,128)(2,1)S(1)} collective-permute-done((bf16[136,2176]{1,0:T(8,128)(2,1)S(1)}, bf16[136,2176]{1,0:T(8,128)(2,1)S(1)}, u32[]{:S(2)}, u32[]{:S(2)}) %collective-permute-start.32) | collective-permute-done | bytes 591904 | tf_op jit(solution)/shard_map/ppermute | solution.py:185
  173.3 11.8 %collective-permute-done.30.refs_4_ = bf16[136,2176]{1,0:T(8,128)(2,1)S(1)} collective-permute-done((bf16[136,2176]{1,0:T(8,128)(2,1)S(1)}, bf16[136,2176]{1,0:T(8,128)(2,1)S(1)}, u32[]{:S(2)}, u32[]{:S(2)}) %collective-permute-start.30) | collective-permute-done | bytes 591904 | tf_op jit(solution)/shard_map/ppermute | solution.py:185
  188.1 4.7 place.7
  192.7 10.8 %all-gather.8.cloned.1.call-done = bf16[1024,1088]{0,1:T(8,128)(2,1)} async-done(((bf16[256,1088]{0,1:T(8,128)(2,1)}), bf16[1024,1088]{0,1:T(8,128)(2,1)}) %all-gather.8.cloned.1.call-update) | async-done | bytes 2228240 | tf_op jit(solution)/shard_map/all_gather | solution.py:286
  203.5 5.7 %convolution_add_fusion = f32[1024,1088]{0,1:T(8,128)S(1)} fusion(bf16[1024,1088]{0,1:T(8,128)(2,1)} %all-gather.8.cloned.1.call-done, f32[1088]{0:T(1024)S(1)} %dynamic_slice.122, bf16[1088,2176]{1,0:T(8,128)(2,1)} %bitcast.220), kind=kOutput, calls=%fused_computation.13 | convolution fusion | flops 2425421824 | bytes 9195776 | tf_op jit(solution)/shard_map/dot_general | solution.py:19
  209.3 8.0 %fusion.116 = (bf16[1088]{0:T(1024)(128)(2,1)S(1)}, bf16[1024,1088]{0,1:T(8,128)(2,1)S(1)}) fusion(f32[1024,1088]{0,1:T(8,128)S(1)} %convolution_add_fusion, bf16[1088,2176]{1,0:T(8,128)(2,1)S(1)} %bitcast.221, bf16[1024,1088]{0,1:T(8,128)(2,1)S(1)} %copy-done.63, bf16[1024]{0:T(1024)(128)(2,1)S(1)} %copy-done.61), kind=kOutput, calls=%fused_computation.257 | convolution fusion | flops 2447703040 | bytes 11423872 | tf_op jit(solution)/shard_map/dot_general | solution.py:19
  218.7 4.2 convolution_convert_fusion.6
  223.5 5.5 %convolution_convert_fusion.4 = bf16[1088,1088]{1,0:T(8,128)(2,1)S(1)} fusion(bf16[1024,1088]{0,1:T(8,128)(2,1)} %all-gather.8.cloned.1.call-done, bf16[1024,1088]{0,1:T(8,128)(2,1)} %copy-done.66), kind=kOutput, calls=%fused_computation.5 | convolution fusion | flops 2425491456 | bytes 6823936 | tf_op jit(solution)/shard_map/dot_general | solution.py:19
  229.1 5.5 %convolution_convert_fusion.3 = bf16[1088,1088]{1,0:T(8,128)(2,1)S(1)} fusion(bf16[1024,1088]{0,1:T(8,128)(2,1)S(1)} %copy-done.64, bf16[1024]{0:T(1024)(128)(2,1)S(1)} %copy-done.61, f32[1024,1088]{0,1:T(8,128)} %copy-done.65), kind=kOutput, calls=%fused_computation.4 | convolution fusion | flops 2436632576 | bytes 9054208 | tf_op jit(solution)/shard_map/dot_general | solution.py:19
  238.4 5.0 convolution_convert_fusion.5
  244.6 3.1 add_convert_fusion.1
  253.3 13.7 %reduce-scatter.8.cloned.1.call-done = bf16[256,1088]{0,1:T(8,128)(2,1)} async-done(((bf16[1024,1088]{0,1:T(8,128)(2,1)}), bf16[256,1088]{0,1:T(8,128)(2,1)}) %reduce-scatter.8.cloned.1.call-update) | async-done | bytes 557072 | tf_op jit(solution)/shard_map/reduce_scatter | solution.py:290
  267.0 2.4 multiply_reduce_fusion
  269.4 2.4 fusion.110
  275.9 3.5 convolution_convert_fusion.1
  279.4 21.4 %attend_back.1 = (bf16[256,1152]{1,0:T(8,128)(2,1)}, bf16[1024,2304]{1,0:T(8,128)(2,1)}) custom-call(s32[2]{0:T(128)} %pad_add_fusion.meta, bf16[256,1152]{1,0:T(8,128)(2,1)} %fusion.17.q_ref, bf16[1024,2304]{1,0:T(8,128)(2,1)} %add_convert_fusion.kv_ref, f32[9,2,256]{2,1,0:T(2,128)} %get-tuple-element.69.lse_ref, bf16[256,1152]{1,0:T(8,128)(2,1)} %pad.38.g_ref), custom_call_target="tpu_custom_call" | custom-call | flops 6039797760 | bytes 14155776 | tf_op jit(solution)/shard_map/attend_back/pallas_call | solution.py:155
  300.8 13.4 %reduce-scatter.10.cloned.1.call-done = bf16[256,1088]{0,1:T(8,128)(2,1)} async-done(((bf16[1024,1088]{0,1:T(8,128)(2,1)}), bf16[256,1088]{0,1:T(8,128)(2,1)}) %reduce-scatter.10.cloned.1.call-update) | async-done | bytes 557072 | tf_op jit(solution)/shard_map/reduce_scatter | solution.py:290
  315.3 2.3 convolution_convert_fusion.2
  319.3 6.4 %convolution_convert_fusion = bf16[1088,2304]{1,0:T(8,128)(2,1)S(1)} fusion(bf16[1024,2304]{1,0:T(8,128)(2,1)S(1)} %copy-done.10, bf16[1024,1088]{0,1:T(8,128)(2,1)S(1)} %copy-done.2, f32[1088]{0:T(1024)S(1)} %add.376, f32[1088]{0:T(1024)S(1)} %mul.194, f32[1024]{0:T(1024)S(1)} %copy-done.49, f32[1024]{0:T(1024)S(1)} %copy-done.40), kind=kOutput, calls=%fused_computation | convolution fusion | flops 5143019520 | bytes 11977216 | tf_op jit(solution)/shard_map/dot_general | solution.py:19
  331.3 7.3 %fusion.115 = (bf16[1024,1088]{0,1:T(8,128)(2,1)}, f32[1024,1088]{0,1:T(8,128)}) fusion(bf16[1024,2304]{1,0:T(8,128)(2,1)S(1)} %copy-done.10, bf16[1088,3456]{1,0:T(8,128)(2,1)S(1)} %bitcast.215), kind=kOutput, calls=%fused_computation.256 | convolution fusion | flops 5134942208 | bytes 16416768 | tf_op jit(solution)/shard_map/dot_general | solution.py:19
  347.3 4.4 collective-permute-done.40
  353.2 6.2 %collective-permute-done.42 = bf16[136,1088]{1,0:T(8,128)(2,1)S(1)} collective-permute-done((bf16[136,1088]{1,0:T(8,128)(2,1)S(1)}, bf16[136,1088]{1,0:T(8,128)(2,1)S(1)}, u32[]{:S(2)}, u32[]{:S(2)}) %collective-permute-start.42) | collective-permute-done | bytes 295968 | tf_op jit(solution)/shard_map/ppermute | solution.py:185
  363.3 5.9 %collective-permute-done.47 = bf16[72,3456]{1,0:T(8,128)(2,1)S(1)} collective-permute-done((bf16[72,3456]{1,0:T(8,128)(2,1)S(1)}, bf16[72,3456]{1,0:T(8,128)(2,1)S(1)}, u32[]{:S(2)}, u32[]{:S(2)}) %collective-permute-start.47) | collective-permute-done | bytes 497696 | tf_op jit(solution)/shard_map/ppermute | solution.py:185
  370.7 9.3 %collective-permute-done.49 = bf16[72,3456]{1,0:T(8,128)(2,1)S(1)} collective-permute-done((bf16[72,3456]{1,0:T(8,128)(2,1)S(1)}, bf16[72,3456]{1,0:T(8,128)(2,1)S(1)}, u32[]{:S(2)}, u32[]{:S(2)}) %collective-permute-start.49) | collective-permute-done | bytes 497696 | tf_op jit(solution)/shard_map/ppermute | solution.py:185
  380.0 6.6 %collective-permute-done.48 = bf16[72,3456]{1,0:T(8,128)(2,1)S(1)} collective-permute-done((bf16[72,3456]{1,0:T(8,128)(2,1)S(1)}, bf16[72,3456]{1,0:T(8,128)(2,1)S(1)}, u32[]{:S(2)}, u32[]{:S(2)}) %collective-permute-start.48) | collective-permute-done | bytes 497696 | tf_op jit(solution)/shard_map/ppermute | solution.py:185
  392.8 4.2 collective-permute-done.52
  403.1 3.2 reduce.1
  408.2 3.3 fusion.107
  422.1 9.4 %collective-permute-done.36 = bf16[64,3456]{1,0:T(8,128)(2,1)S(1)} collective-permute-done((bf16[64,3456]{1,0:T(8,128)(2,1)S(1)}, bf16[64,3456]{1,0:T(8,128)(2,1)S(1)}, u32[]{:S(2)}, u32[]{:S(2)}) %collective-permute-start.36) | collective-permute-done | bytes 442400 | tf_op jit(solution)/shard_map/ppermute | solution.py:185
  431.5 8.0 %collective-permute-done.38 = bf16[64,3456]{1,0:T(8,128)(2,1)S(1)} collective-permute-done((bf16[64,3456]{1,0:T(8,128)(2,1)S(1)}, bf16[64,3456]{1,0:T(8,128)(2,1)S(1)}, u32[]{:S(2)}, u32[]{:S(2)}) %collective-permute-start.38) | collective-permute-done | bytes 442400 | tf_op jit(solution)/shard_map/ppermute | solution.py:185
  450.6 10.2 %reduce-scatter.12.cloned.1.call-done = bf16[256,1088]{0,1:T(8,128)(2,1)} async-done(((bf16[1024,1088]{0,1:T(8,128)(2,1)}), bf16[256,1088]{0,1:T(8,128)(2,1)}) %reduce-scatter.12.cloned.1.call-update) | async-done | bytes 557072 | tf_op jit(solution)/shard_map/reduce_scatter | solution.py:290
  460.7 2.2 convert_element_type.356
  465.9 19.5 %reduce-scatter.14.cloned.1.call-done = bf16[80,1088]{1,0:T(8,128)(2,1)} async-done(((bf16[320,1088]{1,0:T(8,128)(2,1)}), bf16[80,1088]{1,0:T(8,128)(2,1)}) %reduce-scatter.14.cloned.1.call-update) | async-done | bytes 174096 | tf_op jit(solution)/shard_map/reduce_scatter | solution.py:290
  (424 shorter events, 130.9 us)
Async XLA Ops:
  7.2 81.5 %all-gather.4.cloned.1.call-start = ((), (), s32[]{:S(2)}) async-start(), calls=%async_computation.5 | async-start | bytes 2785280 | tf_op jit(solution)/shard_map/all_gather | solution.py:286
  7.2 25.8 %collective-permute-start.1 = (bf16[136,816]{1,0:T(8,128)(2,1)}, bf16[136,816]{1,0:T(8,128)(2,1)S(1)}, u32[]{:S(2)}, u32[]{:S(2)}) collective-permute-start(bf16[136,816]{1,0:T(8,128)(2,1)} %param.21), channel_id=1, source_target_pairs={{0,2},{1,3},{2,0},{3,1},{4,6},{5,7},{6,4},{7,5},{8,10},{9,11},{10,... | collective-permute-start | bytes 665864 | tf_op jit(solution)/shard_map/ppermute | solution.py:193
  11.4 21.7 %collective-permute-start = (bf16[136,816]{1,0:T(8,128)(2,1)}, bf16[136,816]{1,0:T(8,128)(2,1)S(1)}, u32[]{:S(2)}, u32[]{:S(2)}) collective-permute-start(bf16[136,816]{1,0:T(8,128)(2,1)} %param.21), channel_id=1, source_target_pairs={{0,3},{1,0},{2,1},{3,2},{4,7},{5,4},{6,5},{7,6},{8,11},{9,8},{10,9... | collective-permute-start | bytes 665864 | tf_op jit(solution)/shard_map/ppermute | solution.py:193
  12.7 20.3 %collective-permute-start.2 = (bf16[136,816]{1,0:T(8,128)(2,1)}, bf16[136,816]{1,0:T(8,128)(2,1)S(1)}, u32[]{:S(2)}, u32[]{:S(2)}) collective-permute-start(bf16[136,816]{1,0:T(8,128)(2,1)} %param.21), channel_id=1, source_target_pairs={{0,1},{1,2},{2,3},{3,0},{4,5},{5,6},{6,7},{7,4},{8,9},{9,10},{10,1... | collective-permute-start | bytes 665864 | tf_op jit(solution)/shard_map/ppermute | solution.py:193
  34.1 117.0 %all-gather.6.cloned.1.call-start = ((), (), s32[]{:S(2)}) async-start(), calls=%async_computation.6 | async-start | bytes 2785280 | tf_op jit(solution)/shard_map/all_gather | solution.py:286
  37.4 25.0 %collective-permute-start.18 = (bf16[136,3456]{1,0:T(8,128)(2,1)}, bf16[136,3456]{1,0:T(8,128)(2,1)}, u32[]{:S(2)}, u32[]{:S(2)}) collective-permute-start(bf16[136,3456]{1,0:T(8,128)(2,1)} %pad_maximum_fusion.4.refs_0_), channel_id=1, source_target_pairs={{0,24},{4,28},{8,16},{12,20},{16,8},{20,12},{24,0},{28,4},{1,25},{... | collective-permute-start | bytes 2820104 | tf_op jit(solution)/shard_map/ppermute | solution.py:185
  39.8 41.8 %collective-permute-start.16 = (bf16[136,3456]{1,0:T(8,128)(2,1)}, bf16[136,3456]{1,0:T(8,128)(2,1)}, u32[]{:S(2)}, u32[]{:S(2)}) collective-permute-start(bf16[136,3456]{1,0:T(8,128)(2,1)} %pad_maximum_fusion.4.refs_0_), channel_id=1, source_target_pairs={{0,16},{4,20},{8,24},{12,28},{16,0},{20,4},{24,8},{28,12},{1,17},{... | collective-permute-start | bytes 2820104 | tf_op jit(solution)/shard_map/ppermute | solution.py:185
  40.3 41.4 %collective-permute-start.14 = (bf16[136,3456]{1,0:T(8,128)(2,1)}, bf16[136,3456]{1,0:T(8,128)(2,1)}, u32[]{:S(2)}, u32[]{:S(2)}) collective-permute-start(bf16[136,3456]{1,0:T(8,128)(2,1)} %pad_maximum_fusion.4.refs_0_), channel_id=1, source_target_pairs={{0,8},{4,12},{8,0},{12,4},{16,24},{20,28},{24,16},{28,20},{1,9},{5... | collective-permute-start | bytes 2820104 | tf_op jit(solution)/shard_map/ppermute | solution.py:185
  40.9 61.9 %collective-permute-start.11 = (bf16[136,272]{1,0:T(8,128)(2,1)S(1)}, bf16[136,272]{1,0:T(8,128)(2,1)S(1)}, u32[]{:S(2)}, u32[]{:S(2)}) collective-permute-start(bf16[136,272]{1,0:T(8,128)(2,1)S(1)} %copy-done.32), channel_id=1, source_target_pairs={{0,2},{1,3},{2,0},{3,1},{4,6},{5,7},{6,4},{7,5},{8,10},{9,11},{10,... | collective-permute-start | bytes 221960 | tf_op jit(solution)/shard_map/ppermute | solution.py:193
  43.9 49.1 %collective-permute-start.13 = (bf16[136,3456]{1,0:T(8,128)(2,1)}, bf16[136,3456]{1,0:T(8,128)(2,1)}, u32[]{:S(2)}, u32[]{:S(2)}) collective-permute-start(bf16[136,3456]{1,0:T(8,128)(2,1)} %pad_maximum_fusion.4.refs_0_), channel_id=1, source_target_pairs={{0,4},{4,0},{8,12},{12,8},{16,20},{20,16},{24,28},{28,24},{1,5},{5... | collective-permute-start | bytes 2820104 | tf_op jit(solution)/shard_map/ppermute | solution.py:185
  62.4 29.9 %collective-permute-start.19 = (bf16[136,3456]{1,0:T(8,128)(2,1)}, bf16[136,3456]{1,0:T(8,128)(2,1)}, u32[]{:S(2)}, u32[]{:S(2)}) collective-permute-start(bf16[136,3456]{1,0:T(8,128)(2,1)} %collective-permute-done.18.refs_6_), channel_id=1, source_target_pairs={{0,4},{4,0},{8,12},{12,8},{16,20},{20,16},{24,28},{28,24},{1,5},{5... | collective-permute-start | bytes 2820104 | tf_op jit(solution)/shard_map/ppermute | solution.py:185
  81.7 12.6 %collective-permute-start.17 = (bf16[136,3456]{1,0:T(8,128)(2,1)}, bf16[136,3456]{1,0:T(8,128)(2,1)}, u32[]{:S(2)}, u32[]{:S(2)}) collective-permute-start(bf16[136,3456]{1,0:T(8,128)(2,1)} %collective-permute-done.16.refs_4_), channel_id=1, source_target_pairs={{0,4},{4,0},{8,12},{12,8},{16,20},{20,16},{24,28},{28,24},{1,5},{5... | collective-permute-start | bytes 2820104 | tf_op jit(solution)/shard_map/ppermute | solution.py:185
  81.8 12.5 %collective-permute-start.15 = (bf16[136,3456]{1,0:T(8,128)(2,1)}, bf16[136,3456]{1,0:T(8,128)(2,1)}, u32[]{:S(2)}, u32[]{:S(2)}) collective-permute-start(bf16[136,3456]{1,0:T(8,128)(2,1)} %collective-permute-done.14.refs_2_), channel_id=1, source_target_pairs={{0,4},{4,0},{8,12},{12,8},{16,20},{20,16},{24,28},{28,24},{1,5},{5... | collective-permute-start | bytes 2820104 | tf_op jit(solution)/shard_map/ppermute | solution.py:185
  92.2 10.5 %collective-permute-start.10 = (bf16[136,272]{1,0:T(8,128)(2,1)S(1)}, bf16[136,272]{1,0:T(8,128)(2,1)S(1)}, u32[]{:S(2)}, u32[]{:S(2)}) collective-permute-start(bf16[136,272]{1,0:T(8,128)(2,1)S(1)} %copy-done.32), channel_id=1, source_target_pairs={{0,3},{1,0},{2,1},{3,2},{4,7},{5,4},{6,5},{7,6},{8,11},{9,8},{10,9... | collective-permute-start | bytes 221960 | tf_op jit(solution)/shard_map/ppermute | solution.py:193
  92.9 10.5 %collective-permute-start.12 = (bf16[136,272]{1,0:T(8,128)(2,1)S(1)}, bf16[136,272]{1,0:T(8,128)(2,1)}, u32[]{:S(2)}, u32[]{:S(2)}) collective-permute-start(bf16[136,272]{1,0:T(8,128)(2,1)S(1)} %copy-done.32), channel_id=1, source_target_pairs={{0,1},{1,2},{2,3},{3,0},{4,5},{5,6},{6,7},{7,4},{8,9},{9,10},{10,1... | collective-permute-start | bytes 221960 | tf_op jit(solution)/shard_map/ppermute | solution.py:193
  100.5 103.0 %all-gather.8.cloned.1.call-start = ((), (), s32[]{:S(2)}) async-start(), calls=%async_computation.7 | async-start | bytes 2785280 | tf_op jit(solution)/shard_map/all_gather | solution.py:286
  106.2 14.4 %collective-permute-start.25 = (bf16[136,1088]{1,0:T(8,128)(2,1)S(1)}, bf16[136,1088]{1,0:T(8,128)(2,1)S(1)}, u32[]{:S(2)}, u32[]{:S(2)}) collective-permute-start(bf16[136,1088]{1,0:T(8,128)(2,1)S(1)} %concatenate.105.refs_0_), channel_id=1, source_target_pairs={{0,24},{4,28},{8,16},{12,20},{16,8},{20,12},{24,0},{28,4},{1,25},{... | collective-permute-start | bytes 887816 | tf_op jit(solution)/shard_map/ppermute | solution.py:185
  108.7 13.8 %collective-permute-start.23 = (bf16[136,1088]{1,0:T(8,128)(2,1)S(1)}, bf16[136,1088]{1,0:T(8,128)(2,1)}, u32[]{:S(2)}, u32[]{:S(2)}) collective-permute-start(bf16[136,1088]{1,0:T(8,128)(2,1)S(1)} %concatenate.105.refs_0_), channel_id=1, source_target_pairs={{0,16},{4,20},{8,24},{12,28},{16,0},{20,4},{24,8},{28,12},{1,17},{... | collective-permute-start | bytes 887816 | tf_op jit(solution)/shard_map/ppermute | solution.py:185
  109.2 13.4 %collective-permute-start.21 = (bf16[136,1088]{1,0:T(8,128)(2,1)S(1)}, bf16[136,1088]{1,0:T(8,128)(2,1)}, u32[]{:S(2)}, u32[]{:S(2)}) collective-permute-start(bf16[136,1088]{1,0:T(8,128)(2,1)S(1)} %concatenate.105.refs_0_), channel_id=1, source_target_pairs={{0,8},{4,12},{8,0},{12,4},{16,24},{20,28},{24,16},{28,20},{1,9},{5... | collective-permute-start | bytes 887816 | tf_op jit(solution)/shard_map/ppermute | solution.py:185
  109.7 36.7 %collective-permute-start.20 = (bf16[136,1088]{1,0:T(8,128)(2,1)S(1)}, bf16[136,1088]{1,0:T(8,128)(2,1)}, u32[]{:S(2)}, u32[]{:S(2)}) collective-permute-start(bf16[136,1088]{1,0:T(8,128)(2,1)S(1)} %concatenate.105.refs_0_), channel_id=1, source_target_pairs={{0,4},{4,0},{8,12},{12,8},{16,20},{20,16},{24,28},{28,24},{1,5},{5... | collective-permute-start | bytes 887816 | tf_op jit(solution)/shard_map/ppermute | solution.py:185
  120.6 25.8 %collective-permute-start.26 = (bf16[136,1088]{1,0:T(8,128)(2,1)S(1)}, bf16[136,1088]{1,0:T(8,128)(2,1)S(1)}, u32[]{:S(2)}, u32[]{:S(2)}) collective-permute-start(bf16[136,1088]{1,0:T(8,128)(2,1)S(1)} %collective-permute-done.25.refs_6_), channel_id=1, source_target_pairs={{0,4},{4,0},{8,12},{12,8},{16,20},{20,16},{24,28},{28,24},{1,5},{5... | collective-permute-start | bytes 887816 | tf_op jit(solution)/shard_map/ppermute | solution.py:185
  122.5 23.9 %collective-permute-start.24 = (bf16[136,1088]{1,0:T(8,128)(2,1)}, bf16[136,1088]{1,0:T(8,128)(2,1)S(1)}, u32[]{:S(2)}, u32[]{:S(2)}) collective-permute-start(bf16[136,1088]{1,0:T(8,128)(2,1)} %collective-permute-done.23.refs_4_), channel_id=1, source_target_pairs={{0,4},{4,0},{8,12},{12,8},{16,20},{20,16},{24,28},{28,24},{1,5},{5... | collective-permute-start | bytes 887816 | tf_op jit(solution)/shard_map/ppermute | solution.py:185
  122.7 23.8 %collective-permute-start.22 = (bf16[136,1088]{1,0:T(8,128)(2,1)}, bf16[136,1088]{1,0:T(8,128)(2,1)S(1)}, u32[]{:S(2)}, u32[]{:S(2)}) collective-permute-start(bf16[136,1088]{1,0:T(8,128)(2,1)} %collective-permute-done.21.refs_2_), channel_id=1, source_target_pairs={{0,4},{4,0},{8,12},{12,8},{16,20},{20,16},{24,28},{28,24},{1,5},{5... | collective-permute-start | bytes 887816 | tf_op jit(solution)/shard_map/ppermute | solution.py:185
  155.6 111.5 %reduce-scatter.8.cloned.1.call-start = ((), (), s32[]{:S(2)}) async-start(), calls=%async_computation.8 | async-start | bytes 2785280 | tf_op jit(solution)/shard_map/reduce_scatter | solution.py:290
  156.0 17.3 %collective-permute-start.32 = (bf16[136,2176]{1,0:T(8,128)(2,1)S(1)}, bf16[136,2176]{1,0:T(8,128)(2,1)S(1)}, u32[]{:S(2)}, u32[]{:S(2)}) collective-permute-start(bf16[136,2176]{1,0:T(8,128)(2,1)S(1)} %pad_maximum_fusion.7.refs_0_), channel_id=1, source_target_pairs={{0,24},{4,28},{8,16},{12,20},{16,8},{20,12},{24,0},{28,4},{1,25},{... | collective-permute-start | bytes 1775624 | tf_op jit(solution)/shard_map/ppermute | solution.py:185
  157.8 27.2 %collective-permute-start.30 = (bf16[136,2176]{1,0:T(8,128)(2,1)S(1)}, bf16[136,2176]{1,0:T(8,128)(2,1)S(1)}, u32[]{:S(2)}, u32[]{:S(2)}) collective-permute-start(bf16[136,2176]{1,0:T(8,128)(2,1)S(1)} %pad_maximum_fusion.7.refs_0_), channel_id=1, source_target_pairs={{0,16},{4,20},{8,24},{12,28},{16,0},{20,4},{24,8},{28,12},{1,17},{... | collective-permute-start | bytes 1775624 | tf_op jit(solution)/shard_map/ppermute | solution.py:185
  159.0 26.2 %collective-permute-start.28 = (bf16[136,2176]{1,0:T(8,128)(2,1)S(1)}, bf16[136,2176]{1,0:T(8,128)(2,1)}, u32[]{:S(2)}, u32[]{:S(2)}) collective-permute-start(bf16[136,2176]{1,0:T(8,128)(2,1)S(1)} %pad_maximum_fusion.7.refs_0_), channel_id=1, source_target_pairs={{0,8},{4,12},{8,0},{12,4},{16,24},{20,28},{24,16},{28,20},{1,9},{5... | collective-permute-start | bytes 1775624 | tf_op jit(solution)/shard_map/ppermute | solution.py:185
  159.6 26.8 %collective-permute-start.27 = (bf16[136,2176]{1,0:T(8,128)(2,1)S(1)}, bf16[136,2176]{1,0:T(8,128)(2,1)}, u32[]{:S(2)}, u32[]{:S(2)}) collective-permute-start(bf16[136,2176]{1,0:T(8,128)(2,1)S(1)} %pad_maximum_fusion.7.refs_0_), channel_id=1, source_target_pairs={{0,4},{4,0},{8,12},{12,8},{16,20},{20,16},{24,28},{28,24},{1,5},{5... | collective-permute-start | bytes 1775624 | tf_op jit(solution)/shard_map/ppermute | solution.py:185
  173.3 13.1 %collective-permute-start.33 = (bf16[136,2176]{1,0:T(8,128)(2,1)S(1)}, bf16[136,2176]{1,0:T(8,128)(2,1)}, u32[]{:S(2)}, u32[]{:S(2)}) collective-permute-start(bf16[136,2176]{1,0:T(8,128)(2,1)S(1)} %collective-permute-done.32.refs_6_), channel_id=1, source_target_pairs={{0,4},{4,0},{8,12},{12,8},{16,20},{20,16},{24,28},{28,24},{1,5},{5... | collective-permute-start | bytes 1775624 | tf_op jit(solution)/shard_map/ppermute | solution.py:185
  223.0 91.2 %reduce-scatter.10.cloned.1.call-start = ((), (), s32[]{:S(2)}) async-start(), calls=%async_computation.9 | async-start | bytes 2785280 | tf_op jit(solution)/shard_map/reduce_scatter | solution.py:290
  243.4 206.2 %reduce-scatter.16.cloned.1.call-start = ((), (), s32[]{:S(2)}) async-start(), calls=%async_computation.12 | async-start | bytes 829440
  250.4 142.4 %collective-permute-start.51 = (bf16[136,2176]{1,0:T(8,128)(2,1)}, bf16[136,2176]{1,0:T(8,128)(2,1)}, u32[]{:S(2)}, u32[]{:S(2)}) collective-permute-start(bf16[136,2176]{1,0:T(8,128)(2,1)} %get-tuple-element.123), channel_id=1, source_target_pairs={{0,8},{4,12},{8,0},{12,4},{16,24},{20,28},{24,16},{28,20},{1,9},{5... | collective-permute-start | bytes 1775624 | tf_op jit(solution)/shard_map/ppermute | solution.py:185
  251.9 140.9 %collective-permute-start.53 = (bf16[136,2176]{1,0:T(8,128)(2,1)}, bf16[136,2176]{1,0:T(8,128)(2,1)}, u32[]{:S(2)}, u32[]{:S(2)}) collective-permute-start(bf16[136,2176]{1,0:T(8,128)(2,1)} %get-tuple-element.124), channel_id=1, source_target_pairs={{0,24},{4,28},{8,16},{12,20},{16,8},{20,12},{24,0},{28,4},{1,25},{... | collective-permute-start | bytes 1775624 | tf_op jit(solution)/shard_map/ppermute | solution.py:185
  327.7 13.3 %collective-permute-start.39 = (bf16[4,136,1088]{2,1,0:T(8,128)(2,1)S(1)}, bf16[4,136,1088]{2,1,0:T(8,128)(2,1)S(1)}, u32[]{:S(2)}, u32[]{:S(2)}) collective-permute-start(bf16[4,136,1088]{2,1,0:T(8,128)(2,1)S(1)} %dynamic-slice_bitcast_fusion.6), channel_id=1, source_target_pairs={{0,4},{4,0},{8,12},{12,8},{16,20},{20,16},{24,28},{28,24},{1,5},{5... | collective-permute-start | bytes 3551240 | tf_op jit(solution)/shard_map/ppermute | solution.py:185
  328.7 14.2 %collective-permute-start.35 = (bf16[4,64,3456]{2,1,0:T(8,128)(2,1)S(1)}, bf16[4,64,3456]{2,1,0:T(8,128)(2,1)S(1)}, u32[]{:S(2)}, u32[]{:S(2)}) collective-permute-start(bf16[4,64,3456]{2,1,0:T(8,128)(2,1)S(1)} %pad_maximum_fusion.2), channel_id=1, source_target_pairs={{0,4},{4,0},{8,12},{12,8},{16,20},{20,16},{24,28},{28,24},{1,5},{5... | collective-permute-start | bytes 5308424 | tf_op jit(solution)/shard_map/ppermute | solution.py:185
  338.6 7.5 %collective-permute-start.34 = (bf16[4,72,3456]{2,1,0:T(8,128)(2,1)S(1)}, bf16[4,72,3456]{2,1,0:T(8,128)(2,1)S(1)}, u32[]{:S(2)}, u32[]{:S(2)}) collective-permute-start(bf16[4,72,3456]{2,1,0:T(8,128)(2,1)S(1)} %pad_maximum_fusion.1), channel_id=1, source_target_pairs={{0,4},{4,0},{8,12},{12,8},{16,20},{20,16},{24,28},{28,24},{1,5},{5... | collective-permute-start | bytes 5971976 | tf_op jit(solution)/shard_map/ppermute | solution.py:185
  341.4 10.3 %collective-permute-start.40 = (bf16[136,1088]{1,0:T(8,128)(2,1)S(1)}, bf16[136,1088]{1,0:T(8,128)(2,1)S(1)}, u32[]{:S(2)}, u32[]{:S(2)}) collective-permute-start(bf16[136,1088]{1,0:T(8,128)(2,1)S(1)} %get-tuple-element.136), channel_id=1, source_target_pairs={{0,8},{4,12},{8,0},{12,4},{16,24},{20,28},{24,16},{28,20},{1,9},{5... | collective-permute-start | bytes 887816 | tf_op jit(solution)/shard_map/ppermute | solution.py:185
  343.0 16.4 %collective-permute-start.42 = (bf16[136,1088]{1,0:T(8,128)(2,1)S(1)}, bf16[136,1088]{1,0:T(8,128)(2,1)S(1)}, u32[]{:S(2)}, u32[]{:S(2)}) collective-permute-start(bf16[136,1088]{1,0:T(8,128)(2,1)S(1)} %get-tuple-element.137), channel_id=1, source_target_pairs={{0,24},{4,28},{8,16},{12,20},{16,8},{20,12},{24,0},{28,4},{1,25},{... | collective-permute-start | bytes 887816 | tf_op jit(solution)/shard_map/ppermute | solution.py:185
  346.1 15.6 %collective-permute-start.41 = (bf16[136,1088]{1,0:T(8,128)(2,1)S(1)}, bf16[136,1088]{1,0:T(8,128)(2,1)S(1)}, u32[]{:S(2)}, u32[]{:S(2)}) collective-permute-start(bf16[136,1088]{1,0:T(8,128)(2,1)S(1)} %get-tuple-element.138), channel_id=1, source_target_pairs={{0,16},{4,20},{8,24},{12,28},{16,0},{20,4},{24,8},{28,12},{1,17},{... | collective-permute-start | bytes 887816 | tf_op jit(solution)/shard_map/ppermute | solution.py:185
  351.8 17.4 %collective-permute-start.47 = (bf16[72,3456]{1,0:T(8,128)(2,1)S(1)}, bf16[72,3456]{1,0:T(8,128)(2,1)S(1)}, u32[]{:S(2)}, u32[]{:S(2)}) collective-permute-start(bf16[72,3456]{1,0:T(8,128)(2,1)S(1)} %get-tuple-element.128), channel_id=1, source_target_pairs={{0,8},{4,12},{8,0},{12,4},{16,24},{20,28},{24,16},{28,20},{1,9},{5... | collective-permute-start | bytes 1493000 | tf_op jit(solution)/shard_map/ppermute | solution.py:185
  359.4 20.5 %collective-permute-start.49 = (bf16[72,3456]{1,0:T(8,128)(2,1)S(1)}, bf16[72,3456]{1,0:T(8,128)(2,1)S(1)}, u32[]{:S(2)}, u32[]{:S(2)}) collective-permute-start(bf16[72,3456]{1,0:T(8,128)(2,1)S(1)} %get-tuple-element.129), channel_id=1, source_target_pairs={{0,24},{4,28},{8,16},{12,20},{16,8},{20,12},{24,0},{28,4},{1,25},{... | collective-permute-start | bytes 1493000 | tf_op jit(solution)/shard_map/ppermute | solution.py:185
  361.7 24.9 %collective-permute-start.48 = (bf16[72,3456]{1,0:T(8,128)(2,1)S(1)}, bf16[72,3456]{1,0:T(8,128)(2,1)S(1)}, u32[]{:S(2)}, u32[]{:S(2)}) collective-permute-start(bf16[72,3456]{1,0:T(8,128)(2,1)S(1)} %get-tuple-element.130), channel_id=1, source_target_pairs={{0,16},{4,20},{8,24},{12,28},{16,0},{20,4},{24,8},{28,12},{1,17},{... | collective-permute-start | bytes 1493000 | tf_op jit(solution)/shard_map/ppermute | solution.py:185
  369.2 27.8 %collective-permute-start.52 = (bf16[136,2176]{1,0:T(8,128)(2,1)}, bf16[136,2176]{1,0:T(8,128)(2,1)}, u32[]{:S(2)}, u32[]{:S(2)}) collective-permute-start(bf16[136,2176]{1,0:T(8,128)(2,1)} %get-tuple-element.125), channel_id=1, source_target_pairs={{0,16},{4,20},{8,24},{12,28},{16,0},{20,4},{24,8},{28,12},{1,17},{... | collective-permute-start | bytes 1775624 | tf_op jit(solution)/shard_map/ppermute | solution.py:185
  392.7 68.0 %reduce-scatter.12.cloned.1.call-start = ((), (), s32[]{:S(2)}) async-start(), calls=%async_computation.10 | async-start | bytes 2785280 | tf_op jit(solution)/shard_map/reduce_scatter | solution.py:290
  401.9 83.5 %reduce-scatter.14.cloned.1.call-start = ((), (), s32[]{:S(2)}) async-start(), calls=%async_computation.11 | async-start | bytes 921600 | tf_op jit(solution)/shard_map/reduce_scatter | solution.py:290
  418.4 13.1 %collective-permute-start.36 = (bf16[64,3456]{1,0:T(8,128)(2,1)S(1)}, bf16[64,3456]{1,0:T(8,128)(2,1)S(1)}, u32[]{:S(2)}, u32[]{:S(2)}) collective-permute-start(bf16[64,3456]{1,0:T(8,128)(2,1)S(1)} %get-tuple-element.131), channel_id=1, source_target_pairs={{0,8},{4,12},{8,0},{12,4},{16,24},{20,28},{24,16},{28,20},{1,9},{5... | collective-permute-start | bytes 1327112 | tf_op jit(solution)/shard_map/ppermute | solution.py:185
  420.0 19.6 %collective-permute-start.38 = (bf16[64,3456]{1,0:T(8,128)(2,1)S(1)}, bf16[64,3456]{1,0:T(8,128)(2,1)S(1)}, u32[]{:S(2)}, u32[]{:S(2)}) collective-permute-start(bf16[64,3456]{1,0:T(8,128)(2,1)S(1)} %get-tuple-element.132), channel_id=1, source_target_pairs={{0,24},{4,28},{8,16},{12,20},{16,8},{20,12},{24,0},{28,4},{1,25},{... | collective-permute-start | bytes 1327112 | tf_op jit(solution)/shard_map/ppermute | solution.py:185
  420.6 20.3 %collective-permute-start.37 = (bf16[64,3456]{1,0:T(8,128)(2,1)S(1)}, bf16[64,3456]{1,0:T(8,128)(2,1)S(1)}, u32[]{:S(2)}, u32[]{:S(2)}) collective-permute-start(bf16[64,3456]{1,0:T(8,128)(2,1)S(1)} %get-tuple-element.133), channel_id=1, source_target_pairs={{0,16},{4,20},{8,24},{12,28},{16,0},{20,4},{24,8},{28,12},{1,17},{... | collective-permute-start | bytes 1327112 | tf_op jit(solution)/shard_map/ppermute | solution.py:185
  (89 other events, 763.8 us)
Sparse Core Ops, SparseCore 0:
  34.3 54.3 all-gather.3
  100.6 48.5 all-gather.5
  155.7 47.8 all-gather.7
  223.1 43.8 reduce-scatter.7
  269.2 44.9 reduce-scatter.9
  392.9 20.9 reduce-scatter.15
  416.2 44.4 reduce-scatter.11
  463.0 22.3 reduce-scatter.13

commit v4 on v2

--- a/solution.py
+++ b/solution.py
@@ -233,16 +233,21 @@
     )(me.reshape(1).astype(jnp.int32), *pieces)
 
 
-def gather_dp(chunks):
+def gather_dp(chunks, value=None, work=None):
     n = lax.axis_size("dp")
     if n != 8:
-        return lax.all_gather(jnp.concatenate(chunks, axis=0), "dp", axis=0)
+        full = lax.all_gather(jnp.concatenate(chunks, axis=0), "dp", axis=0)
+        return full if work is None else (full, work(value))
     pieces = []
     for x in chunks:
         for d in range(n // 2):
             got = swap(x, 2 * d) if d else x
             pieces += [got, swap(got, 1)]
-    return place(lax.axis_index("dp"), pieces, n, sum(x.shape[0] for x in chunks))
+    if work is not None:
+        pieces[2], pieces[4], pieces[6], value = lax.optimization_barrier((pieces[2], pieces[4], pieces[6], value))
+        pieces[-1], done = lax.optimization_barrier((pieces[-1], work(value)))
+    full = place(lax.axis_index("dp"), pieces, n, sum(x.shape[0] for x in chunks))
+    return full if work is None else (full, done)
 
 
 def core_half(grads, mine):
@@ -342,31 +347,37 @@
     gain1, shift1, bias_q, bias_v, bias_o, gain2, shift2, bias_d = [vectors[i] for i in range(8)]
     up_shift = lax.dynamic_slice_in_dim(up_bias_all, z * ff, ff)
     x_full = gather_z(own_x)
-    cot, _ = lax.optimization_barrier((cotangent[0], x_full))
-    g_full = gather_z(cot)
     raw = jnp.concatenate(raw, axis=1)
     wq_s = pad_cols(raw[:, :width], wide)
     wk_s = pad_cols(raw[:, width : 2 * width], wide)
     wv_s = pad_cols(raw[:, 2 * width :], wide)
     qkv_s = jnp.concatenate([wq_s, pair_up(wk_s, wv_s)], axis=1)
-    qkv_full = gather_dp([qkv_s]).reshape(width, 3 * wide)
+
+    def row_stats(x):
+        x_wide = x.astype(F32)
+        mean = jnp.mean(x_wide, axis=-1, keepdims=True)
+        inv = lax.rsqrt(jnp.mean((x_wide - mean) * (x_wide - mean), axis=-1, keepdims=True) + EPS)
+        return x, mean, inv
+
+    qkv_full, (x_full, mean_full, inv_full) = gather_dp([qkv_s], x_full, row_stats)
+    cot, x_full = lax.optimization_barrier((cotangent[0], x_full))
+    g_full = gather_z(cot)
+    x_wide = x_full.astype(F32)
+    normed1_full = (x_wide - mean_full) * inv_full
+    qkv_full = qkv_full.reshape(width, 3 * wide)
     out_rows = jnp.concatenate(ring_z(out_weight), axis=1)
-    out_rows, up_s, down_s, qkv_full = lax.optimization_barrier((out_rows, up_weight, down_weight, qkv_full))
+    out_rows, qkv_full = lax.optimization_barrier((out_rows, qkv_full))
     wq = qkv_full[:, :wide]
     wkv = qkv_full[:, wide:]
 
     x_own = inputs[0].astype(F32)
     normed1, inv1 = ln_stats(x_own)
     attn_own = (normed1 * gain1 + shift1).astype(BF)
-    normed1_full, _ = ln_stats(x_full.astype(F32))
     attn_full = (normed1_full * gain1 + shift1).astype(BF)
     q = (mm(attn_own, wq) + pad_cols(bias_q, wide)).astype(BF)
     bias_kv = pair_up(jnp.zeros((wide,), F32), pad_cols(bias_v, wide))
     kv = (mm(attn_full, wkv) + bias_kv).astype(BF)
     wo = gather_dp([out_rows]).reshape(width, width)
-    mlp_w = gather_dp([jnp.concatenate([up_s, down_s.T], axis=1)]).reshape(width, 2 * ff)
-    up_full = mlp_w[:, :ff]
-    down_t = mlp_w[:, ff:]
     ctx, lse = attend(meta, q, kv)
     ctx, g_full = lax.optimization_barrier((ctx, g_full))
     ctx = ctx[:, :width]
@@ -374,6 +385,10 @@
     normed2, inv2 = ln_stats(resid)
     mlp_in = (normed2 * gain2 + shift2).astype(BF)
     mlp_full = gather_z(mlp_in)
+    up_s, down_s, resid = lax.optimization_barrier((up_weight, down_weight, resid))
+    mlp_w = gather_dp([jnp.concatenate([up_s, down_s.T], axis=1)]).reshape(width, 2 * ff)
+    up_full = mlp_w[:, :ff]
+    down_t = mlp_w[:, ff:]
     pre = mm(mlp_full, up_full) + up_shift
     act, slope = gelu_parts(pre)
     hidden = act.astype(BF)

time: 535 us -> 524 us (0.979)
  waiting for transfers between devices: 217 us -> 210 us
    all_gather x3, waiting for transfers between devices: 9.03 us -> 19.9 us  [gather_z(): return lax.all_gather(x, 'seq', axis=0, tiled=True)]
    ppermute x6, waiting for transfers between devices: 10.3 us -> 0.02 us  [ring_z(): lax.ppermute(x, 'seq', [(i, (i + d) % size) for i in range(size)])]
    ppermute x48, waiting for transfers between devices: 157 us -> 148 us  [swap(): return lax.ppermute(x, 'dp', [(i, i ^ bit) for i in range(n)])]
    unnamed x135 -> x165, local copies, waits for them, and re-layouts: 14.3 us -> 14.7 us
  transfers between devices with their start and end apart: 62 -> 62, of which waited for: 30 -> 32; matrix products, arithmetic and copies ran while one was open for 24% -> 24% of each run, Pallas kernels for 11% -> 11%
where the time goes in v4:
time: 524 us; the launch traced here: 518 us
  waiting for transfers between devices  210 us (40%)
  matrix products  80.5 us (15%)
  Pallas kernels  56.9 us (11%)
  local copies, waits for them, and re-layouts  53.1 us (10%)
  other arithmetic  52 us (10%)
  starting transfers between devices  49 us (9%)
  between operations  16.5 us (3%)
    ppermute x48, waiting for transfers between devices, swap(): return lax.ppermute(x, 'dp', [(i, i ^ bit) for i in range(n)])  148 us
    dot_general x15, matrix products, mm(): return lax.dot_general(a, b, (dims, ((), ())), preferred_element_type=F32)  80.5 us
    reduce_scatter x4, waiting for transfers between devices, scatter_z(): lax.psum_scatter(x, 'seq', scatter_dimension=0, tiled=True).astype(F32)  42.5 us
    ppermute x48, starting transfers between devices, swap(): return lax.ppermute(x, 'dp', [(i, i ^ bit) for i in range(n)])  35.9 us
    pallas_call x1, Pallas kernels, attend_back(): pl.pallas_call(attend_back_kernel, grid_spec=pltpu.PrefetchScalarGridSpec...  21.6 us
    all_gather x3, waiting for transfers between devices, gather_z(): return lax.all_gather(x, 'seq', axis=0, tiled=True)  19.9 us
    pallas_call x1, Pallas kernels, attend(): pl.pallas_call(attend_kernel, grid_spec=pltpu.PrefetchScalarGridSpec(num_...  19.6 us
    pallas_call x4, Pallas kernels, place(): pl.pallas_call(place_kernel, grid_spec=pltpu.PrefetchScalarGridSpec(num_s...  15.7 us
  transfers between devices with their start and end apart: 62, of which 32 were waited for; matrix products, arithmetic and copies ran while one was open for 24% of the time, Pallas kernels for 11%

profile of v4, /device:TPU:0, one launch (start us, length us, event | category | flops | bytes accessed | tf_op | source)
XLA Modules:
  0.0 518.0 jit_solution(3261067866291792828)
XLA Ops:
  7.2 4.1 collective-permute-start.1
  19.6 2.5 collective-permute-start.8
  36.5 2.5 collective-permute-start.16
  40.0 2.8 collective-permute-start.11
  44.1 17.2 %collective-permute-done.16.refs_6_ = bf16[136,3456]{1,0:T(8,128)(2,1)} collective-permute-done((bf16[136,3456]{1,0:T(8,128)(2,1)S(1)}, bf16[136,3456]{1,0:T(8,128)(2,1)}, u32[]{:S(2)}, u32[]{:S(2)}) %collective-permute-start.16) | collective-permute-done | bytes 940064 | tf_op jit(solution)/shard_map/ppermute | solution.py:185
  62.9 17.6 %collective-permute-done.15.refs_4_ = bf16[136,3456]{1,0:T(8,128)(2,1)S(1)} collective-permute-done((bf16[136,3456]{1,0:T(8,128)(2,1)S(1)}, bf16[136,3456]{1,0:T(8,128)(2,1)S(1)}, u32[]{:S(2)}, u32[]{:S(2)}) %collective-permute-start.15) | collective-permute-done | bytes 940064 | tf_op jit(solution)/shard_map/ppermute | solution.py:185
  81.7 9.8 %all-gather.4.cloned.1.call-done = bf16[1024,1088]{0,1:T(8,128)(2,1)} async-done(((bf16[256,1088]{0,1:T(8,128)(2,1)}), bf16[1024,1088]{0,1:T(8,128)(2,1)}) %all-gather.4.cloned.1.call-update) | async-done | bytes 2228240 | tf_op jit(solution)/shard_map/all_gather | solution.py:278
  91.4 2.1 convert_reduce_fusion
  102.3 6.3 %place.5 = bf16[8,136,3456]{2,1,0:T(8,128)(2,1)} custom-call(s32[1]{0:T(128)} %bitcast.2.meta, bf16[136,3456]{1,0:T(8,128)(2,1)} %copy-done.11, bf16[136,3456]{1,0:T(8,128)(2,1)} %collective-permute-done.13.refs_1_, bf16[136,3456]{1,0:T(8,128)(2,1)} %collective-permute-done.14.refs_2_, bf16[136,3456]{1,0:T(8,128)(2,1)} %collective-permute-done.17.refs_3_, ...), custom_call_target="tpu_custom_call" | custom-call | tf_op jit(solution)/shard_map/place/pallas_call | solution.py:222
  108.6 2.6 collective-permute-start.25
  112.2 10.8 %add_convert_fusion.kv_ref = bf16[1024,2304]{1,0:T(8,128)(2,1)} fusion(f32[2304]{0:T(1024)S(1)} %add.385, bf16[1088,3456]{1,0:T(8,128)(2,1)} %bitcast.211, bf16[1024,1088]{0,1:T(8,128)(2,1)S(1)} %copy-done.3, f32[1088]{0:T(1024)S(1)} %add.376, f32[1088]{0:T(1024)S(1)} %mul.194, f32[1024]{0:T(1024)S(1)} %copy-done.65, f32[1024]{0:T(1024)S(1)} %copy-done.49), kind=kOutput, calls=%fused_computation.1 | convolution fusion | flops 5145231360 | bytes 11986432 | tf_op jit(solution)/shard_map/dot_general | solution.py:19
  123.5 2.4 collective-permute-done.23.refs_4_
  126.4 3.8 fusion.11.q_ref
  130.2 19.6 %attend.1 = (bf16[256,1152]{1,0:T(8,128)(2,1)}, f32[9,2,256]{2,1,0:T(2,128)}) custom-call(s32[2]{0:T(128)} %pad_add_fusion.meta, bf16[256,1152]{1,0:T(8,128)(2,1)} %fusion.11.q_ref, bf16[1024,2304]{1,0:T(8,128)(2,1)} %add_convert_fusion.kv_ref), custom_call_target="tpu_custom_call" | custom-call | flops 2415919104 | bytes 7077888 | tf_op jit(solution)/shard_map/attend/pallas_call | solution.py:90
  151.3 3.2 place.6
  154.5 2.9 fusion.106
  162.9 13.7 %collective-permute-done.32.refs_6_ = bf16[136,2176]{1,0:T(8,128)(2,1)S(1)} collective-permute-done((bf16[136,2176]{1,0:T(8,128)(2,1)S(1)}, bf16[136,2176]{1,0:T(8,128)(2,1)S(1)}, u32[]{:S(2)}, u32[]{:S(2)}) %collective-permute-start.32) | collective-permute-done | bytes 591904 | tf_op jit(solution)/shard_map/ppermute | solution.py:185
  176.6 11.8 %collective-permute-done.30.refs_4_ = bf16[136,2176]{1,0:T(8,128)(2,1)S(1)} collective-permute-done((bf16[136,2176]{1,0:T(8,128)(2,1)S(1)}, bf16[136,2176]{1,0:T(8,128)(2,1)S(1)}, u32[]{:S(2)}, u32[]{:S(2)}) %collective-permute-start.30) | collective-permute-done | bytes 591904 | tf_op jit(solution)/shard_map/ppermute | solution.py:185
  191.4 4.7 place.7
  196.1 10.2 %all-gather.8.cloned.1.call-done = bf16[1024,1088]{0,1:T(8,128)(2,1)} async-done(((bf16[256,1088]{0,1:T(8,128)(2,1)}), bf16[1024,1088]{0,1:T(8,128)(2,1)}) %all-gather.8.cloned.1.call-update) | async-done | bytes 2228240 | tf_op jit(solution)/shard_map/all_gather | solution.py:278
  206.2 5.7 %convolution_add_fusion = f32[1024,1088]{0,1:T(8,128)S(1)} fusion(bf16[1024,1088]{0,1:T(8,128)(2,1)} %all-gather.8.cloned.1.call-done, f32[1088]{0:T(1024)S(1)} %dynamic_slice.122, bf16[1088,2176]{1,0:T(8,128)(2,1)} %bitcast.220), kind=kOutput, calls=%fused_computation.12 | convolution fusion | flops 2425421824 | bytes 9195776 | tf_op jit(solution)/shard_map/dot_general | solution.py:19
  212.0 8.0 %fusion.107 = (bf16[1088]{0:T(1024)(128)(2,1)S(1)}, bf16[1024,1088]{0,1:T(8,128)(2,1)S(1)}) fusion(f32[1024,1088]{0,1:T(8,128)S(1)} %convolution_add_fusion, bf16[1088,2176]{1,0:T(8,128)(2,1)S(1)} %bitcast.222, bf16[1024,1088]{0,1:T(8,128)(2,1)S(1)} %copy-done.69, bf16[1024]{0:T(1024)(128)(2,1)S(1)} %copy-done.67), kind=kOutput, calls=%fused_computation.252 | convolution fusion | flops 2447703040 | bytes 11423872 | tf_op jit(solution)/shard_map/dot_general | solution.py:19
  221.4 4.2 convolution_convert_fusion.6
  226.2 5.5 %convolution_convert_fusion.4 = bf16[1088,1088]{1,0:T(8,128)(2,1)S(1)} fusion(bf16[1024,1088]{0,1:T(8,128)(2,1)} %all-gather.8.cloned.1.call-done, bf16[1024,1088]{0,1:T(8,128)(2,1)} %copy-done.72), kind=kOutput, calls=%fused_computation.5 | convolution fusion | flops 2425491456 | bytes 6823936 | tf_op jit(solution)/shard_map/dot_general | solution.py:19
  231.7 5.5 %convolution_convert_fusion.3 = bf16[1088,1088]{1,0:T(8,128)(2,1)S(1)} fusion(bf16[1024,1088]{0,1:T(8,128)(2,1)S(1)} %copy-done.70, bf16[1024]{0:T(1024)(128)(2,1)S(1)} %copy-done.67, f32[1024,1088]{0,1:T(8,128)} %copy-done.71), kind=kOutput, calls=%fused_computation.4 | convolution fusion | flops 2436632576 | bytes 9054208 | tf_op jit(solution)/shard_map/dot_general | solution.py:19
  238.8 2.1 pad_maximum_fusion
  240.9 7.8 %convolution_convert_fusion.5 = bf16[1024,1088]{0,1:T(8,128)(2,1)} fusion(bf16[1088,2176]{1,0:T(8,128)(2,1)} %bitcast.221, f32[1024,1088]{0,1:T(8,128)} %copy-done.71), kind=kOutput, calls=%fused_computation.28 | convolution fusion | flops 2435448832 | bytes 9191424 | tf_op jit(solution)/shard_map/dot_general | solution.py:19
  248.8 3.1 add_convert_fusion.1
  257.7 12.2 %collective-permute-done.51 = bf16[136,2176]{1,0:T(8,128)(2,1)} collective-permute-done((bf16[136,2176]{1,0:T(8,128)(2,1)S(1)}, bf16[136,2176]{1,0:T(8,128)(2,1)}, u32[]{:S(2)}, u32[]{:S(2)}) %collective-permute-start.51) | collective-permute-done | bytes 591904 | tf_op jit(solution)/shard_map/ppermute | solution.py:185
  269.8 13.2 %collective-permute-done.53 = bf16[136,2176]{1,0:T(8,128)(2,1)} collective-permute-done((bf16[136,2176]{1,0:T(8,128)(2,1)S(1)}, bf16[136,2176]{1,0:T(8,128)(2,1)}, u32[]{:S(2)}, u32[]{:S(2)}) %collective-permute-start.53) | collective-permute-done | bytes 591904 | tf_op jit(solution)/shard_map/ppermute | solution.py:185
  295.1 3.5 convolution_convert_fusion.1
  298.6 21.6 %attend_back.1 = (bf16[256,1152]{1,0:T(8,128)(2,1)}, bf16[1024,2304]{1,0:T(8,128)(2,1)}) custom-call(s32[2]{0:T(128)} %pad_add_fusion.meta, bf16[256,1152]{1,0:T(8,128)(2,1)} %fusion.11.q_ref, bf16[1024,2304]{1,0:T(8,128)(2,1)} %add_convert_fusion.kv_ref, f32[9,2,256]{2,1,0:T(2,128)} %get-tuple-element.73.lse_ref, bf16[256,1152]{1,0:T(8,128)(2,1)} %pad.38.g_ref), custom_call_target="tpu_custom_call" | custom-call | flops 6039797760 | bytes 14155776 | tf_op jit(solution)/shard_map/attend_back/pallas_call | solution.py:155
  320.2 2.1 convert_element_type.320
  322.3 2.3 convolution_convert_fusion.2
  326.3 6.2 %convolution_convert_fusion = bf16[1088,2304]{1,0:T(8,128)(2,1)S(1)} fusion(bf16[1024,2304]{1,0:T(8,128)(2,1)S(1)} %copy-done.10, bf16[1024,1088]{0,1:T(8,128)(2,1)S(1)} %copy-done.4, f32[1088]{0:T(1024)S(1)} %add.376, f32[1088]{0:T(1024)S(1)} %mul.194, f32[1024]{0:T(1024)S(1)} %copy-done.66, f32[1024]{0:T(1024)S(1)} %copy-done.50), kind=kOutput, calls=%fused_computation | convolution fusion | flops 5143019520 | bytes 11977216 | tf_op jit(solution)/shard_map/dot_general | solution.py:19
  343.3 8.0 %fusion.99 = (f32[1088]{0:T(1024)S(1)}, f32[1088]{0:T(1024)}, bf16[1024,1088]{0,1:T(8,128)(2,1)}) fusion(f32[1024]{0:T(1024)S(1)} %copy-done.66, f32[1024]{0:T(1024)S(1)} %copy-done.50, bf16[1024,1088]{0,1:T(8,128)(2,1)S(1)} %copy-done.4, bf16[1024,2304]{1,0:T(8,128)(2,1)S(1)} %copy-done.10, bf16[1088,3456]{1,0:T(8,128)(2,1)S(1)} %bitcast.216), kind=kOutput, calls=%fused_computation.244 | convolution fusion | flops 5141624832 | bytes 14205440 | tf_op jit(solution)/shard_map/dot_general | solution.py:19
  351.3 3.1 reduce.1
  360.0 4.5 fusion.101
  365.2 2.1 fusion.12
  375.3 2.5 collective-permute-done.39
  378.4 6.2 %collective-permute-done.41 = bf16[136,1088]{1,0:T(8,128)(2,1)S(1)} collective-permute-done((bf16[136,1088]{1,0:T(8,128)(2,1)S(1)}, bf16[136,1088]{1,0:T(8,128)(2,1)S(1)}, u32[]{:S(2)}, u32[]{:S(2)}) %collective-permute-start.41) | collective-permute-done | bytes 295968 | tf_op jit(solution)/shard_map/ppermute | solution.py:185
  387.4 7.8 %collective-permute-done.47 = bf16[72,3456]{1,0:T(8,128)(2,1)S(1)} collective-permute-done((bf16[72,3456]{1,0:T(8,128)(2,1)S(1)}, bf16[72,3456]{1,0:T(8,128)(2,1)S(1)}, u32[]{:S(2)}, u32[]{:S(2)}) %collective-permute-start.47) | collective-permute-done | bytes 497696 | tf_op jit(solution)/shard_map/ppermute | solution.py:185
  395.2 9.8 %collective-permute-done.49 = bf16[72,3456]{1,0:T(8,128)(2,1)S(1)} collective-permute-done((bf16[72,3456]{1,0:T(8,128)(2,1)S(1)}, bf16[72,3456]{1,0:T(8,128)(2,1)S(1)}, u32[]{:S(2)}, u32[]{:S(2)}) %collective-permute-start.49) | collective-permute-done | bytes 497696 | tf_op jit(solution)/shard_map/ppermute | solution.py:185
  414.8 2.4 fusion.60
  429.3 9.5 %collective-permute-done.35 = bf16[64,3456]{1,0:T(8,128)(2,1)S(1)} collective-permute-done((bf16[64,3456]{1,0:T(8,128)(2,1)}, bf16[64,3456]{1,0:T(8,128)(2,1)S(1)}, u32[]{:S(2)}, u32[]{:S(2)}) %collective-permute-start.35) | collective-permute-done | bytes 442400 | tf_op jit(solution)/shard_map/ppermute | solution.py:185
  438.7 8.8 %collective-permute-done.37 = bf16[64,3456]{1,0:T(8,128)(2,1)S(1)} collective-permute-done((bf16[64,3456]{1,0:T(8,128)(2,1)}, bf16[64,3456]{1,0:T(8,128)(2,1)S(1)}, u32[]{:S(2)}, u32[]{:S(2)}) %collective-permute-start.37) | collective-permute-done | bytes 442400 | tf_op jit(solution)/shard_map/ppermute | solution.py:185
  458.8 21.8 %reduce-scatter.12.cloned.1.call-done = bf16[256,1088]{0,1:T(8,128)(2,1)} async-done(((bf16[1024,1088]{0,1:T(8,128)(2,1)}), bf16[256,1088]{0,1:T(8,128)(2,1)}) %reduce-scatter.12.cloned.1.call-update) | async-done | bytes 557072 | tf_op jit(solution)/shard_map/reduce_scatter | solution.py:282
  484.7 20.6 %reduce-scatter.14.cloned.1.call-done = bf16[80,1088]{1,0:T(8,128)(2,1)} async-done(((bf16[320,1088]{1,0:T(8,128)(2,1)}), bf16[80,1088]{1,0:T(8,128)(2,1)}) %reduce-scatter.14.cloned.1.call-update) | async-done | bytes 174096 | tf_op jit(solution)/shard_map/reduce_scatter | solution.py:282
  (424 shorter events, 140.9 us)
Async XLA Ops:
  7.2 84.2 %all-gather.4.cloned.1.call-start = ((), (), s32[]{:S(2)}) async-start(), calls=%async_computation.5 | async-start | bytes 2785280 | tf_op jit(solution)/shard_map/all_gather | solution.py:278
  7.2 25.8 %collective-permute-start.1 = (bf16[136,816]{1,0:T(8,128)(2,1)}, bf16[136,816]{1,0:T(8,128)(2,1)S(1)}, u32[]{:S(2)}, u32[]{:S(2)}) collective-permute-start(bf16[136,816]{1,0:T(8,128)(2,1)} %param.21), channel_id=1, source_target_pairs={{0,2},{1,3},{2,0},{3,1},{4,6},{5,7},{6,4},{7,5},{8,10},{9,11},{10,... | collective-permute-start | bytes 665864 | tf_op jit(solution)/shard_map/ppermute | solution.py:193
  11.4 21.7 %collective-permute-start = (bf16[136,816]{1,0:T(8,128)(2,1)}, bf16[136,816]{1,0:T(8,128)(2,1)S(1)}, u32[]{:S(2)}, u32[]{:S(2)}) collective-permute-start(bf16[136,816]{1,0:T(8,128)(2,1)} %param.21), channel_id=1, source_target_pairs={{0,3},{1,0},{2,1},{3,2},{4,7},{5,4},{6,5},{7,6},{8,11},{9,8},{10,9... | collective-permute-start | bytes 665864 | tf_op jit(solution)/shard_map/ppermute | solution.py:193
  12.7 20.3 %collective-permute-start.2 = (bf16[136,816]{1,0:T(8,128)(2,1)}, bf16[136,816]{1,0:T(8,128)(2,1)S(1)}, u32[]{:S(2)}, u32[]{:S(2)}) collective-permute-start(bf16[136,816]{1,0:T(8,128)(2,1)} %param.21), channel_id=1, source_target_pairs={{0,1},{1,2},{2,3},{3,0},{4,5},{5,6},{6,7},{7,4},{8,9},{9,10},{10,1... | collective-permute-start | bytes 665864 | tf_op jit(solution)/shard_map/ppermute | solution.py:193
  34.1 120.4 %all-gather.6.cloned.1.call-start = ((), (), s32[]{:S(2)}) async-start(), calls=%async_computation.6 | async-start | bytes 2785280 | tf_op jit(solution)/shard_map/all_gather | solution.py:278
  36.5 24.8 %collective-permute-start.16 = (bf16[136,3456]{1,0:T(8,128)(2,1)S(1)}, bf16[136,3456]{1,0:T(8,128)(2,1)}, u32[]{:S(2)}, u32[]{:S(2)}) collective-permute-start(bf16[136,3456]{1,0:T(8,128)(2,1)S(1)} %pad_maximum_fusion.4.refs_0_), channel_id=1, source_target_pairs={{0,24},{4,28},{8,16},{12,20},{16,8},{20,12},{24,0},{28,4},{1,25},{... | collective-permute-start | bytes 2820104 | tf_op jit(solution)/shard_map/ppermute | solution.py:185
  39.0 41.5 %collective-permute-start.15 = (bf16[136,3456]{1,0:T(8,128)(2,1)S(1)}, bf16[136,3456]{1,0:T(8,128)(2,1)S(1)}, u32[]{:S(2)}, u32[]{:S(2)}) collective-permute-start(bf16[136,3456]{1,0:T(8,128)(2,1)S(1)} %pad_maximum_fusion.4.refs_0_), channel_id=1, source_target_pairs={{0,16},{4,20},{8,24},{12,28},{16,0},{20,4},{24,8},{28,12},{1,17},{... | collective-permute-start | bytes 2820104 | tf_op jit(solution)/shard_map/ppermute | solution.py:185
  39.5 42.2 %collective-permute-start.14 = (bf16[136,3456]{1,0:T(8,128)(2,1)S(1)}, bf16[136,3456]{1,0:T(8,128)(2,1)}, u32[]{:S(2)}, u32[]{:S(2)}) collective-permute-start(bf16[136,3456]{1,0:T(8,128)(2,1)S(1)} %pad_maximum_fusion.4.refs_0_), channel_id=1, source_target_pairs={{0,8},{4,12},{8,0},{12,4},{16,24},{20,28},{24,16},{28,20},{1,9},{5... | collective-permute-start | bytes 2820104 | tf_op jit(solution)/shard_map/ppermute | solution.py:185
  40.0 57.2 %collective-permute-start.11 = (bf16[136,272]{1,0:T(8,128)(2,1)S(1)}, bf16[136,272]{1,0:T(8,128)(2,1)S(1)}, u32[]{:S(2)}, u32[]{:S(2)}) collective-permute-start(bf16[136,272]{1,0:T(8,128)(2,1)S(1)} %copy-done.33), channel_id=1, source_target_pairs={{0,2},{1,3},{2,0},{3,1},{4,6},{5,7},{6,4},{7,5},{8,10},{9,11},{10,... | collective-permute-start | bytes 221960 | tf_op jit(solution)/shard_map/ppermute | solution.py:193
  42.8 55.1 %collective-permute-start.10 = (bf16[136,272]{1,0:T(8,128)(2,1)S(1)}, bf16[136,272]{1,0:T(8,128)(2,1)S(1)}, u32[]{:S(2)}, u32[]{:S(2)}) collective-permute-start(bf16[136,272]{1,0:T(8,128)(2,1)S(1)} %copy-done.33), channel_id=1, source_target_pairs={{0,3},{1,0},{2,1},{3,2},{4,7},{5,4},{6,5},{7,6},{8,11},{9,8},{10,9... | collective-permute-start | bytes 221960 | tf_op jit(solution)/shard_map/ppermute | solution.py:193
  61.3 37.3 %collective-permute-start.12 = (bf16[136,272]{1,0:T(8,128)(2,1)S(1)}, bf16[136,272]{1,0:T(8,128)(2,1)}, u32[]{:S(2)}, u32[]{:S(2)}) collective-permute-start(bf16[136,272]{1,0:T(8,128)(2,1)S(1)} %copy-done.33), channel_id=1, source_target_pairs={{0,1},{1,2},{2,3},{3,0},{4,5},{5,6},{6,7},{7,4},{8,9},{9,10},{10,1... | collective-permute-start | bytes 221960 | tf_op jit(solution)/shard_map/ppermute | solution.py:193
  81.5 13.4 %collective-permute-start.19 = (bf16[136,3456]{1,0:T(8,128)(2,1)}, bf16[136,3456]{1,0:T(8,128)(2,1)}, u32[]{:S(2)}, u32[]{:S(2)}) collective-permute-start(bf16[136,3456]{1,0:T(8,128)(2,1)} %collective-permute-done.16.refs_6_), channel_id=1, source_target_pairs={{0,4},{4,0},{8,12},{12,8},{16,20},{20,16},{24,28},{28,24},{1,5},{5... | collective-permute-start | bytes 2820104 | tf_op jit(solution)/shard_map/ppermute | solution.py:185
  95.0 111.2 %all-gather.8.cloned.1.call-start = ((), (), s32[]{:S(2)}) async-start(), calls=%async_computation.7 | async-start | bytes 2785280 | tf_op jit(solution)/shard_map/all_gather | solution.py:278
  108.6 14.4 %collective-permute-start.25 = (bf16[136,1088]{1,0:T(8,128)(2,1)S(1)}, bf16[136,1088]{1,0:T(8,128)(2,1)S(1)}, u32[]{:S(2)}, u32[]{:S(2)}) collective-permute-start(bf16[136,1088]{1,0:T(8,128)(2,1)S(1)} %concatenate.105.refs_0_), channel_id=1, source_target_pairs={{0,24},{4,28},{8,16},{12,20},{16,8},{20,12},{24,0},{28,4},{1,25},{... | collective-permute-start | bytes 887816 | tf_op jit(solution)/shard_map/ppermute | solution.py:185
  111.2 14.7 %collective-permute-start.23 = (bf16[136,1088]{1,0:T(8,128)(2,1)S(1)}, bf16[136,1088]{1,0:T(8,128)(2,1)}, u32[]{:S(2)}, u32[]{:S(2)}) collective-permute-start(bf16[136,1088]{1,0:T(8,128)(2,1)S(1)} %concatenate.105.refs_0_), channel_id=1, source_target_pairs={{0,16},{4,20},{8,24},{12,28},{16,0},{20,4},{24,8},{28,12},{1,17},{... | collective-permute-start | bytes 887816 | tf_op jit(solution)/shard_map/ppermute | solution.py:185
  111.7 14.3 %collective-permute-start.21 = (bf16[136,1088]{1,0:T(8,128)(2,1)S(1)}, bf16[136,1088]{1,0:T(8,128)(2,1)}, u32[]{:S(2)}, u32[]{:S(2)}) collective-permute-start(bf16[136,1088]{1,0:T(8,128)(2,1)S(1)} %concatenate.105.refs_0_), channel_id=1, source_target_pairs={{0,8},{4,12},{8,0},{12,4},{16,24},{20,28},{24,16},{28,20},{1,9},{5... | collective-permute-start | bytes 887816 | tf_op jit(solution)/shard_map/ppermute | solution.py:185
  112.2 37.6 %collective-permute-start.20 = (bf16[136,1088]{1,0:T(8,128)(2,1)S(1)}, bf16[136,1088]{1,0:T(8,128)(2,1)}, u32[]{:S(2)}, u32[]{:S(2)}) collective-permute-start(bf16[136,1088]{1,0:T(8,128)(2,1)S(1)} %concatenate.105.refs_0_), channel_id=1, source_target_pairs={{0,4},{4,0},{8,12},{12,8},{16,20},{20,16},{24,28},{28,24},{1,5},{5... | collective-permute-start | bytes 887816 | tf_op jit(solution)/shard_map/ppermute | solution.py:185
  123.0 26.8 %collective-permute-start.26 = (bf16[136,1088]{1,0:T(8,128)(2,1)S(1)}, bf16[136,1088]{1,0:T(8,128)(2,1)S(1)}, u32[]{:S(2)}, u32[]{:S(2)}) collective-permute-start(bf16[136,1088]{1,0:T(8,128)(2,1)S(1)} %collective-permute-done.25.refs_6_), channel_id=1, source_target_pairs={{0,4},{4,0},{8,12},{12,8},{16,20},{20,16},{24,28},{28,24},{1,5},{5... | collective-permute-start | bytes 887816 | tf_op jit(solution)/shard_map/ppermute | solution.py:185
  125.9 23.9 %collective-permute-start.24 = (bf16[136,1088]{1,0:T(8,128)(2,1)}, bf16[136,1088]{1,0:T(8,128)(2,1)S(1)}, u32[]{:S(2)}, u32[]{:S(2)}) collective-permute-start(bf16[136,1088]{1,0:T(8,128)(2,1)} %collective-permute-done.23.refs_4_), channel_id=1, source_target_pairs={{0,4},{4,0},{8,12},{12,8},{16,20},{20,16},{24,28},{28,24},{1,5},{5... | collective-permute-start | bytes 887816 | tf_op jit(solution)/shard_map/ppermute | solution.py:185
  126.0 23.9 %collective-permute-start.22 = (bf16[136,1088]{1,0:T(8,128)(2,1)}, bf16[136,1088]{1,0:T(8,128)(2,1)S(1)}, u32[]{:S(2)}, u32[]{:S(2)}) collective-permute-start(bf16[136,1088]{1,0:T(8,128)(2,1)} %collective-permute-done.21.refs_2_), channel_id=1, source_target_pairs={{0,4},{4,0},{8,12},{12,8},{16,20},{20,16},{24,28},{28,24},{1,5},{5... | collective-permute-start | bytes 887816 | tf_op jit(solution)/shard_map/ppermute | solution.py:185
  158.9 128.6 %reduce-scatter.8.cloned.1.call-start = ((), (), s32[]{:S(2)}) async-start(), calls=%async_computation.8 | async-start | bytes 2785280 | tf_op jit(solution)/shard_map/reduce_scatter | solution.py:282
  159.4 17.3 %collective-permute-start.32 = (bf16[136,2176]{1,0:T(8,128)(2,1)S(1)}, bf16[136,2176]{1,0:T(8,128)(2,1)S(1)}, u32[]{:S(2)}, u32[]{:S(2)}) collective-permute-start(bf16[136,2176]{1,0:T(8,128)(2,1)S(1)} %pad_maximum_fusion.7.refs_0_), channel_id=1, source_target_pairs={{0,24},{4,28},{8,16},{12,20},{16,8},{20,12},{24,0},{28,4},{1,25},{... | collective-permute-start | bytes 1775624 | tf_op jit(solution)/shard_map/ppermute | solution.py:185
  161.2 27.2 %collective-permute-start.30 = (bf16[136,2176]{1,0:T(8,128)(2,1)S(1)}, bf16[136,2176]{1,0:T(8,128)(2,1)S(1)}, u32[]{:S(2)}, u32[]{:S(2)}) collective-permute-start(bf16[136,2176]{1,0:T(8,128)(2,1)S(1)} %pad_maximum_fusion.7.refs_0_), channel_id=1, source_target_pairs={{0,16},{4,20},{8,24},{12,28},{16,0},{20,4},{24,8},{28,12},{1,17},{... | collective-permute-start | bytes 1775624 | tf_op jit(solution)/shard_map/ppermute | solution.py:185
  162.4 26.2 %collective-permute-start.28 = (bf16[136,2176]{1,0:T(8,128)(2,1)S(1)}, bf16[136,2176]{1,0:T(8,128)(2,1)}, u32[]{:S(2)}, u32[]{:S(2)}) collective-permute-start(bf16[136,2176]{1,0:T(8,128)(2,1)S(1)} %pad_maximum_fusion.7.refs_0_), channel_id=1, source_target_pairs={{0,8},{4,12},{8,0},{12,4},{16,24},{20,28},{24,16},{28,20},{1,9},{5... | collective-permute-start | bytes 1775624 | tf_op jit(solution)/shard_map/ppermute | solution.py:185
  162.9 26.8 %collective-permute-start.27 = (bf16[136,2176]{1,0:T(8,128)(2,1)S(1)}, bf16[136,2176]{1,0:T(8,128)(2,1)}, u32[]{:S(2)}, u32[]{:S(2)}) collective-permute-start(bf16[136,2176]{1,0:T(8,128)(2,1)S(1)} %pad_maximum_fusion.7.refs_0_), channel_id=1, source_target_pairs={{0,4},{4,0},{8,12},{12,8},{16,20},{20,16},{24,28},{28,24},{1,5},{5... | collective-permute-start | bytes 1775624 | tf_op jit(solution)/shard_map/ppermute | solution.py:185
  176.6 13.1 %collective-permute-start.33 = (bf16[136,2176]{1,0:T(8,128)(2,1)S(1)}, bf16[136,2176]{1,0:T(8,128)(2,1)}, u32[]{:S(2)}, u32[]{:S(2)}) collective-permute-start(bf16[136,2176]{1,0:T(8,128)(2,1)S(1)} %collective-permute-done.32.refs_6_), channel_id=1, source_target_pairs={{0,4},{4,0},{8,12},{12,8},{16,20},{20,16},{24,28},{28,24},{1,5},{5... | collective-permute-start | bytes 1775624 | tf_op jit(solution)/shard_map/ppermute | solution.py:185
  225.7 94.5 %reduce-scatter.10.cloned.1.call-start = ((), (), s32[]{:S(2)}) async-start(), calls=%async_computation.9 | async-start | bytes 2785280 | tf_op jit(solution)/shard_map/reduce_scatter | solution.py:282
  240.9 7.9 %collective-permute-start.50 = (bf16[4,136,2176]{2,1,0:T(8,128)(2,1)}, bf16[4,136,2176]{2,1,0:T(8,128)(2,1)}, u32[]{:S(2)}, u32[]{:S(2)}) collective-permute-start(bf16[4,136,2176]{2,1,0:T(8,128)(2,1)} %pad_maximum_fusion), channel_id=1, source_target_pairs={{0,4},{4,0},{8,12},{12,8},{16,20},{20,16},{24,28},{28,24},{1,5},{5... | collective-permute-start | bytes 7102472 | tf_op jit(solution)/shard_map/ppermute | solution.py:185
  248.7 209.2 %reduce-scatter.16.cloned.1.call-start = ((), (), s32[]{:S(2)}) async-start(), calls=%async_computation.12 | async-start | bytes 829440
  253.4 16.4 %collective-permute-start.51 = (bf16[136,2176]{1,0:T(8,128)(2,1)S(1)}, bf16[136,2176]{1,0:T(8,128)(2,1)}, u32[]{:S(2)}, u32[]{:S(2)}) collective-permute-start(bf16[136,2176]{1,0:T(8,128)(2,1)S(1)} %get-tuple-element.120), channel_id=1, source_target_pairs={{0,8},{4,12},{8,0},{12,4},{16,24},{20,28},{24,16},{28,20},{1,9},{5... | collective-permute-start | bytes 1775624 | tf_op jit(solution)/shard_map/ppermute | solution.py:185
  254.9 28.1 %collective-permute-start.53 = (bf16[136,2176]{1,0:T(8,128)(2,1)S(1)}, bf16[136,2176]{1,0:T(8,128)(2,1)}, u32[]{:S(2)}, u32[]{:S(2)}) collective-permute-start(bf16[136,2176]{1,0:T(8,128)(2,1)S(1)} %get-tuple-element.121), channel_id=1, source_target_pairs={{0,24},{4,28},{8,16},{12,20},{16,8},{20,12},{24,0},{28,4},{1,25},{... | collective-permute-start | bytes 1775624 | tf_op jit(solution)/shard_map/ppermute | solution.py:185
  256.3 28.0 %collective-permute-start.52 = (bf16[136,2176]{1,0:T(8,128)(2,1)S(1)}, bf16[136,2176]{1,0:T(8,128)(2,1)}, u32[]{:S(2)}, u32[]{:S(2)}) collective-permute-start(bf16[136,2176]{1,0:T(8,128)(2,1)S(1)} %get-tuple-element.122), channel_id=1, source_target_pairs={{0,16},{4,20},{8,24},{12,28},{16,0},{20,4},{24,8},{28,12},{1,17},{... | collective-permute-start | bytes 1775624 | tf_op jit(solution)/shard_map/ppermute | solution.py:185
  335.5 29.7 %collective-permute-start.38 = (bf16[4,136,1088]{2,1,0:T(8,128)(2,1)}, bf16[4,136,1088]{2,1,0:T(8,128)(2,1)}, u32[]{:S(2)}, u32[]{:S(2)}) collective-permute-start(bf16[4,136,1088]{2,1,0:T(8,128)(2,1)} %dynamic-slice_bitcast_fusion.6), channel_id=1, source_target_pairs={{0,4},{4,0},{8,12},{12,8},{16,20},{20,16},{24,28},{28,24},{1,5},{5... | collective-permute-start | bytes 3551240 | tf_op jit(solution)/shard_map/ppermute | solution.py:185
  342.8 28.2 %collective-permute-start.46 = (bf16[4,72,3456]{2,1,0:T(8,128)(2,1)}, bf16[4,72,3456]{2,1,0:T(8,128)(2,1)}, u32[]{:S(2)}, u32[]{:S(2)}) collective-permute-start(bf16[4,72,3456]{2,1,0:T(8,128)(2,1)} %pad_maximum_fusion.1), channel_id=1, source_target_pairs={{0,4},{4,0},{8,12},{12,8},{16,20},{20,16},{24,28},{28,24},{1,5},{5... | collective-permute-start | bytes 5971976 | tf_op jit(solution)/shard_map/ppermute | solution.py:185
  367.4 10.3 %collective-permute-start.39 = (bf16[136,1088]{1,0:T(8,128)(2,1)S(1)}, bf16[136,1088]{1,0:T(8,128)(2,1)S(1)}, u32[]{:S(2)}, u32[]{:S(2)}) collective-permute-start(bf16[136,1088]{1,0:T(8,128)(2,1)S(1)} %get-tuple-element.133), channel_id=1, source_target_pairs={{0,8},{4,12},{8,0},{12,4},{16,24},{20,28},{24,16},{28,20},{1,9},{5... | collective-permute-start | bytes 887816 | tf_op jit(solution)/shard_map/ppermute | solution.py:185
  368.9 15.6 %collective-permute-start.41 = (bf16[136,1088]{1,0:T(8,128)(2,1)S(1)}, bf16[136,1088]{1,0:T(8,128)(2,1)S(1)}, u32[]{:S(2)}, u32[]{:S(2)}) collective-permute-start(bf16[136,1088]{1,0:T(8,128)(2,1)S(1)} %get-tuple-element.134), channel_id=1, source_target_pairs={{0,24},{4,28},{8,16},{12,20},{16,8},{20,12},{24,0},{28,4},{1,25},{... | collective-permute-start | bytes 887816 | tf_op jit(solution)/shard_map/ppermute | solution.py:185
  369.6 16.8 %collective-permute-start.40 = (bf16[136,1088]{1,0:T(8,128)(2,1)S(1)}, bf16[136,1088]{1,0:T(8,128)(2,1)S(1)}, u32[]{:S(2)}, u32[]{:S(2)}) collective-permute-start(bf16[136,1088]{1,0:T(8,128)(2,1)S(1)} %get-tuple-element.135), channel_id=1, source_target_pairs={{0,16},{4,20},{8,24},{12,28},{16,0},{20,4},{24,8},{28,12},{1,17},{... | collective-permute-start | bytes 887816 | tf_op jit(solution)/shard_map/ppermute | solution.py:185
  373.2 22.0 %collective-permute-start.47 = (bf16[72,3456]{1,0:T(8,128)(2,1)S(1)}, bf16[72,3456]{1,0:T(8,128)(2,1)S(1)}, u32[]{:S(2)}, u32[]{:S(2)}) collective-permute-start(bf16[72,3456]{1,0:T(8,128)(2,1)S(1)} %get-tuple-element.125), channel_id=1, source_target_pairs={{0,8},{4,12},{8,0},{12,4},{16,24},{20,28},{24,16},{28,20},{1,9},{5... | collective-permute-start | bytes 1493000 | tf_op jit(solution)/shard_map/ppermute | solution.py:185
  374.7 30.4 %collective-permute-start.49 = (bf16[72,3456]{1,0:T(8,128)(2,1)S(1)}, bf16[72,3456]{1,0:T(8,128)(2,1)S(1)}, u32[]{:S(2)}, u32[]{:S(2)}) collective-permute-start(bf16[72,3456]{1,0:T(8,128)(2,1)S(1)} %get-tuple-element.126), channel_id=1, source_target_pairs={{0,24},{4,28},{8,16},{12,20},{16,8},{20,12},{24,0},{28,4},{1,25},{... | collective-permute-start | bytes 1493000 | tf_op jit(solution)/shard_map/ppermute | solution.py:185
  377.8 28.6 %collective-permute-start.48 = (bf16[72,3456]{1,0:T(8,128)(2,1)S(1)}, bf16[72,3456]{1,0:T(8,128)(2,1)S(1)}, u32[]{:S(2)}, u32[]{:S(2)}) collective-permute-start(bf16[72,3456]{1,0:T(8,128)(2,1)S(1)} %get-tuple-element.127), channel_id=1, source_target_pairs={{0,16},{4,20},{8,24},{12,28},{16,0},{20,4},{24,8},{28,12},{1,17},{... | collective-permute-start | bytes 1493000 | tf_op jit(solution)/shard_map/ppermute | solution.py:185
  412.6 68.0 %reduce-scatter.12.cloned.1.call-start = ((), (), s32[]{:S(2)}) async-start(), calls=%async_computation.10 | async-start | bytes 2785280 | tf_op jit(solution)/shard_map/reduce_scatter | solution.py:282
  414.5 90.9 %reduce-scatter.14.cloned.1.call-start = ((), (), s32[]{:S(2)}) async-start(), calls=%async_computation.11 | async-start | bytes 921600 | tf_op jit(solution)/shard_map/reduce_scatter | solution.py:282
  417.7 10.7 %collective-permute-start.43 = (bf16[1,1632]{1,0:T(2,128)(2,1)S(1)}, bf16[1,1632]{1,0:T(2,128)(2,1)S(1)}, u32[]{:S(2)}, u32[]{:S(2)}) collective-permute-start(bf16[1,1632]{1,0:T(2,128)(2,1)S(1)} %get-tuple-element.170), channel_id=1, source_target_pairs={{0,8},{4,12},{8,0},{12,4},{16,24},{20,28},{24,16},{28,20},{1,9},{5... | collective-permute-start | bytes 9800 | tf_op jit(solution)/shard_map/ppermute | solution.py:185
  419.2 9.7 %collective-permute-start.45 = (bf16[1,1632]{1,0:T(2,128)(2,1)S(1)}, bf16[1,1632]{1,0:T(2,128)(2,1)S(1)}, u32[]{:S(2)}, u32[]{:S(2)}) collective-permute-start(bf16[1,1632]{1,0:T(2,128)(2,1)S(1)} %get-tuple-element.171), channel_id=1, source_target_pairs={{0,24},{4,28},{8,16},{12,20},{16,8},{20,12},{24,0},{28,4},{1,25},{... | collective-permute-start | bytes 9800 | tf_op jit(solution)/shard_map/ppermute | solution.py:185
  420.7 8.3 %collective-permute-start.44 = (bf16[1,1632]{1,0:T(2,128)(2,1)S(1)}, bf16[1,1632]{1,0:T(2,128)(2,1)S(1)}, u32[]{:S(2)}, u32[]{:S(2)}) collective-permute-start(bf16[1,1632]{1,0:T(2,128)(2,1)S(1)} %get-tuple-element.172), channel_id=1, source_target_pairs={{0,16},{4,20},{8,24},{12,28},{16,0},{20,4},{24,8},{28,12},{1,17},{... | collective-permute-start | bytes 9800 | tf_op jit(solution)/shard_map/ppermute | solution.py:185
  425.5 13.3 %collective-permute-start.35 = (bf16[64,3456]{1,0:T(8,128)(2,1)}, bf16[64,3456]{1,0:T(8,128)(2,1)S(1)}, u32[]{:S(2)}, u32[]{:S(2)}) collective-permute-start(bf16[64,3456]{1,0:T(8,128)(2,1)} %get-tuple-element.128), channel_id=1, source_target_pairs={{0,8},{4,12},{8,0},{12,4},{16,24},{20,28},{24,16},{28,20},{1,9},{5... | collective-permute-start | bytes 1327112 | tf_op jit(solution)/shard_map/ppermute | solution.py:185
  427.0 20.6 %collective-permute-start.37 = (bf16[64,3456]{1,0:T(8,128)(2,1)}, bf16[64,3456]{1,0:T(8,128)(2,1)S(1)}, u32[]{:S(2)}, u32[]{:S(2)}) collective-permute-start(bf16[64,3456]{1,0:T(8,128)(2,1)} %get-tuple-element.129), channel_id=1, source_target_pairs={{0,24},{4,28},{8,16},{12,20},{16,8},{20,12},{24,0},{28,4},{1,25},{... | collective-permute-start | bytes 1327112 | tf_op jit(solution)/shard_map/ppermute | solution.py:185
  428.4 20.6 %collective-permute-start.36 = (bf16[64,3456]{1,0:T(8,128)(2,1)}, bf16[64,3456]{1,0:T(8,128)(2,1)}, u32[]{:S(2)}, u32[]{:S(2)}) collective-permute-start(bf16[64,3456]{1,0:T(8,128)(2,1)} %get-tuple-element.130), channel_id=1, source_target_pairs={{0,16},{4,20},{8,24},{12,28},{16,0},{20,4},{24,8},{28,12},{1,17},{... | collective-permute-start | bytes 1327112 | tf_op jit(solution)/shard_map/ppermute | solution.py:185
  (91 other events, 824.7 us)
Sparse Core Ops, SparseCore 0:
  34.3 57.1 all-gather.3
  95.1 47.5 all-gather.5
  159.0 47.1 all-gather.7
  225.8 43.8 reduce-scatter.7
  271.8 44.9 reduce-scatter.9
  412.7 21.0 reduce-scatter.15
  436.1 44.4 reduce-scatter.11
  482.9 22.3 reduce-scatter.13
